TPU v7x, 32 devices: a whole 2x2x4 slice. The times are simulated.
32 devices in a mesh: clip: 2 (over x), tile: 8 (over z, y), chan: 2 (over core).
Axes of the slice: x: 2, y: 2, z: 4, core: 2. Of those that a mesh axis runs over, the one named last changes fastest.
Arguments:
- owner_latent: bfloat16 [16, 5, 1536], P(('clip', 'tile')), parts along dimension 0, may hold values from -40 to 40, as said below
- tile_counts: int32 [16], P('clip'), parts along dimension 0, may hold values from 1 to 5, as said below
- stem_weight: bfloat16 [27, 16, 384], P(None, None, 'chan'), may hold values from -0.3125 to 0.3125
- stem_bias: float32 [384], P('chan'), may hold values from -1.5 to 1.5
- first_gain: float32 [384], P('chan'), may hold values from 0.5 to 1.5
- first_shift: float32 [384], P('chan'), may hold values from -2.5 to 2.5
- first_weight: bfloat16 [27, 384, 384], P(None, None, 'chan'), may hold values from -0.0625 to 0.0625
- first_bias: float32 [384], P('chan'), may hold values from -2.5 to 2.5
- second_gain: float32 [384], P('chan'), may hold values from 0.5 to 1.5
- second_shift: float32 [384], P('chan'), may hold values from -2.5 to 2.5
- second_weight: bfloat16 [27, 384, 384], P(None, None, 'chan'), may hold values from -0.0625 to 0.0625
- second_bias: float32 [384], P('chan'), may hold values from -1.5 to 1.5
- upsample_weight: bfloat16 [9, 384, 192], replicated, may hold values from -0.109375 to 0.109375
- upsample_bias: float32 [192], replicated, may hold values from -1.5 to 1.5
Outputs:
- upsampled: bfloat16 [8, 48, 32, 192], P(('clip', 'chan'), None, 'tile'), parts along dimension 0
There are 2 independent parts, one for each index of `clip`. A program takes and returns all parts, laid end to end along the dimension named above; an argument that names none is the same for every part. Nothing has to cross between parts.
Inputs may be any that keep to these rules, and one draw needn't show every extreme that they name: Owner o holds latent columns starts[o] to starts[o] + tile_counts[o] - 1 in its first slots, in order; every count is at least 1; the owners of each aligned group of 4 together hold exactly the 8 columns of the strips of the devices with the same group's indices along tile. `owner_latent`: slots at or beyond an owner's count hold no latent column.
All inputs are finite; a program needn't handle non-finite values.
Results may differ from a plain program's by a relative error of at most 0.012.
Values may be sent and summed in bfloat16 or wider, within the bound.
No kernel may reach another device: no remote copies, remote signals or barrier semaphores. Data moves between devices by JAX's collectives and lax.ppermute only.
A program may use at most 128 MiB of HBM per device.

v0:
```python
import functools

import jax
import jax.numpy as jnp
from jax import lax
from jax.experimental import pallas as pl
from jax.experimental.pallas import tpu as pltpu
from jax.sharding import PartitionSpec as P

GROUPS = 32
F = 4
H = 24
W_DEV = 2
HALO = 2
PITCH = 8
H_PAD = 32
EPSILON = 1e-06


def joined(own, other, core):
    low = jnp.concatenate([own, other], axis=-1)
    high = jnp.concatenate([other, own], axis=-1)
    return jnp.where(core == 0, low, high)


def group_mean(column_sums, per_group, cells):
    channels = column_sums.shape[1]
    row = lax.broadcasted_iota(jnp.int32, (channels, channels), 0).astype(jnp.float32)
    column = lax.broadcasted_iota(jnp.int32, (channels, channels), 1).astype(jnp.float32)
    same = jnp.floor((row + 0.5) / per_group) == jnp.floor((column + 0.5) / per_group)
    total = jnp.dot(
        column_sums,
        same.astype(jnp.float32),
        precision=lax.Precision.HIGHEST,
        preferred_element_type=jnp.float32,
    )
    return total[0:1] * (1.0 / (cells * per_group))


def put(ref, place, value):
    for block in range(ref.shape[0]):
        part = value[:, block * 128 : (block + 1) * 128]
        ref[block, place, 0 : part.shape[1]] = part


def take(ref, place, channels):
    parts = []
    for block in range(ref.shape[0]):
        parts.append(ref[block, place, :][:, : channels - block * 128])
    return jnp.concatenate(parts, axis=1)


def silu(value):
    half = 0.5 * value
    return half + half * jnp.tanh(half)


def first_kernel(
    power,
    counts,
    owners,
    stem_own,
    stem_other,
    small_own,
    small_other,
    weight,
    act_out,
    hidden_out,
    shifted,
    patches,
    stem_full,
    hidden,
    acts,
    produced,
    sums,
):
    tile_count = counts.shape[0]
    width = tile_count * W_DEV
    me = lax.axis_index("tile")
    core = lax.axis_index("chan")
    zc, half = stem_own.shape[1], stem_own.shape[2]
    full = 2 * half
    frame_lanes = H_PAD * zc
    pieces = max(1, width // 16)
    rows = H // pieces
    cells = F * H * width
    leftmost = me * W_DEV - HALO

    slots = PITCH * tile_count
    lane = lax.broadcasted_iota(jnp.int32, (3 * width, slots), 1)
    owner_at = lane // PITCH
    slot_at = lane - owner_at * PITCH
    held = jnp.full((3 * width, slots), -5, jnp.int32)
    start = jnp.int32(0)
    for owner in range(tile_count):
        place = (me ^ owner) if power else jnp.int32(owner)
        count = counts[owner]
        held = jnp.where((owner_at == place) & (slot_at < count), start + slot_at, held)
        start = start + count
    position = lax.broadcasted_iota(jnp.int32, (3 * width, slots), 0)
    shift = (position >= width).astype(jnp.int32) + (position >= 2 * width).astype(jnp.int32)
    column = position - shift * width + leftmost
    column = jnp.where(column < 0, column + width, column)
    column = jnp.where(column >= width, column - width, column)
    selection = (held == column + shift - 1).astype(jnp.bfloat16)
    for frame in range(F):
        lanes = slice(frame * frame_lanes, (frame + 1) * frame_lanes)
        chosen = jnp.dot(selection, owners[:, lanes], preferred_element_type=jnp.float32)
        shifted[:, frame] = chosen.reshape(3, width, frame_lanes)

    stem_full[...] = jnp.zeros(stem_full.shape, jnp.bfloat16)
    for tap in range(27):
        a, b, e = tap // 9, tap // 3 % 3, tap % 3
        at = e * 4 * zc + b * zc
        stem_full[a, at : at + zc, :] = joined(stem_own[tap], stem_other[tap], core)
    stem_bias = joined(small_own[0:1], small_other[0:1], core)
    first_gain = joined(small_own[1:2], small_other[1:2], core)
    first_shift = joined(small_own[2:3], small_other[2:3], core)

    per_block = 128 // zc
    lane128 = lax.broadcasted_iota(jnp.int32, (F, width, 128), 2)
    for row in range(H):
        block = row // per_block * 128
        offset = row % per_block * zc
        window = shifted[:, :, :, block : block + 256]
        one = pltpu.roll(window[0], (256 - offset) % 256, axis=2)[:, :, :128]
        two = pltpu.roll(window[1], (320 - offset) % 256, axis=2)[:, :, :128]
        three = pltpu.roll(window[2], (256 - offset) % 256, axis=2)[:, :, :128]
        patches[:, row, :, 0:128] = jnp.where(lane128 < 64, one, two).astype(jnp.bfloat16)
        patches[:, row, :, 128:256] = three.astype(jnp.bfloat16)

    def over_pieces(body):
        if pieces == 1:
            body(0)
        else:
            lax.fori_loop(0, pieces, lambda i, _: (body(i * rows), 0)[1], 0)

    def span(frame, row):
        return pl.ds(pl.multiple_of((frame * H + row) * width, 16), rows * width)

    sums[...] = jnp.zeros_like(sums)
    for frame in range(F):

        def stem(row):
            total = jnp.zeros((rows * width, full), jnp.float32)
            for a in range(max(0, 2 - frame), 3):
                lhs = patches[frame + a - 2, pl.ds(row, rows)].reshape(rows * width, 256)
                total += jnp.dot(lhs, stem_full[a], preferred_element_type=jnp.float32)
            value = (total + stem_bias).astype(jnp.bfloat16).astype(jnp.float32)
            put(hidden, span(frame, row), value)
            sums[0:1, :] += jnp.sum(value, axis=0, keepdims=True)

        over_pieces(stem)

    per_group = full // GROUPS
    mean = group_mean(jnp.broadcast_to(sums[0:1, :], (8, full)), per_group, cells)
    for frame in range(F):

        def squares(row):
            spread = take(hidden, span(frame, row), full) - mean
            sums[1:2, :] += jnp.sum(spread * spread, axis=0, keepdims=True)

        over_pieces(squares)
    variance = group_mean(jnp.broadcast_to(sums[1:2, :], (8, full)), per_group, cells)
    scale = lax.rsqrt(variance + EPSILON) * first_gain

    spot = lax.broadcasted_iota(jnp.int32, (1, width, full), 1) + leftmost
    spot = jnp.where(spot < 0, spot + width, spot)
    spot = jnp.where(spot >= width, spot - width, spot)
    zero_row = jnp.zeros((width, full), jnp.bfloat16)
    for e in range(3):
        for frame in range(F):
            acts[e, frame, 0] = zero_row
            acts[e, frame, H + 1] = zero_row
    for frame in range(F):

        def activate(row):
            spread = take(hidden, span(frame, row), full) - mean
            value = silu(spread * scale + first_shift).reshape(rows, width, full)
            left = jnp.where(spot == 0, 0.0, pltpu.roll(value, 1, axis=1))
            right = jnp.where(spot == width - 1, 0.0, pltpu.roll(value, width - 1, axis=1))
            place = pl.ds(row + 1, rows)
            acts[0, frame, place] = left.astype(jnp.bfloat16)
            acts[1, frame, place] = value.astype(jnp.bfloat16)
            acts[2, frame, place] = right.astype(jnp.bfloat16)

        over_pieces(activate)

    first_bias = small_own[4:5]
    for frame in range(F):

        def convolve(row):
            total = jnp.zeros((rows * width, half), jnp.float32)
            for a in range(max(0, 2 - frame), 3):
                for b in range(3):
                    lhs = jnp.concatenate(
                        [
                            acts[e, frame + a - 2, pl.ds(row + b, rows)].reshape(rows * width, full)
                            for e in range(3)
                        ],
                        axis=1,
                    )
                    tap = 9 * a + 3 * b
                    rhs = weight[tap : tap + 3].reshape(3 * full, half)
                    total += jnp.dot(lhs, rhs, preferred_element_type=jnp.float32)
            value = (total + first_bias).astype(jnp.bfloat16).astype(jnp.float32)
            put(produced, span(frame, row), value)
            sums[2:3, 0:half] += jnp.sum(value, axis=0, keepdims=True)

        over_pieces(convolve)

    mean = group_mean(jnp.broadcast_to(sums[2:3, 0:half], (8, half)), per_group, cells)
    for frame in range(F):

        def squares_again(row):
            spread = take(produced, span(frame, row), half) - mean
            sums[3:4, 0:half] += jnp.sum(spread * spread, axis=0, keepdims=True)

        over_pieces(squares_again)
    variance = group_mean(jnp.broadcast_to(sums[3:4, 0:half], (8, half)), per_group, cells)
    scale = lax.rsqrt(variance + EPSILON) * small_own[5:6]
    second_shift = small_own[6:7]
    for spot_at in range(W_DEV + 2 * HALO):
        value = take(produced, pl.ds(spot_at, F * H, stride=width), half)
        value = silu((value - mean) * scale + second_shift)
        real = (leftmost + spot_at >= 0) & (leftmost + spot_at < width)
        act_out[spot_at] = jnp.where(real, value, 0.0).astype(jnp.bfloat16)
    frames = F // 2
    for spot_at in range(1, W_DEV + 3):
        begin = core * (frames * H * width) + spot_at
        value = take(hidden, pl.ds(begin, frames * H, stride=width), full)
        hidden_out[spot_at - 1] = value.astype(jnp.bfloat16)


def second_kernel(
    tile_count,
    act_own,
    act_other,
    hidden_in,
    weight_own,
    weight_other,
    small_own,
    small_other,
    up_weight,
    up_bias,
    out,
    slots,
    taps,
    flat,
):
    width = tile_count * W_DEV
    me = lax.axis_index("tile")
    core = lax.axis_index("chan")
    columns, cells, half = act_own.shape
    full = 2 * half
    frames = F // 2
    rows = frames * H
    inner = columns - 2
    slots[...] = jnp.zeros_like(slots)
    for column in range(columns):
        value = joined(
            act_own[column].astype(jnp.float32), act_other[column].astype(jnp.float32), core
        )
        before = jnp.where(core == 0, 0.0, value[0:rows])
        now = jnp.where(core == 0, value[0:rows], value[rows:])
        for slot in range(frames):
            at = slot * 32 + 8
            slots[column, at : at + H, :] = before[slot * H : (slot + 1) * H]
            at = (slot + frames) * 32 + 8
            slots[column, at : at + H, :] = now[slot * H : (slot + 1) * H]
    for a in range(3):
        for b in range(3):
            parts = []
            for frame in range(frames):
                at = (frame + a) * 32 + 7 + b
                parts.append(slots[:, at : at + H, :])
            taps[3 * a + b] = jnp.concatenate(parts, axis=1).astype(jnp.bfloat16)
    mine = jnp.zeros((inner * rows, half), jnp.float32)
    theirs = jnp.zeros((inner * rows, half), jnp.float32)
    for pair in range(9):
        lhs = jnp.concatenate(
            [taps[pair, e : e + inner].reshape(inner * rows, full) for e in range(3)], axis=1
        )
        rhs = weight_own[3 * pair : 3 * pair + 3].reshape(3 * full, half)
        mine += jnp.dot(lhs, rhs, preferred_element_type=jnp.float32)
        rhs = weight_other[3 * pair : 3 * pair + 3].reshape(3 * full, half)
        theirs += jnp.dot(lhs, rhs, preferred_element_type=jnp.float32)
    second_out = joined(mine + small_own[3:4], theirs + small_other[3:4], core)
    hidden = hidden_in[...].astype(jnp.float32) + second_out.reshape(inner, rows, full)
    spot = lax.broadcasted_iota(jnp.int32, (inner, rows, full), 0) + me * W_DEV - 1
    hidden = jnp.where((spot >= 0) & (spot < width), hidden, 0.0).astype(jnp.bfloat16)
    hidden = hidden.reshape(inner * rows, full)

    line = lax.broadcasted_iota(jnp.int32, (inner * frames, H, half), 1)
    upper, lower = [], []
    for e in range(3):
        made = [
            jnp.dot(hidden, up_weight[3 * b + e], preferred_element_type=jnp.float32).reshape(
                inner * frames, H, half
            )
            for b in range(3)
        ]
        above = jnp.where(line == 0, 0.0, pltpu.roll(made[0], 1, axis=1))
        below = jnp.where(line == H - 1, 0.0, pltpu.roll(made[2], H - 1, axis=1))
        upper.append((above + made[1] + made[2]).reshape(inner, frames, H, half))
        lower.append((made[0] + made[1] + below).reshape(inner, frames, H, half))
    bias = up_bias[...]
    span = 2 * W_DEV
    for parity, sums in ((0, upper), (1, lower)):
        for x in range(W_DEV):
            at = x + 1
            for side in range(2):
                if side == 0:
                    value = sums[0][at - 1] + sums[1][at] + sums[2][at]
                else:
                    value = sums[0][at] + sums[1][at] + sums[2][at + 1]
                for frame in range(frames):
                    begin = frame * 2 * H * span + parity * span + 2 * x + side
                    put(flat, pl.ds(begin, H, stride=2 * span), value[frame] + bias)
    out[...] = take(flat, slice(None), out.shape[-1]).astype(jnp.bfloat16).reshape(out.shape)


def gathered(block, axis):
    count = lax.axis_size(axis)
    if count & (count - 1):
        return lax.all_gather(block, axis, axis=0, tiled=True), False
    step = 1
    while step < count:
        moved = lax.ppermute(block, axis, [(i, i ^ step) for i in range(count)])
        block = jnp.concatenate([block, moved], axis=0)
        step *= 2
    return block, True


def on_device(
    owner_latent,
    tile_counts,
    stem_weight,
    stem_bias,
    first_gain,
    first_shift,
    first_weight,
    first_bias,
    second_gain,
    second_shift,
    second_weight,
    second_bias,
    upsample_weight,
    upsample_bias,
):
    tile_count = lax.axis_size("tile")
    width = tile_count * W_DEV
    _, slot_count, row_length = owner_latent.shape
    zc, half = stem_weight.shape[1], stem_weight.shape[2]
    full = 2 * half
    out_channels = upsample_weight.shape[2]
    swap = [(0, 1), (1, 0)]
    frames = F // 2

    padded = owner_latent.reshape(1, slot_count, F, H, zc)
    padded = jnp.pad(
        padded, ((0, 0), (0, PITCH - slot_count), (0, 0), (1, H_PAD - H - 1), (0, 0))
    ).reshape(1, PITCH, F * H_PAD * zc)
    small = jnp.stack(
        [
            stem_bias,
            first_gain,
            first_shift,
            second_bias,
            first_bias,
            second_gain,
            second_shift,
            jnp.zeros_like(stem_bias),
        ]
    )
    small_other = lax.ppermute(small, "chan", swap)
    stem_other = lax.ppermute(stem_weight, "chan", swap)
    second_other = lax.ppermute(second_weight, "chan", swap)
    owners, power = gathered(padded, "tile")
    owners = owners.reshape(tile_count * PITCH, F * H_PAD * zc)

    window = W_DEV + 2 * HALO
    vmem = pl.BlockSpec(memory_space=pltpu.VMEM)
    act, hidden = pl.pallas_call(
        functools.partial(first_kernel, power),
        out_shape=(
            jax.ShapeDtypeStruct((window, F * H, half), jnp.bfloat16),
            jax.ShapeDtypeStruct((window - 2, frames * H, full), jnp.bfloat16),
        ),
        in_specs=[pl.BlockSpec(memory_space=pltpu.SMEM)] + [vmem] * 6,
        out_specs=(vmem, vmem),
        scratch_shapes=[
            pltpu.VMEM((3, F, width, H_PAD * zc), jnp.float32),
            pltpu.VMEM((F, H, width, 256), jnp.bfloat16),
            pltpu.VMEM((3, 256, full), jnp.bfloat16),
            pltpu.VMEM((full // 128, F * H * width, 128), jnp.float32),
            pltpu.VMEM((3, F, H + 2, width, full), jnp.bfloat16),
            pltpu.VMEM((pl.cdiv(half, 128), F * H * width, 128), jnp.float32),
            pltpu.VMEM((8, full), jnp.float32),
        ],
        cost_estimate=pl.CostEstimate(
            flops=2 * F * H * width * 27 * full * half * 3 // 4,
            bytes_accessed=27 * full * half * 2,
            transcendentals=F * H * width * full,
        ),
        compiler_params=pltpu.CompilerParams(vmem_limit_bytes=60 * 1024 * 1024),
    )(tile_counts, owners, stem_weight, stem_other, small, small_other, first_weight)

    act_other = lax.ppermute(act, "chan", swap)

    out = pl.pallas_call(
        functools.partial(second_kernel, tile_count),
        out_shape=jax.ShapeDtypeStruct((frames, 2 * H, 2 * W_DEV, out_channels), jnp.bfloat16),
        in_specs=[vmem] * 9,
        out_specs=vmem,
        scratch_shapes=[
            pltpu.VMEM((window, 2 * frames * 32 + 8, full), jnp.float32),
            pltpu.VMEM((9, window, frames * H, full), jnp.bfloat16),
            pltpu.VMEM((pl.cdiv(out_channels, 128), frames * 2 * H * 2 * W_DEV, 128), jnp.float32),
        ],
        cost_estimate=pl.CostEstimate(
            flops=2 * 4 * 48 * 27 * full * full,
            bytes_accessed=2 * 27 * full * half * 2,
            transcendentals=0,
        ),
        compiler_params=pltpu.CompilerParams(vmem_limit_bytes=40 * 1024 * 1024),
    )(
        act,
        act_other,
        hidden,
        second_weight,
        second_other,
        small,
        small_other,
        upsample_weight,
        upsample_bias.reshape(1, -1),
    )
    return out


def solution(mesh):
    placed = (
        P(("clip", "tile"), None, None),
        P("clip"),
        P(None, None, "chan"),
        P("chan"),
        P("chan"),
        P("chan"),
        P(None, None, "chan"),
        P("chan"),
        P("chan"),
        P("chan"),
        P(None, None, "chan"),
        P("chan"),
        P(),
        P(),
    )
    return jax.shard_map(
        on_device,
        mesh=mesh,
        in_specs=placed,
        out_specs=P(("clip", "chan"), None, "tile", None),
        check_vma=False,
    )
```

profile of v0, /device:TPU:0, one launch (start us, length us, event | category | flops | bytes accessed | tf_op | source)
XLA Modules:
  0.0 65.2 jit_solution(11647694839627658758)
XLA Ops:
  0.0 0.5 collective-permute-start.6
  0.5 0.9 %reshape.12 = bf16[1,5,4,24,16]{4,3,2,1,0:T(8,128)(2,1)S(1)} reshape(bf16[1,5,1536]{2,1,0:T(8,128)(2,1)} %param.14) | data formatting | bytes 30720 | tf_op jit(solution)/shard_map/reshape | solution.py:360
  1.4 0.1 pad.4
  1.4 0.3 reshape.13
  1.8 2.6 %collective-permute-start = (bf16[1,8,2048]{2,1,0:T(8,128)(2,1)S(1)}, bf16[1,8,2048]{2,1,0:T(8,128)(2,1)S(1)}, u32[]{:S(2)}, u32[]{:S(2)}) collective-permute-start(bf16[1,8,2048]{2,1,0:T(8,128)(2,1)S(1)} %reshape.13), channel_id=1, source_target_pairs={{0,2},{2,0},{4,6},{6,4},{8,10},{10,8},{12,14},{14,12},{1,3},{3,1},... | collective-permute-start | bytes 98312 | tf_op jit(solution)/shard_map/ppermute | solution.py:329
  4.3 2.1 %collective-permute-done = bf16[1,8,2048]{2,1,0:T(8,128)(2,1)S(1)} collective-permute-done((bf16[1,8,2048]{2,1,0:T(8,128)(2,1)S(1)}, bf16[1,8,2048]{2,1,0:T(8,128)(2,1)S(1)}, u32[]{:S(2)}, u32[]{:S(2)}) %collective-permute-start) | collective-permute-done | bytes 32800 | tf_op jit(solution)/shard_map/ppermute | solution.py:329
  6.4 2.0 %collective-permute-start.1 = (bf16[2,8,2048]{2,1,0:T(8,128)(2,1)S(1)}, bf16[2,8,2048]{2,1,0:T(8,128)(2,1)S(1)}, u32[]{:S(2)}, u32[]{:S(2)}) collective-permute-start(bf16[2,8,2048]{2,1,0:T(8,128)(2,1)S(1)} %pad_maximum_fusion.1), channel_id=1, source_target_pairs={{0,4},{2,6},{4,0},{6,2},{8,12},{10,14},{12,8},{14,10},{1,5},{3,7},... | collective-permute-start | bytes 196616 | tf_op jit(solution)/shard_map/ppermute | solution.py:329
  8.4 2.4 %collective-permute-done.1 = bf16[2,8,2048]{2,1,0:T(8,128)(2,1)S(1)} collective-permute-done((bf16[2,8,2048]{2,1,0:T(8,128)(2,1)S(1)}, bf16[2,8,2048]{2,1,0:T(8,128)(2,1)S(1)}, u32[]{:S(2)}, u32[]{:S(2)}) %collective-permute-start.1) | collective-permute-done | bytes 65568 | tf_op jit(solution)/shard_map/ppermute | solution.py:329
  10.7 3.0 %collective-permute-start.2 = (bf16[4,8,2048]{2,1,0:T(8,128)(2,1)S(1)}, bf16[4,8,2048]{2,1,0:T(8,128)(2,1)S(1)}, u32[]{:S(2)}, u32[]{:S(2)}) collective-permute-start(bf16[4,8,2048]{2,1,0:T(8,128)(2,1)S(1)} %pad_maximum_fusion), channel_id=1, source_target_pairs={{0,8},{2,10},{4,12},{6,14},{8,0},{10,2},{12,4},{14,6},{1,9},{3,11}... | collective-permute-start | bytes 393224 | tf_op jit(solution)/shard_map/ppermute | solution.py:329
  13.7 0.8 %stack.31.small_own = f32[8,192]{1,0:T(8,128)S(1)} concatenate(f32[1,192]{1,0:T(1,128)} %bitcast.13, f32[1,192]{1,0:T(1,128)} %bitcast.14, f32[1,192]{1,0:T(1,128)} %bitcast.15, f32[1,192]{1,0:T(1,128)} %bitcast.16, f32[1,192]{1,0:T(1,128)} %bitcast.17, f32[1,192]{1,0:T(1,128)} %bitcast.18, f32[1,192]{1,0:T(1,128)} %bitcast.19, f32[1,192]{1,0:T(1,128)S(1)} %stack_broadcast_in_dim.3), dimensions={0} | concatenate | bytes 12288 | tf_op jit(solution)/shard_map/stack | solution.py:364
  14.5 0.1 collective-permute-start.4
  14.6 0.5 collective-permute-start.3
  15.1 7.2 %copy.23.weight = bf16[27,384,192]{2,1,0:T(8,128)(2,1)} copy(bf16[27,384,192]{1,2,0:T(8,128)(2,1)} %param.20) | data formatting | bytes 7962624 | tf_op args[6]
  22.3 0.7 %maximum_bitcast_fusion.owners = bf16[64,2048]{1,0:T(8,128)(2,1)} fusion(bf16[4,8,2048]{2,1,0:T(8,128)(2,1)S(1)} %collective-permute-done.2, bf16[2,8,2048]{2,1,0:T(8,128)(2,1)S(1)} %collective-permute-done.1, bf16[1,8,2048]{2,1,0:T(8,128)(2,1)S(1)} %collective-permute-done, bf16[1,8,2048]{2,1,0:T(8,128)(2,1)S(1)} %reshape.13), kind=kLoop, calls=%fused_computation | loop fusion | flops 393216 | bytes 524288 | tf_op jit(solution)/shard_map/reshape | solution.py:380
  23.1 0.6 copy-done.6
  23.7 0.7 %copy-done.10 = bf16[27,16,192]{2,1,0:T(8,128)(2,1)} copy-done((bf16[27,16,192]{2,1,0:T(8,128)(2,1)}, bf16[27,16,192]{2,1,0:T(8,128)(2,1)S(1)}, u32[]{:S(2)}) %copy-start.10) | copy-done | bytes 165912
  24.4 16.1 %shard_map.136 = (bf16[6,96,192]{2,1,0:T(8,128)(2,1)}, bf16[4,48,384]{2,1,0:T(8,128)(2,1)}) custom-call(s32[8]{0:T(128)} %counts.1, bf16[64,2048]{1,0:T(8,128)(2,1)} %maximum_bitcast_fusion.owners, bf16[27,16,192]{2,1,0:T(8,128)(2,1)} %stem_own.1, bf16[27,16,192]{2,1,0:T(8,128)(2,1)} %copy-done.10, f32[8,192]{1,0:T(8,128)} %copy-done.4, f32[8,192]{1,0:T(8,128)} %copy-done.6, ...), custom_call_target="tpu_custom_call" | custom-call | flops 4586471424 | bytes 3981312 | tf_op jit(solution)/shard_map/pallas_call | solution.py:384
  40.4 0.1 collective-permute-start.5
  40.5 7.3 %copy.24.weight_own = bf16[27,384,192]{2,1,0:T(8,128)(2,1)} copy(bf16[27,384,192]{1,2,0:T(8,128)(2,1)} %param.24) | data formatting | bytes 7962624 | tf_op args[10]
  47.8 0.9 %copy.26.up_weight = bf16[9,384,192]{2,1,0:T(8,128)(2,1)S(1)} copy(bf16[9,384,192]{1,2,0:T(8,128)(2,1)S(1)} %copy-done.9) | data formatting | bytes 2654208 | tf_op args[12]
  48.8 7.3 %copy.25.weight_other = bf16[27,384,192]{2,1,0:T(8,128)(2,1)} copy(bf16[27,384,192]{1,2,0:T(8,128)(2,1)} %collective-permute-done.6) | data formatting | bytes 7962624 | tf_op jit(solution)/shard_map/ppermute | solution.py:378
  56.2 2.5 %copy-done = bf16[27,384,192]{2,1,0:T(8,128)(2,1)S(1)} copy-done((bf16[27,384,192]{2,1,0:T(8,128)(2,1)S(1)}, bf16[27,384,192]{2,1,0:T(8,128)(2,1)}, u32[]{:S(2)}) %copy-start) | copy-done | bytes 3981336
  58.7 2.5 %copy-done.1 = bf16[27,384,192]{2,1,0:T(8,128)(2,1)S(1)} copy-done((bf16[27,384,192]{2,1,0:T(8,128)(2,1)S(1)}, bf16[27,384,192]{2,1,0:T(8,128)(2,1)}, u32[]{:S(2)}) %copy-start.1) | copy-done | bytes 3981336
  61.2 4.1 %shard_map.137 = bf16[2,48,4,192]{3,2,1,0:T(4,128)(2,1)} custom-call(bf16[6,96,192]{2,1,0:T(8,128)(2,1)S(1)} %copy-done.2, bf16[6,96,192]{2,1,0:T(8,128)(2,1)S(1)} %collective-permute-done.5.act_other, bf16[4,48,384]{2,1,0:T(8,128)(2,1)S(1)} %copy-done.3, bf16[27,384,192]{2,1,0:T(8,128)(2,1)S(1)} %copy-done, bf16[27,384,192]{2,1,0:T(8,128)(2,1)S(1)} %copy-done.1, ...), custom_call_target="tpu_custom_call" | custom-call | flops 1528823808 | bytes 7962624 | tf_op jit(solution)/shard_map/pallas_call | solution.py:411
  (26 shorter events, 0.1 us)
Async XLA Ops:
  0.0 48.8 %collective-permute-start.6 = (bf16[27,384,192]{1,2,0:T(8,128)(2,1)}, bf16[27,384,192]{1,2,0:T(8,128)(2,1)}, u32[]{:S(2)}, u32[]{:S(2)}) collective-permute-start(bf16[27,384,192]{1,2,0:T(8,128)(2,1)} %param.24), channel_id=1, source_target_pairs={{0,1},{1,0},{2,3},{3,2},{4,5},{5,4},{6,7},{7,6},{8,9},{9,8},{10,11... | collective-permute-start | bytes 11943944 | tf_op jit(solution)/shard_map/ppermute | solution.py:378
  1.8 4.6 %collective-permute-start = (bf16[1,8,2048]{2,1,0:T(8,128)(2,1)S(1)}, bf16[1,8,2048]{2,1,0:T(8,128)(2,1)S(1)}, u32[]{:S(2)}, u32[]{:S(2)}) collective-permute-start(bf16[1,8,2048]{2,1,0:T(8,128)(2,1)S(1)} %reshape.13), channel_id=1, source_target_pairs={{0,2},{2,0},{4,6},{6,4},{8,10},{10,8},{12,14},{14,12},{1,3},{3,1},... | collective-permute-start | bytes 98312 | tf_op jit(solution)/shard_map/ppermute | solution.py:329
  6.4 4.3 %collective-permute-start.1 = (bf16[2,8,2048]{2,1,0:T(8,128)(2,1)S(1)}, bf16[2,8,2048]{2,1,0:T(8,128)(2,1)S(1)}, u32[]{:S(2)}, u32[]{:S(2)}) collective-permute-start(bf16[2,8,2048]{2,1,0:T(8,128)(2,1)S(1)} %pad_maximum_fusion.1), channel_id=1, source_target_pairs={{0,4},{2,6},{4,0},{6,2},{8,12},{10,14},{12,8},{14,10},{1,5},{3,7},... | collective-permute-start | bytes 196616 | tf_op jit(solution)/shard_map/ppermute | solution.py:329
  10.7 11.6 %collective-permute-start.2 = (bf16[4,8,2048]{2,1,0:T(8,128)(2,1)S(1)}, bf16[4,8,2048]{2,1,0:T(8,128)(2,1)S(1)}, u32[]{:S(2)}, u32[]{:S(2)}) collective-permute-start(bf16[4,8,2048]{2,1,0:T(8,128)(2,1)S(1)} %pad_maximum_fusion), channel_id=1, source_target_pairs={{0,8},{2,10},{4,12},{6,14},{8,0},{10,2},{12,4},{14,6},{1,9},{3,11}... | collective-permute-start | bytes 393224 | tf_op jit(solution)/shard_map/ppermute | solution.py:329
  14.5 7.8 %copy-start.4 = (f32[8,192]{1,0:T(8,128)}, f32[8,192]{1,0:T(8,128)S(1)}, u32[]{:S(2)}) copy-start(f32[8,192]{1,0:T(8,128)S(1)} %stack.31.small_own) | copy-start | bytes 18436
  14.5 8.5 %collective-permute-start.4 = (f32[8,192]{1,0:T(8,128)S(1)}, f32[8,192]{1,0:T(8,128)S(1)}, u32[]{:S(2)}, u32[]{:S(2)}) collective-permute-start(f32[8,192]{1,0:T(8,128)S(1)} %stack.31.small_own), channel_id=1, source_target_pairs={{0,1},{1,0},{2,3},{3,2},{4,5},{5,4},{6,7},{7,6},{8,9},{9,8},{10,11... | collective-permute-start | bytes 18440 | tf_op jit(solution)/shard_map/ppermute | solution.py:376
  14.6 8.5 %collective-permute-start.3 = (bf16[27,16,192]{2,1,0:T(8,128)(2,1)}, bf16[27,16,192]{2,1,0:T(8,128)(2,1)S(1)}, u32[]{:S(2)}, u32[]{:S(2)}) collective-permute-start(bf16[27,16,192]{2,1,0:T(8,128)(2,1)} %stem_own.1), channel_id=1, source_target_pairs={{0,1},{1,0},{2,3},{3,2},{4,5},{5,4},{6,7},{7,6},{8,9},{9,8},{10,11... | collective-permute-start | bytes 497672 | tf_op jit(solution)/shard_map/ppermute | solution.py:377
  23.1 0.6 copy-start.6
  23.7 0.7 %copy-start.10 = (bf16[27,16,192]{2,1,0:T(8,128)(2,1)}, bf16[27,16,192]{2,1,0:T(8,128)(2,1)S(1)}, u32[]{:S(2)}) copy-start(bf16[27,16,192]{2,1,0:T(8,128)(2,1)S(1)} %collective-permute-done.3.stem_other) | copy-start | bytes 497668
  40.4 7.4 %copy-start.9 = (bf16[9,384,192]{1,2,0:T(8,128)(2,1)S(1)}, bf16[9,384,192]{1,2,0:T(8,128)(2,1)}, u32[]{:S(2)}) copy-start(bf16[9,384,192]{1,2,0:T(8,128)(2,1)} %param.26) | copy-start | bytes 3981316
  40.4 15.7 %collective-permute-start.5 = (bf16[6,96,192]{2,1,0:T(8,128)(2,1)}, bf16[6,96,192]{2,1,0:T(8,128)(2,1)S(1)}, u32[]{:S(2)}, u32[]{:S(2)}) collective-permute-start(bf16[6,96,192]{2,1,0:T(8,128)(2,1)} %get-tuple-element.7.act_own), channel_id=1, source_target_pairs={{0,1},{1,0},{2,3},{3,2},{4,5},{5,4},{6,7},{7,6},{8,9},{9,8},{10,11... | collective-permute-start | bytes 663560 | tf_op jit(solution)/shard_map/ppermute | solution.py:409
  48.7 7.4 %copy-start.2 = (bf16[6,96,192]{2,1,0:T(8,128)(2,1)S(1)}, bf16[6,96,192]{2,1,0:T(8,128)(2,1)}, u32[]{:S(2)}) copy-start(bf16[6,96,192]{2,1,0:T(8,128)(2,1)} %get-tuple-element.7.act_own) | copy-start | bytes 663556
  48.7 7.4 %copy-start.3 = (bf16[4,48,384]{2,1,0:T(8,128)(2,1)S(1)}, bf16[4,48,384]{2,1,0:T(8,128)(2,1)}, u32[]{:S(2)}) copy-start(bf16[4,48,384]{2,1,0:T(8,128)(2,1)} %get-tuple-element.8.hidden_in) | copy-start | bytes 442372
  48.8 7.4 %copy-start.5 = (f32[8,192]{1,0:T(8,128)S(1)}, f32[8,192]{1,0:T(8,128)}, u32[]{:S(2)}) copy-start(f32[8,192]{1,0:T(8,128)} %copy-done.4) | copy-start | bytes 18436
  48.8 7.4 %copy-start.7 = (f32[8,192]{1,0:T(8,128)S(1)}, f32[8,192]{1,0:T(8,128)}, u32[]{:S(2)}) copy-start(f32[8,192]{1,0:T(8,128)} %copy-done.6) | copy-start | bytes 18436
  48.8 7.4 %copy-start.8 = (f32[192]{0:T(256)S(1)}, f32[192]{0:T(256)}, u32[]{:S(2)}) copy-start(f32[192]{0:T(256)} %param.27) | copy-start | bytes 2308
  56.2 2.5 %copy-start = (bf16[27,384,192]{2,1,0:T(8,128)(2,1)S(1)}, bf16[27,384,192]{2,1,0:T(8,128)(2,1)}, u32[]{:S(2)}) copy-start(bf16[27,384,192]{2,1,0:T(8,128)(2,1)} %copy.24.weight_own) | copy-start | bytes 11943940
  58.7 2.5 %copy-start.1 = (bf16[27,384,192]{2,1,0:T(8,128)(2,1)S(1)}, bf16[27,384,192]{2,1,0:T(8,128)(2,1)}, u32[]{:S(2)}) copy-start(bf16[27,384,192]{2,1,0:T(8,128)(2,1)} %copy.25.weight_other) | copy-start | bytes 11943940
where the time goes:
time: 66 us; the launch traced here: 65.2 us
  local copies, waits for them, and re-layouts  31.1 us (47%)
  Pallas kernels  20.1 us (30%)
  starting transfers between devices  8.65 us (13%)
  waiting for transfers between devices  4.43 us (7%)
  other arithmetic  0.76 us (1%)
    unnamed x25, local copies, waits for them, and re-layouts  21.7 us
    pallas_call x1, Pallas kernels, on_device(): pl.pallas_call(functools.partial(first_kernel, power), out_shape=(jax.Sha...  16.1 us
    ppermute x3, starting transfers between devices, gathered(): moved = lax.ppermute(block, axis, [(i, i ^ step) for i in range(count)])  7.53 us
    ppermute x1, local copies, waits for them, and re-layouts, on_device(): second_other = lax.ppermute(second_weight, 'chan', swap)  7.32 us
    ppermute x3, waiting for transfers between devices, gathered(): moved = lax.ppermute(block, axis, [(i, i ^ step) for i in range(count)])  4.42 us
    pallas_call x1, Pallas kernels, on_device(): pl.pallas_call(functools.partial(second_kernel, tile_count), out_shape=ja...  4.07 us
  transfers between devices with their start and end apart: 7, of which 2 were waited for; matrix products, arithmetic and copies ran while one was open for 39% of the time, Pallas kernels for 25%

commit v1 on v0

--- a/solution.py
+++ b/solution.py
@@ -50,6 +50,11 @@
     return jnp.concatenate(parts, axis=1)
 
 
+def times(lhs, weight, taps):
+    rhs = jnp.concatenate([weight[tap] for tap in taps], axis=1)
+    return lax.dot_general(lhs, rhs, (((1,), (1,)), ((), ())), preferred_element_type=jnp.float32)
+
+
 def silu(value):
     half = 0.5 * value
     return half + half * jnp.tanh(half)
@@ -63,7 +68,7 @@
     stem_other,
     small_own,
     small_other,
-    weight,
+    weight_far,
     act_out,
     hidden_out,
     shifted,
@@ -73,7 +78,11 @@
     acts,
     produced,
     sums,
+    weight,
+    arrival,
 ):
+    fetch = pltpu.make_async_copy(weight_far, weight, arrival)
+    fetch.start()
     tile_count = counts.shape[0]
     width = tile_count * W_DEV
     me = lax.axis_index("tile")
@@ -186,6 +195,7 @@
 
         over_pieces(activate)
 
+    fetch.wait()
     first_bias = small_own[4:5]
     for frame in range(F):
 
@@ -201,8 +211,7 @@
                         axis=1,
                     )
                     tap = 9 * a + 3 * b
-                    rhs = weight[tap : tap + 3].reshape(3 * full, half)
-                    total += jnp.dot(lhs, rhs, preferred_element_type=jnp.float32)
+                    total += times(lhs, weight, range(tap, tap + 3))
             value = (total + first_bias).astype(jnp.bfloat16).astype(jnp.float32)
             put(produced, span(frame, row), value)
             sums[2:3, 0:half] += jnp.sum(value, axis=0, keepdims=True)
@@ -238,7 +247,7 @@
     act_other,
     hidden_in,
     weight_own,
-    weight_other,
+    weight_far,
     small_own,
     small_other,
     up_weight,
@@ -247,7 +256,11 @@
     slots,
     taps,
     flat,
+    weight_other,
+    arrival,
 ):
+    fetch = pltpu.make_async_copy(weight_far, weight_other, arrival)
+    fetch.start()
     width = tile_count * W_DEV
     me = lax.axis_index("tile")
     core = lax.axis_index("chan")
@@ -275,16 +288,20 @@
                 at = (frame + a) * 32 + 7 + b
                 parts.append(slots[:, at : at + H, :])
             taps[3 * a + b] = jnp.concatenate(parts, axis=1).astype(jnp.bfloat16)
-    mine = jnp.zeros((inner * rows, half), jnp.float32)
-    theirs = jnp.zeros((inner * rows, half), jnp.float32)
-    for pair in range(9):
-        lhs = jnp.concatenate(
-            [taps[pair, e : e + inner].reshape(inner * rows, full) for e in range(3)], axis=1
-        )
-        rhs = weight_own[3 * pair : 3 * pair + 3].reshape(3 * full, half)
-        mine += jnp.dot(lhs, rhs, preferred_element_type=jnp.float32)
-        rhs = weight_other[3 * pair : 3 * pair + 3].reshape(3 * full, half)
-        theirs += jnp.dot(lhs, rhs, preferred_element_type=jnp.float32)
+
+
+    def convolve(weight):
+        total = jnp.zeros((inner * rows, half), jnp.float32)
+        for pair in range(9):
+            lhs = jnp.concatenate(
+                [taps[pair, e : e + inner].reshape(inner * rows, full) for e in range(3)], axis=1
+            )
+            total += times(lhs, weight, range(3 * pair, 3 * pair + 3))
+        return total
+
+    mine = convolve(weight_own)
+    fetch.wait()
+    theirs = convolve(weight_other)
     second_out = joined(mine + small_own[3:4], theirs + small_other[3:4], core)
     hidden = hidden_in[...].astype(jnp.float32) + second_out.reshape(inner, rows, full)
     spot = lax.broadcasted_iota(jnp.int32, (inner, rows, full), 0) + me * W_DEV - 1
@@ -295,9 +312,7 @@
     upper, lower = [], []
     for e in range(3):
         made = [
-            jnp.dot(hidden, up_weight[3 * b + e], preferred_element_type=jnp.float32).reshape(
-                inner * frames, H, half
-            )
+            times(hidden, up_weight, [3 * b + e]).reshape(inner * frames, H, half)
             for b in range(3)
         ]
         above = jnp.where(line == 0, 0.0, pltpu.roll(made[0], 1, axis=1))
@@ -354,6 +369,9 @@
     zc, half = stem_weight.shape[1], stem_weight.shape[2]
     full = 2 * half
     out_channels = upsample_weight.shape[2]
+    first_weight = first_weight.transpose(0, 2, 1)
+    second_weight = second_weight.transpose(0, 2, 1)
+    upsample_weight = upsample_weight.transpose(0, 2, 1)
     swap = [(0, 1), (1, 0)]
     frames = F // 2
 
@@ -381,13 +399,14 @@
 
     window = W_DEV + 2 * HALO
     vmem = pl.BlockSpec(memory_space=pltpu.VMEM)
+    far = pl.BlockSpec(memory_space=pltpu.HBM)
     act, hidden = pl.pallas_call(
         functools.partial(first_kernel, power),
         out_shape=(
             jax.ShapeDtypeStruct((window, F * H, half), jnp.bfloat16),
             jax.ShapeDtypeStruct((window - 2, frames * H, full), jnp.bfloat16),
         ),
-        in_specs=[pl.BlockSpec(memory_space=pltpu.SMEM)] + [vmem] * 6,
+        in_specs=[pl.BlockSpec(memory_space=pltpu.SMEM)] + [vmem] * 5 + [far],
         out_specs=(vmem, vmem),
         scratch_shapes=[
             pltpu.VMEM((3, F, width, H_PAD * zc), jnp.float32),
@@ -397,13 +416,15 @@
             pltpu.VMEM((3, F, H + 2, width, full), jnp.bfloat16),
             pltpu.VMEM((pl.cdiv(half, 128), F * H * width, 128), jnp.float32),
             pltpu.VMEM((8, full), jnp.float32),
+            pltpu.VMEM(first_weight.shape, jnp.bfloat16),
+            pltpu.SemaphoreType.DMA,
         ],
         cost_estimate=pl.CostEstimate(
             flops=2 * F * H * width * 27 * full * half * 3 // 4,
             bytes_accessed=27 * full * half * 2,
             transcendentals=F * H * width * full,
         ),
-        compiler_params=pltpu.CompilerParams(vmem_limit_bytes=60 * 1024 * 1024),
+        compiler_params=pltpu.CompilerParams(vmem_limit_bytes=min(60, 12 + 12 * width // 16) * 1024 * 1024),
     )(tile_counts, owners, stem_weight, stem_other, small, small_other, first_weight)
 
     act_other = lax.ppermute(act, "chan", swap)
@@ -411,19 +432,21 @@
     out = pl.pallas_call(
         functools.partial(second_kernel, tile_count),
         out_shape=jax.ShapeDtypeStruct((frames, 2 * H, 2 * W_DEV, out_channels), jnp.bfloat16),
-        in_specs=[vmem] * 9,
+        in_specs=[vmem] * 4 + [far] + [vmem] * 4,
         out_specs=vmem,
         scratch_shapes=[
             pltpu.VMEM((window, 2 * frames * 32 + 8, full), jnp.float32),
             pltpu.VMEM((9, window, frames * H, full), jnp.bfloat16),
             pltpu.VMEM((pl.cdiv(out_channels, 128), frames * 2 * H * 2 * W_DEV, 128), jnp.float32),
+            pltpu.VMEM(second_weight.shape, jnp.bfloat16),
+            pltpu.SemaphoreType.DMA,
         ],
         cost_estimate=pl.CostEstimate(
             flops=2 * 4 * 48 * 27 * full * full,
             bytes_accessed=2 * 27 * full * half * 2,
             transcendentals=0,
         ),
-        compiler_params=pltpu.CompilerParams(vmem_limit_bytes=40 * 1024 * 1024),
+        compiler_params=pltpu.CompilerParams(vmem_limit_bytes=24 * 1024 * 1024),
     )(
         act,
         act_other,

time: 66 us -> 47.6 us (0.72)
  local copies, waits for them, and re-layouts: 31.1 us -> 5.77 us
  waiting for transfers between devices: 4.43 us -> 9.59 us
  Pallas kernels: 20.1 us -> 23.1 us
  other arithmetic: 0.76 us -> 0.05 us
    unnamed x25 -> x12, local copies, waits for them, and re-layouts: 21.7 us -> 3.72 us
    ppermute x1 -> x0, local copies, waits for them, and re-layouts: 7.32 us -> none  [on_device(): second_other = lax.ppermute(second_weight, 'chan', swap)]
    pallas_call x1, Pallas kernels: 4.07 us -> 8.44 us  [on_device(): pl.pallas_call(functools.partial(second_kernel, tile_count), out_shape=ja...]
    ppermute x3, waiting for transfers between devices: 4.42 us -> 8.01 us  [gathered(): moved = lax.ppermute(block, axis, [(i, i ^ step) for i in range(count)])]
    ppermute x1, waiting for transfers between devices: 0.01 us -> 1.57 us  [on_device(): act_other = lax.ppermute(act, 'chan', swap)]
    pallas_call x1, Pallas kernels: 16.1 us -> 14.7 us  [on_device(): pl.pallas_call(functools.partial(first_kernel, power), out_shape=(jax.Sha...]
    reshape x1, other arithmetic: 0.74 us -> 0.03 us  [on_device(): owners = owners.reshape(tile_count * PITCH, F * H_PAD * zc)]
  transfers between devices with their start and end apart: 7 -> 7, of which waited for: 2 -> 4; matrix products, arithmetic and copies ran while one was open for 39% -> 4% of each run, Pallas kernels for 25% -> 31%
where the time goes in v1:
time: 47.6 us; the launch traced here: 47.3 us
  Pallas kernels  23.1 us (49%)
  waiting for transfers between devices  9.59 us (20%)
  starting transfers between devices  8.65 us (18%)
  local copies, waits for them, and re-layouts  5.77 us (12%)
    pallas_call x1, Pallas kernels, on_device(): pl.pallas_call(functools.partial(first_kernel, power), out_shape=(jax.Sha...  14.7 us
    pallas_call x1, Pallas kernels, on_device(): pl.pallas_call(functools.partial(second_kernel, tile_count), out_shape=ja...  8.44 us
    ppermute x3, waiting for transfers between devices, gathered(): moved = lax.ppermute(block, axis, [(i, i ^ step) for i in range(count)])  8.01 us
    ppermute x3, starting transfers between devices, gathered(): moved = lax.ppermute(block, axis, [(i, i ^ step) for i in range(count)])  7.53 us
    unnamed x12, local copies, waits for them, and re-layouts  3.72 us
    ppermute x1, waiting for transfers between devices, on_device(): act_other = lax.ppermute(act, 'chan', swap)  1.57 us
  transfers between devices with their start and end apart: 7, of which 4 were waited for; matrix products, arithmetic and copies ran while one was open for 4% of the time, Pallas kernels for 31%

profile of v1, /device:TPU:0, one launch (start us, length us, event | category | flops | bytes accessed | tf_op | source)
XLA Modules:
  0.0 47.3 jit_solution(16811252568759724319)
XLA Ops:
  0.0 0.5 %collective-permute-start.6 = (bf16[27,192,384]{2,1,0:T(8,128)(2,1)}, bf16[27,192,384]{2,1,0:T(8,128)(2,1)}, u32[]{:S(2)}, u32[]{:S(2)}) collective-permute-start(bf16[27,192,384]{2,1,0:T(8,128)(2,1)} %bitcast.15), channel_id=1, source_target_pairs={{0,1},{1,0},{2,3},{3,2},{4,5},{5,4},{6,7},{7,6},{8,9},{9,8},{10,11... | collective-permute-start | bytes 11943944 | tf_op jit(solution)/shard_map/ppermute | solution.py:396
  0.5 0.9 %reshape.12 = bf16[1,5,4,24,16]{4,3,2,1,0:T(8,128)(2,1)S(1)} reshape(bf16[1,5,1536]{2,1,0:T(8,128)(2,1)} %param.14) | data formatting | bytes 30720 | tf_op jit(solution)/shard_map/reshape | solution.py:378
  1.4 0.1 pad.4
  1.4 0.3 reshape.13
  1.8 2.6 %collective-permute-start = (bf16[1,8,2048]{2,1,0:T(8,128)(2,1)S(1)}, bf16[1,8,2048]{2,1,0:T(8,128)(2,1)S(1)}, u32[]{:S(2)}, u32[]{:S(2)}) collective-permute-start(bf16[1,8,2048]{2,1,0:T(8,128)(2,1)S(1)} %reshape.13), channel_id=1, source_target_pairs={{0,2},{2,0},{4,6},{6,4},{8,10},{10,8},{12,14},{14,12},{1,3},{3,1},... | collective-permute-start | bytes 98312 | tf_op jit(solution)/shard_map/ppermute | solution.py:344
  4.3 2.1 %collective-permute-done = bf16[1,8,2048]{2,1,0:T(8,128)(2,1)S(1)} collective-permute-done((bf16[1,8,2048]{2,1,0:T(8,128)(2,1)S(1)}, bf16[1,8,2048]{2,1,0:T(8,128)(2,1)S(1)}, u32[]{:S(2)}, u32[]{:S(2)}) %collective-permute-start) | collective-permute-done | bytes 32800 | tf_op jit(solution)/shard_map/ppermute | solution.py:344
  6.4 2.0 %collective-permute-start.1 = (bf16[2,8,2048]{2,1,0:T(8,128)(2,1)S(1)}, bf16[2,8,2048]{2,1,0:T(8,128)(2,1)S(1)}, u32[]{:S(2)}, u32[]{:S(2)}) collective-permute-start(bf16[2,8,2048]{2,1,0:T(8,128)(2,1)S(1)} %pad_maximum_fusion.1), channel_id=1, source_target_pairs={{0,4},{2,6},{4,0},{6,2},{8,12},{10,14},{12,8},{14,10},{1,5},{3,7},... | collective-permute-start | bytes 196616 | tf_op jit(solution)/shard_map/ppermute | solution.py:344
  8.4 2.4 %collective-permute-done.1 = bf16[2,8,2048]{2,1,0:T(8,128)(2,1)S(1)} collective-permute-done((bf16[2,8,2048]{2,1,0:T(8,128)(2,1)S(1)}, bf16[2,8,2048]{2,1,0:T(8,128)(2,1)S(1)}, u32[]{:S(2)}, u32[]{:S(2)}) %collective-permute-start.1) | collective-permute-done | bytes 65568 | tf_op jit(solution)/shard_map/ppermute | solution.py:344
  10.7 3.0 %collective-permute-start.2 = (bf16[4,8,2048]{2,1,0:T(8,128)(2,1)S(1)}, bf16[4,8,2048]{2,1,0:T(8,128)(2,1)S(1)}, u32[]{:S(2)}, u32[]{:S(2)}) collective-permute-start(bf16[4,8,2048]{2,1,0:T(8,128)(2,1)S(1)} %pad_maximum_fusion), channel_id=1, source_target_pairs={{0,8},{2,10},{4,12},{6,14},{8,0},{10,2},{12,4},{14,6},{1,9},{3,11}... | collective-permute-start | bytes 393224 | tf_op jit(solution)/shard_map/ppermute | solution.py:344
  13.7 0.8 %stack.31.small_own = f32[8,192]{1,0:T(8,128)S(1)} concatenate(f32[1,192]{1,0:T(1,128)} %bitcast.20, f32[1,192]{1,0:T(1,128)} %bitcast.21, f32[1,192]{1,0:T(1,128)} %bitcast.22, f32[1,192]{1,0:T(1,128)} %bitcast.23, f32[1,192]{1,0:T(1,128)} %bitcast.24, f32[1,192]{1,0:T(1,128)} %bitcast.25, f32[1,192]{1,0:T(1,128)} %bitcast.26, f32[1,192]{1,0:T(1,128)S(1)} %stack_broadcast_in_dim.3), dimensions={0} | concatenate | bytes 12288 | tf_op jit(solution)/shard_map/stack | solution.py:382
  14.5 0.1 collective-permute-start.4
  14.6 0.5 %collective-permute-start.3 = (bf16[27,16,192]{2,1,0:T(8,128)(2,1)}, bf16[27,16,192]{2,1,0:T(8,128)(2,1)S(1)}, u32[]{:S(2)}, u32[]{:S(2)}) collective-permute-start(bf16[27,16,192]{2,1,0:T(8,128)(2,1)} %stem_own.1), channel_id=1, source_target_pairs={{0,1},{1,0},{2,3},{3,2},{4,5},{5,4},{6,7},{7,6},{8,9},{9,8},{10,11... | collective-permute-start | bytes 497672 | tf_op jit(solution)/shard_map/ppermute | solution.py:395
  15.1 3.6 %collective-permute-done.2 = bf16[4,8,2048]{2,1,0:T(8,128)(2,1)S(1)} collective-permute-done((bf16[4,8,2048]{2,1,0:T(8,128)(2,1)S(1)}, bf16[4,8,2048]{2,1,0:T(8,128)(2,1)S(1)}, u32[]{:S(2)}, u32[]{:S(2)}) %collective-permute-start.2) | collective-permute-done | bytes 131104 | tf_op jit(solution)/shard_map/ppermute | solution.py:344
  18.7 0.0 collective-permute-done.4.small_other
  18.7 0.0 collective-permute-done.3.stem_other
  18.8 0.0 copy-start.3
  18.8 2.1 %copy-done.3 = bf16[27,384,192]{1,2,0:T(8,128)(2,1)S(1)} copy-done((bf16[27,384,192]{1,2,0:T(8,128)(2,1)S(1)}, bf16[27,384,192]{1,2,0:T(8,128)(2,1)}, u32[]{:S(2)}) %copy-start.3) | copy-done | bytes 3981336
  20.9 0.9 %copy-done.4 = bf16[27,16,192]{2,1,0:T(8,128)(2,1)S(1)} copy-done((bf16[27,16,192]{2,1,0:T(8,128)(2,1)S(1)}, bf16[27,16,192]{2,1,0:T(8,128)(2,1)}, u32[]{:S(2)}) %copy-start.4) | copy-done | bytes 165912
  21.8 0.7 %copy-done.5 = s32[8]{0:T(128)S(1)} copy-done((s32[8]{0:T(128)S(1)}, s32[8]{0:T(128)}, u32[]{:S(2)}) %copy-start.5) | copy-done | bytes 56
  22.5 14.7 %shard_map.136 = (bf16[6,96,192]{2,1,0:T(8,128)(2,1)S(1)}, bf16[4,48,384]{2,1,0:T(8,128)(2,1)S(1)}) custom-call(s32[8]{0:T(128)S(1)} %copy-done.5, bf16[64,2048]{1,0:T(8,128)(2,1)S(1)} %maximum_bitcast_fusion.owners, bf16[27,16,192]{2,1,0:T(8,128)(2,1)S(1)} %copy-done.4, bf16[27,16,192]{2,1,0:T(8,128)(2,1)S(1)} %collective-permute-done.3.stem_other, ...), custom_call_target="tpu_custom_call" | custom-call | flops 4586471424 | bytes 3981312 | tf_op jit(solution)/shard_map/pallas_call | solution.py:403
  37.2 0.1 collective-permute-start.5
  37.2 1.6 %collective-permute-done.5.act_other = bf16[6,96,192]{2,1,0:T(8,128)(2,1)S(1)} collective-permute-done((bf16[6,96,192]{2,1,0:T(8,128)(2,1)S(1)}, bf16[6,96,192]{2,1,0:T(8,128)(2,1)S(1)}, u32[]{:S(2)}, u32[]{:S(2)}) %collective-permute-start.5) | collective-permute-done | bytes 221216 | tf_op jit(solution)/shard_map/ppermute | solution.py:430
  38.8 0.0 collective-permute-done.6.weight_far
  38.8 8.4 %shard_map.137 = bf16[2,48,4,192]{3,2,1,0:T(4,128)(2,1)} custom-call(bf16[6,96,192]{2,1,0:T(8,128)(2,1)S(1)} %get-tuple-element.7.act_own, bf16[6,96,192]{2,1,0:T(8,128)(2,1)S(1)} %collective-permute-done.5.act_other, bf16[4,48,384]{2,1,0:T(8,128)(2,1)S(1)} %get-tuple-element.8.hidden_in, bf16[27,192,384]{2,1,0:T(8,128)(2,1)S(1)} %bitcast.16, ...), custom_call_target="tpu_custom_call" | custom-call | flops 1528823808 | bytes 7962624 | tf_op jit(solution)/shard_map/pallas_call | solution.py:432
  (12 shorter events, 0.1 us)
Async XLA Ops:
  0.0 38.8 %collective-permute-start.6 = (bf16[27,192,384]{2,1,0:T(8,128)(2,1)}, bf16[27,192,384]{2,1,0:T(8,128)(2,1)}, u32[]{:S(2)}, u32[]{:S(2)}) collective-permute-start(bf16[27,192,384]{2,1,0:T(8,128)(2,1)} %bitcast.15), channel_id=1, source_target_pairs={{0,1},{1,0},{2,3},{3,2},{4,5},{5,4},{6,7},{7,6},{8,9},{9,8},{10,11... | collective-permute-start | bytes 11943944 | tf_op jit(solution)/shard_map/ppermute | solution.py:396
  1.8 4.6 %collective-permute-start = (bf16[1,8,2048]{2,1,0:T(8,128)(2,1)S(1)}, bf16[1,8,2048]{2,1,0:T(8,128)(2,1)S(1)}, u32[]{:S(2)}, u32[]{:S(2)}) collective-permute-start(bf16[1,8,2048]{2,1,0:T(8,128)(2,1)S(1)} %reshape.13), channel_id=1, source_target_pairs={{0,2},{2,0},{4,6},{6,4},{8,10},{10,8},{12,14},{14,12},{1,3},{3,1},... | collective-permute-start | bytes 98312 | tf_op jit(solution)/shard_map/ppermute | solution.py:344
  6.4 4.3 %collective-permute-start.1 = (bf16[2,8,2048]{2,1,0:T(8,128)(2,1)S(1)}, bf16[2,8,2048]{2,1,0:T(8,128)(2,1)S(1)}, u32[]{:S(2)}, u32[]{:S(2)}) collective-permute-start(bf16[2,8,2048]{2,1,0:T(8,128)(2,1)S(1)} %pad_maximum_fusion.1), channel_id=1, source_target_pairs={{0,4},{2,6},{4,0},{6,2},{8,12},{10,14},{12,8},{14,10},{1,5},{3,7},... | collective-permute-start | bytes 196616 | tf_op jit(solution)/shard_map/ppermute | solution.py:344
  10.7 8.0 %collective-permute-start.2 = (bf16[4,8,2048]{2,1,0:T(8,128)(2,1)S(1)}, bf16[4,8,2048]{2,1,0:T(8,128)(2,1)S(1)}, u32[]{:S(2)}, u32[]{:S(2)}) collective-permute-start(bf16[4,8,2048]{2,1,0:T(8,128)(2,1)S(1)} %pad_maximum_fusion), channel_id=1, source_target_pairs={{0,8},{2,10},{4,12},{6,14},{8,0},{10,2},{12,4},{14,6},{1,9},{3,11}... | collective-permute-start | bytes 393224 | tf_op jit(solution)/shard_map/ppermute | solution.py:344
  14.5 4.2 %collective-permute-start.4 = (f32[8,192]{1,0:T(8,128)S(1)}, f32[8,192]{1,0:T(8,128)S(1)}, u32[]{:S(2)}, u32[]{:S(2)}) collective-permute-start(f32[8,192]{1,0:T(8,128)S(1)} %stack.31.small_own), channel_id=1, source_target_pairs={{0,1},{1,0},{2,3},{3,2},{4,5},{5,4},{6,7},{7,6},{8,9},{9,8},{10,11... | collective-permute-start | bytes 18440 | tf_op jit(solution)/shard_map/ppermute | solution.py:394
  14.6 4.1 %collective-permute-start.3 = (bf16[27,16,192]{2,1,0:T(8,128)(2,1)}, bf16[27,16,192]{2,1,0:T(8,128)(2,1)S(1)}, u32[]{:S(2)}, u32[]{:S(2)}) collective-permute-start(bf16[27,16,192]{2,1,0:T(8,128)(2,1)} %stem_own.1), channel_id=1, source_target_pairs={{0,1},{1,0},{2,3},{3,2},{4,5},{5,4},{6,7},{7,6},{8,9},{9,8},{10,11... | collective-permute-start | bytes 497672 | tf_op jit(solution)/shard_map/ppermute | solution.py:395
  18.8 2.1 %copy-start.3 = (bf16[27,384,192]{1,2,0:T(8,128)(2,1)S(1)}, bf16[27,384,192]{1,2,0:T(8,128)(2,1)}, u32[]{:S(2)}) copy-start(bf16[27,384,192]{1,2,0:T(8,128)(2,1)} %param.20) | copy-start | bytes 11943940
  20.9 0.9 %copy-start.4 = (bf16[27,16,192]{2,1,0:T(8,128)(2,1)S(1)}, bf16[27,16,192]{2,1,0:T(8,128)(2,1)}, u32[]{:S(2)}) copy-start(bf16[27,16,192]{2,1,0:T(8,128)(2,1)} %stem_own.1) | copy-start | bytes 497668
  21.8 0.7 %copy-start.5 = (s32[8]{0:T(128)S(1)}, s32[8]{0:T(128)}, u32[]{:S(2)}) copy-start(s32[8]{0:T(128)} %counts.1) | copy-start | bytes 100
  22.5 16.3 %copy-start = (bf16[27,384,192]{1,2,0:T(8,128)(2,1)S(1)}, bf16[27,384,192]{1,2,0:T(8,128)(2,1)}, u32[]{:S(2)}) copy-start(bf16[27,384,192]{1,2,0:T(8,128)(2,1)} %param.24) | copy-start | bytes 11943940
  22.5 16.3 %copy-start.1 = (bf16[9,384,192]{1,2,0:T(8,128)(2,1)S(1)}, bf16[9,384,192]{1,2,0:T(8,128)(2,1)}, u32[]{:S(2)}) copy-start(bf16[9,384,192]{1,2,0:T(8,128)(2,1)} %param.26) | copy-start | bytes 3981316
  22.5 16.3 %copy-start.2 = (f32[192]{0:T(256)S(1)}, f32[192]{0:T(256)}, u32[]{:S(2)}) copy-start(f32[192]{0:T(256)} %param.27) | copy-start | bytes 2308
  37.2 1.6 %collective-permute-start.5 = (bf16[6,96,192]{2,1,0:T(8,128)(2,1)S(1)}, bf16[6,96,192]{2,1,0:T(8,128)(2,1)S(1)}, u32[]{:S(2)}, u32[]{:S(2)}) collective-permute-start(bf16[6,96,192]{2,1,0:T(8,128)(2,1)S(1)} %get-tuple-element.7.act_own), channel_id=1, source_target_pairs={{0,1},{1,0},{2,3},{3,2},{4,5},{5,4},{6,7},{7,6},{8,9},{9,8},{10,11... | collective-permute-start | bytes 663560 | tf_op jit(solution)/shard_map/ppermute | solution.py:430

commit v2 on v1

--- a/solution.py
+++ b/solution.py
@@ -60,39 +60,14 @@
     return half + half * jnp.tanh(half)
 
 
-def first_kernel(
-    power,
-    counts,
-    owners,
-    stem_own,
-    stem_other,
-    small_own,
-    small_other,
-    weight_far,
-    act_out,
-    hidden_out,
-    shifted,
-    patches,
-    stem_full,
-    hidden,
-    acts,
-    produced,
-    sums,
-    weight,
-    arrival,
+def prepare_kernel(
+    power, counts, stem_own, stem_other, small_own, small_other, selection, stem_full, vectors
 ):
-    fetch = pltpu.make_async_copy(weight_far, weight, arrival)
-    fetch.start()
     tile_count = counts.shape[0]
     width = tile_count * W_DEV
     me = lax.axis_index("tile")
     core = lax.axis_index("chan")
-    zc, half = stem_own.shape[1], stem_own.shape[2]
-    full = 2 * half
-    frame_lanes = H_PAD * zc
-    pieces = max(1, width // 16)
-    rows = H // pieces
-    cells = F * H * width
+    zc = stem_own.shape[1]
     leftmost = me * W_DEV - HALO
 
     slots = PITCH * tile_count
@@ -111,20 +86,55 @@
     column = position - shift * width + leftmost
     column = jnp.where(column < 0, column + width, column)
     column = jnp.where(column >= width, column - width, column)
-    selection = (held == column + shift - 1).astype(jnp.bfloat16)
-    for frame in range(F):
-        lanes = slice(frame * frame_lanes, (frame + 1) * frame_lanes)
-        chosen = jnp.dot(selection, owners[:, lanes], preferred_element_type=jnp.float32)
-        shifted[:, frame] = chosen.reshape(3, width, frame_lanes)
+    selection[...] = (held == column + shift - 1).astype(jnp.bfloat16)
 
     stem_full[...] = jnp.zeros(stem_full.shape, jnp.bfloat16)
     for tap in range(27):
         a, b, e = tap // 9, tap // 3 % 3, tap % 3
         at = e * 4 * zc + b * zc
         stem_full[a, at : at + zc, :] = joined(stem_own[tap], stem_other[tap], core)
-    stem_bias = joined(small_own[0:1], small_other[0:1], core)
-    first_gain = joined(small_own[1:2], small_other[1:2], core)
-    first_shift = joined(small_own[2:3], small_other[2:3], core)
+    vectors[...] = joined(small_own[...], small_other[...], core)
+
+
+def first_kernel(
+    owners,
+    selection,
+    stem_full,
+    vectors,
+    small_own,
+    weight_far,
+    act_out,
+    hidden_out,
+    shifted,
+    patches,
+    hidden,
+    acts,
+    produced,
+    sums,
+    weight,
+    arrival,
+):
+    fetch = pltpu.make_async_copy(weight_far, weight, arrival)
+    fetch.start()
+    tile_count = owners.shape[0] // PITCH
+    width = tile_count * W_DEV
+    me = lax.axis_index("tile")
+    core = lax.axis_index("chan")
+    full, half = vectors.shape[1], small_own.shape[1]
+    frame_lanes = owners.shape[1] // F
+    zc = frame_lanes // H_PAD
+    pieces = max(1, width // 16)
+    rows = H // pieces
+    cells = F * H * width
+    leftmost = me * W_DEV - HALO
+    for frame in range(F):
+        lanes = slice(frame * frame_lanes, (frame + 1) * frame_lanes)
+        chosen = jnp.dot(selection[...], owners[:, lanes], preferred_element_type=jnp.float32)
+        shifted[:, frame] = chosen.reshape(3, width, frame_lanes)
+
+    stem_bias = vectors[0:1]
+    first_gain = vectors[1:2]
+    first_shift = vectors[2:3]
 
     per_block = 128 // zc
     lane128 = lax.broadcasted_iota(jnp.int32, (F, width, 128), 2)
@@ -200,18 +210,17 @@
     for frame in range(F):
 
         def convolve(row):
-            total = jnp.zeros((rows * width, half), jnp.float32)
-            for a in range(max(0, 2 - frame), 3):
-                for b in range(3):
-                    lhs = jnp.concatenate(
-                        [
-                            acts[e, frame + a - 2, pl.ds(row + b, rows)].reshape(rows * width, full)
-                            for e in range(3)
-                        ],
-                        axis=1,
+            used = range(max(0, 2 - frame) * 9, 27)
+            lhs = jnp.concatenate(
+                [
+                    acts[tap % 3, frame + tap // 9 - 2, pl.ds(row + tap // 3 % 3, rows)].reshape(
+                        rows * width, full
                     )
-                    tap = 9 * a + 3 * b
-                    total += times(lhs, weight, range(tap, tap + 3))
+                    for tap in used
+                ],
+                axis=1,
+            )
+            total = times(lhs, weight, used)
             value = (total + first_bias).astype(jnp.bfloat16).astype(jnp.float32)
             put(produced, span(frame, row), value)
             sums[2:3, 0:half] += jnp.sum(value, axis=0, keepdims=True)
@@ -248,8 +257,7 @@
     hidden_in,
     weight_own,
     weight_far,
-    small_own,
-    small_other,
+    vectors,
     up_weight,
     up_bias,
     out,
@@ -291,18 +299,19 @@
 
 
     def convolve(weight):
-        total = jnp.zeros((inner * rows, half), jnp.float32)
-        for pair in range(9):
-            lhs = jnp.concatenate(
-                [taps[pair, e : e + inner].reshape(inner * rows, full) for e in range(3)], axis=1
-            )
-            total += times(lhs, weight, range(3 * pair, 3 * pair + 3))
-        return total
+        lhs = jnp.concatenate(
+            [
+                taps[tap // 3, tap % 3 : tap % 3 + inner].reshape(inner * rows, full)
+                for tap in range(27)
+            ],
+            axis=1,
+        )
+        return times(lhs, weight, range(27))
 
     mine = convolve(weight_own)
     fetch.wait()
     theirs = convolve(weight_other)
-    second_out = joined(mine + small_own[3:4], theirs + small_other[3:4], core)
+    second_out = joined(mine, theirs, core) + vectors[3:4]
     hidden = hidden_in[...].astype(jnp.float32) + second_out.reshape(inner, rows, full)
     spot = lax.broadcasted_iota(jnp.int32, (inner, rows, full), 0) + me * W_DEV - 1
     hidden = jnp.where((spot >= 0) & (spot < width), hidden, 0.0).astype(jnp.bfloat16)
@@ -400,18 +409,29 @@
     window = W_DEV + 2 * HALO
     vmem = pl.BlockSpec(memory_space=pltpu.VMEM)
     far = pl.BlockSpec(memory_space=pltpu.HBM)
+    selection, stem_full, vectors = pl.pallas_call(
+        functools.partial(prepare_kernel, power),
+        out_shape=(
+            jax.ShapeDtypeStruct((3 * width, PITCH * tile_count), jnp.bfloat16),
+            jax.ShapeDtypeStruct((3, 256, full), jnp.bfloat16),
+            jax.ShapeDtypeStruct((small.shape[0], full), jnp.float32),
+        ),
+        in_specs=[pl.BlockSpec(memory_space=pltpu.SMEM)] + [vmem] * 4,
+        out_specs=(vmem,) * 3,
+        cost_estimate=pl.CostEstimate(flops=10**8, bytes_accessed=10**6, transcendentals=0),
+        compiler_params=pltpu.CompilerParams(vmem_limit_bytes=8 * 1024 * 1024),
+    )(tile_counts, stem_weight, stem_other, small, small_other)
     act, hidden = pl.pallas_call(
-        functools.partial(first_kernel, power),
+        first_kernel,
         out_shape=(
             jax.ShapeDtypeStruct((window, F * H, half), jnp.bfloat16),
             jax.ShapeDtypeStruct((window - 2, frames * H, full), jnp.bfloat16),
         ),
-        in_specs=[pl.BlockSpec(memory_space=pltpu.SMEM)] + [vmem] * 5 + [far],
+        in_specs=[vmem] * 5 + [far],
         out_specs=(vmem, vmem),
         scratch_shapes=[
             pltpu.VMEM((3, F, width, H_PAD * zc), jnp.float32),
             pltpu.VMEM((F, H, width, 256), jnp.bfloat16),
-            pltpu.VMEM((3, 256, full), jnp.bfloat16),
             pltpu.VMEM((full // 128, F * H * width, 128), jnp.float32),
             pltpu.VMEM((3, F, H + 2, width, full), jnp.bfloat16),
             pltpu.VMEM((pl.cdiv(half, 128), F * H * width, 128), jnp.float32),
@@ -424,15 +444,24 @@
             bytes_accessed=27 * full * half * 2,
             transcendentals=F * H * width * full,
         ),
-        compiler_params=pltpu.CompilerParams(vmem_limit_bytes=min(60, 12 + 12 * width // 16) * 1024 * 1024),
-    )(tile_counts, owners, stem_weight, stem_other, small, small_other, first_weight)
+        compiler_params=pltpu.CompilerParams(
+            vmem_limit_bytes=min(60, 12 + 12 * width // 16) * 1024 * 1024
+        ),
+    )(
+        owners,
+        selection,
+        stem_full,
+        vectors,
+        small,
+        pltpu.with_memory_space_constraint(first_weight, pltpu.HBM),
+    )
 
     act_other = lax.ppermute(act, "chan", swap)
 
     out = pl.pallas_call(
         functools.partial(second_kernel, tile_count),
         out_shape=jax.ShapeDtypeStruct((frames, 2 * H, 2 * W_DEV, out_channels), jnp.bfloat16),
-        in_specs=[vmem] * 4 + [far] + [vmem] * 4,
+        in_specs=[vmem] * 4 + [far] + [vmem] * 3,
         out_specs=vmem,
         scratch_shapes=[
             pltpu.VMEM((window, 2 * frames * 32 + 8, full), jnp.float32),
@@ -452,9 +481,8 @@
         act_other,
         hidden,
         second_weight,
-        second_other,
-        small,
-        small_other,
+        pltpu.with_memory_space_constraint(second_other, pltpu.HBM),
+        vectors,
         upsample_weight,
         upsample_bias.reshape(1, -1),
     )

time: 47.6 us -> 43.6 us (0.916)
  local copies, waits for them, and re-layouts: 5.77 us -> 3.66 us
  waiting for transfers between devices: 9.59 us -> 7.75 us
  Pallas kernels: 23.1 us -> 23.6 us
  starting transfers between devices: 8.65 us -> 8.16 us
    ppermute x3, waiting for transfers between devices: 8.01 us -> 5.02 us  [gathered(): moved = lax.ppermute(block, axis, [(i, i ^ step) for i in range(count)])]
    unnamed x12 -> x10, local copies, waits for them, and re-layouts: 3.72 us -> 1.61 us
    ppermute x1, waiting for transfers between devices: 0.01 us -> 1.16 us  [on_device(): small_other = lax.ppermute(small, 'chan', swap)]
    pallas_call x1 -> x2, Pallas kernels: 14.7 us -> 15.5 us  [the longest x1 14.8 us: on_device(): pl.pallas_call(first_kernel, out_shape=(jax.ShapeDtypeStruct((window, F *...]
    ppermute x1, starting transfers between devices: 0.5 us -> 0.01 us  [on_device(): stem_other = lax.ppermute(stem_weight, 'chan', swap)]
  transfers between devices with their start and end apart: 7 -> 7, of which waited for: 4 -> 5; matrix products, arithmetic and copies ran while one was open for 4% -> 5% of each run, Pallas kernels for 31% -> 36%
where the time goes in v2:
time: 43.6 us; the launch traced here: 43.3 us
  Pallas kernels  23.6 us (54%)
  starting transfers between devices  8.16 us (19%)
  waiting for transfers between devices  7.75 us (18%)
  local copies, waits for them, and re-layouts  3.66 us (8%)
    pallas_call x1, Pallas kernels, on_device(): pl.pallas_call(first_kernel, out_shape=(jax.ShapeDtypeStruct((window, F *...  14.8 us
    pallas_call x1, Pallas kernels, on_device(): pl.pallas_call(functools.partial(second_kernel, tile_count), out_shape=ja...  8.01 us
    ppermute x3, starting transfers between devices, gathered(): moved = lax.ppermute(block, axis, [(i, i ^ step) for i in range(count)])  7.53 us
    ppermute x3, waiting for transfers between devices, gathered(): moved = lax.ppermute(block, axis, [(i, i ^ step) for i in range(count)])  5.02 us
    unnamed x10, local copies, waits for them, and re-layouts  1.61 us
    ppermute x1, waiting for transfers between devices, on_device(): act_other = lax.ppermute(act, 'chan', swap)  1.57 us
    ppermute x1, waiting for transfers between devices, on_device(): small_other = lax.ppermute(small, 'chan', swap)  1.16 us
    reshape x1, local copies, waits for them, and re-layouts, on_device(): padded = owner_latent.reshape(1, slot_count, F, H, zc)  0.88 us
  transfers between devices with their start and end apart: 7, of which 5 were waited for; matrix products, arithmetic and copies ran while one was open for 5% of the time, Pallas kernels for 36%

profile of v2, /device:TPU:0, one launch (start us, length us, event | category | flops | bytes accessed | tf_op | source)
XLA Modules:
  0.0 43.3 jit_solution(13853487212503963584)
XLA Ops:
  0.0 0.5 %collective-permute-start.6 = (bf16[27,192,384]{2,1,0:T(8,128)(2,1)}, bf16[27,192,384]{2,1,0:T(8,128)(2,1)}, u32[]{:S(2)}, u32[]{:S(2)}) collective-permute-start(bf16[27,192,384]{2,1,0:T(8,128)(2,1)} %bitcast.15), channel_id=1, source_target_pairs={{0,1},{1,0},{2,3},{3,2},{4,5},{5,4},{6,7},{7,6},{8,9},{9,8},{10,11... | collective-permute-start | bytes 11943944 | tf_op jit(solution)/shard_map/ppermute | solution.py:405
  0.5 0.9 %reshape.12 = bf16[1,5,4,24,16]{4,3,2,1,0:T(8,128)(2,1)S(1)} reshape(bf16[1,5,1536]{2,1,0:T(8,128)(2,1)} %param.14) | data formatting | bytes 30720 | tf_op jit(solution)/shard_map/reshape | solution.py:387
  1.4 0.1 pad.4
  1.4 0.3 reshape.13
  1.8 2.6 %collective-permute-start = (bf16[1,8,2048]{2,1,0:T(8,128)(2,1)S(1)}, bf16[1,8,2048]{2,1,0:T(8,128)(2,1)S(1)}, u32[]{:S(2)}, u32[]{:S(2)}) collective-permute-start(bf16[1,8,2048]{2,1,0:T(8,128)(2,1)S(1)} %reshape.13), channel_id=1, source_target_pairs={{0,2},{2,0},{4,6},{6,4},{8,10},{10,8},{12,14},{14,12},{1,3},{3,1},... | collective-permute-start | bytes 98312 | tf_op jit(solution)/shard_map/ppermute | solution.py:353
  4.3 2.1 %collective-permute-done = bf16[1,8,2048]{2,1,0:T(8,128)(2,1)S(1)} collective-permute-done((bf16[1,8,2048]{2,1,0:T(8,128)(2,1)S(1)}, bf16[1,8,2048]{2,1,0:T(8,128)(2,1)S(1)}, u32[]{:S(2)}, u32[]{:S(2)}) %collective-permute-start) | collective-permute-done | bytes 32800 | tf_op jit(solution)/shard_map/ppermute | solution.py:353
  6.4 2.0 %collective-permute-start.1 = (bf16[2,8,2048]{2,1,0:T(8,128)(2,1)S(1)}, bf16[2,8,2048]{2,1,0:T(8,128)(2,1)S(1)}, u32[]{:S(2)}, u32[]{:S(2)}) collective-permute-start(bf16[2,8,2048]{2,1,0:T(8,128)(2,1)S(1)} %pad_maximum_fusion.1), channel_id=1, source_target_pairs={{0,4},{2,6},{4,0},{6,2},{8,12},{10,14},{12,8},{14,10},{1,5},{3,7},... | collective-permute-start | bytes 196616 | tf_op jit(solution)/shard_map/ppermute | solution.py:353
  8.4 2.4 %collective-permute-done.1 = bf16[2,8,2048]{2,1,0:T(8,128)(2,1)S(1)} collective-permute-done((bf16[2,8,2048]{2,1,0:T(8,128)(2,1)S(1)}, bf16[2,8,2048]{2,1,0:T(8,128)(2,1)S(1)}, u32[]{:S(2)}, u32[]{:S(2)}) %collective-permute-start.1) | collective-permute-done | bytes 65568 | tf_op jit(solution)/shard_map/ppermute | solution.py:353
  10.7 3.0 %collective-permute-start.2 = (bf16[4,8,2048]{2,1,0:T(8,128)(2,1)S(1)}, bf16[4,8,2048]{2,1,0:T(8,128)(2,1)S(1)}, u32[]{:S(2)}, u32[]{:S(2)}) collective-permute-start(bf16[4,8,2048]{2,1,0:T(8,128)(2,1)S(1)} %pad_maximum_fusion), channel_id=1, source_target_pairs={{0,8},{2,10},{4,12},{6,14},{8,0},{10,2},{12,4},{14,6},{1,9},{3,11}... | collective-permute-start | bytes 393224 | tf_op jit(solution)/shard_map/ppermute | solution.py:353
  13.7 0.8 %stack.31.small_own = f32[8,192]{1,0:T(8,128)S(1)} concatenate(f32[1,192]{1,0:T(1,128)} %bitcast.19, f32[1,192]{1,0:T(1,128)} %bitcast.20, f32[1,192]{1,0:T(1,128)} %bitcast.21, f32[1,192]{1,0:T(1,128)} %bitcast.22, f32[1,192]{1,0:T(1,128)} %bitcast.23, f32[1,192]{1,0:T(1,128)} %bitcast.24, f32[1,192]{1,0:T(1,128)} %bitcast.25, f32[1,192]{1,0:T(1,128)S(1)} %stack_broadcast_in_dim.3), dimensions={0} | concatenate | bytes 12288 | tf_op jit(solution)/shard_map/stack | solution.py:391
  14.5 0.1 collective-permute-start.4
  14.6 1.2 %collective-permute-done.4.small_other = f32[8,192]{1,0:T(8,128)S(1)} collective-permute-done((f32[8,192]{1,0:T(8,128)S(1)}, f32[8,192]{1,0:T(8,128)S(1)}, u32[]{:S(2)}, u32[]{:S(2)}) %collective-permute-start.4) | collective-permute-done | bytes 6176 | tf_op jit(solution)/shard_map/ppermute | solution.py:403
  15.8 0.0 collective-permute-done.3.stem_other
  15.8 0.9 %copy-done.2 = bf16[27,16,192]{2,1,0:T(8,128)(2,1)S(1)} copy-done((bf16[27,16,192]{2,1,0:T(8,128)(2,1)S(1)}, bf16[27,16,192]{2,1,0:T(8,128)(2,1)}, u32[]{:S(2)}) %copy-start.2) | copy-done | bytes 165912
  16.7 0.7 %copy-done.4 = s32[8]{0:T(128)S(1)} copy-done((s32[8]{0:T(128)S(1)}, s32[8]{0:T(128)}, u32[]{:S(2)}) %copy-start.4) | copy-done | bytes 56
  17.4 0.7 %shard_map.136 = (bf16[48,64]{1,0:T(8,128)(2,1)S(1)}, bf16[3,256,384]{2,1,0:T(8,128)(2,1)S(1)}, f32[8,384]{1,0:T(8,128)S(1)}) custom-call(s32[8]{0:T(128)S(1)} %copy-done.4, bf16[27,16,192]{2,1,0:T(8,128)(2,1)S(1)} %copy-done.2, bf16[27,16,192]{2,1,0:T(8,128)(2,1)S(1)} %collective-permute-done.3.stem_other, f32[8,192]{1,0:T(8,128)S(1)} %stack.31.small_own, ...), custom_call_target="tpu_custom_call" | custom-call | flops 100000000 | bytes 1000000 | tf_op jit(solution)/shard_map/pallas_call | solution.py:412
  18.1 0.6 %collective-permute-done.2 = bf16[4,8,2048]{2,1,0:T(8,128)(2,1)S(1)} collective-permute-done((bf16[4,8,2048]{2,1,0:T(8,128)(2,1)S(1)}, bf16[4,8,2048]{2,1,0:T(8,128)(2,1)S(1)}, u32[]{:S(2)}, u32[]{:S(2)}) %collective-permute-start.2) | collective-permute-done | bytes 131104 | tf_op jit(solution)/shard_map/ppermute | solution.py:353
  18.7 0.0 copy-start
  18.7 0.0 copy-start.1
  18.8 0.0 copy-start.3
  18.8 14.8 %shard_map.137 = (bf16[6,96,192]{2,1,0:T(8,128)(2,1)S(1)}, bf16[4,48,384]{2,1,0:T(8,128)(2,1)S(1)}) custom-call(bf16[64,2048]{1,0:T(8,128)(2,1)S(1)} %maximum_bitcast_fusion.owners, bf16[48,64]{1,0:T(8,128)(2,1)S(1)} %get-tuple-element.10.selection, bf16[3,256,384]{2,1,0:T(8,128)(2,1)S(1)} %get-tuple-element.11.stem_full, ...), custom_call_target="tpu_custom_call" | custom-call | flops 4586471424 | bytes 3981312 | tf_op jit(solution)/shard_map/pallas_call | solution.py:424
  33.6 0.1 collective-permute-start.5
  33.7 1.6 %collective-permute-done.5.act_other = bf16[6,96,192]{2,1,0:T(8,128)(2,1)S(1)} collective-permute-done((bf16[6,96,192]{2,1,0:T(8,128)(2,1)S(1)}, bf16[6,96,192]{2,1,0:T(8,128)(2,1)S(1)}, u32[]{:S(2)}, u32[]{:S(2)}) %collective-permute-start.5) | collective-permute-done | bytes 221216 | tf_op jit(solution)/shard_map/ppermute | solution.py:459
  35.3 8.0 %shard_map.138 = bf16[2,48,4,192]{3,2,1,0:T(4,128)(2,1)} custom-call(bf16[6,96,192]{2,1,0:T(8,128)(2,1)S(1)} %get-tuple-element.13.act_own, bf16[6,96,192]{2,1,0:T(8,128)(2,1)S(1)} %collective-permute-done.5.act_other, bf16[4,48,384]{2,1,0:T(8,128)(2,1)S(1)} %get-tuple-element.14.hidden_in, bf16[27,192,384]{2,1,0:T(8,128)(2,1)S(1)} %bitcast.16, ...), custom_call_target="tpu_custom_call" | custom-call | flops 1528823808 | bytes 7962624 | tf_op jit(solution)/shard_map/pallas_call | solution.py:461
  (11 shorter events, 0.1 us)
Async XLA Ops:
  0.0 35.3 %collective-permute-start.6 = (bf16[27,192,384]{2,1,0:T(8,128)(2,1)}, bf16[27,192,384]{2,1,0:T(8,128)(2,1)}, u32[]{:S(2)}, u32[]{:S(2)}) collective-permute-start(bf16[27,192,384]{2,1,0:T(8,128)(2,1)} %bitcast.15), channel_id=1, source_target_pairs={{0,1},{1,0},{2,3},{3,2},{4,5},{5,4},{6,7},{7,6},{8,9},{9,8},{10,11... | collective-permute-start | bytes 11943944 | tf_op jit(solution)/shard_map/ppermute | solution.py:405
  1.8 4.6 %collective-permute-start = (bf16[1,8,2048]{2,1,0:T(8,128)(2,1)S(1)}, bf16[1,8,2048]{2,1,0:T(8,128)(2,1)S(1)}, u32[]{:S(2)}, u32[]{:S(2)}) collective-permute-start(bf16[1,8,2048]{2,1,0:T(8,128)(2,1)S(1)} %reshape.13), channel_id=1, source_target_pairs={{0,2},{2,0},{4,6},{6,4},{8,10},{10,8},{12,14},{14,12},{1,3},{3,1},... | collective-permute-start | bytes 98312 | tf_op jit(solution)/shard_map/ppermute | solution.py:353
  6.4 4.3 %collective-permute-start.1 = (bf16[2,8,2048]{2,1,0:T(8,128)(2,1)S(1)}, bf16[2,8,2048]{2,1,0:T(8,128)(2,1)S(1)}, u32[]{:S(2)}, u32[]{:S(2)}) collective-permute-start(bf16[2,8,2048]{2,1,0:T(8,128)(2,1)S(1)} %pad_maximum_fusion.1), channel_id=1, source_target_pairs={{0,4},{2,6},{4,0},{6,2},{8,12},{10,14},{12,8},{14,10},{1,5},{3,7},... | collective-permute-start | bytes 196616 | tf_op jit(solution)/shard_map/ppermute | solution.py:353
  8.4 7.4 %collective-permute-start.3 = (bf16[27,16,192]{2,1,0:T(8,128)(2,1)}, bf16[27,16,192]{2,1,0:T(8,128)(2,1)S(1)}, u32[]{:S(2)}, u32[]{:S(2)}) collective-permute-start(bf16[27,16,192]{2,1,0:T(8,128)(2,1)} %stem_own.1), channel_id=1, source_target_pairs={{0,1},{1,0},{2,3},{3,2},{4,5},{5,4},{6,7},{7,6},{8,9},{9,8},{10,11... | collective-permute-start | bytes 497672 | tf_op jit(solution)/shard_map/ppermute | solution.py:404
  10.7 8.0 %collective-permute-start.2 = (bf16[4,8,2048]{2,1,0:T(8,128)(2,1)S(1)}, bf16[4,8,2048]{2,1,0:T(8,128)(2,1)S(1)}, u32[]{:S(2)}, u32[]{:S(2)}) collective-permute-start(bf16[4,8,2048]{2,1,0:T(8,128)(2,1)S(1)} %pad_maximum_fusion), channel_id=1, source_target_pairs={{0,8},{2,10},{4,12},{6,14},{8,0},{10,2},{12,4},{14,6},{1,9},{3,11}... | collective-permute-start | bytes 393224 | tf_op jit(solution)/shard_map/ppermute | solution.py:353
  14.5 1.2 %collective-permute-start.4 = (f32[8,192]{1,0:T(8,128)S(1)}, f32[8,192]{1,0:T(8,128)S(1)}, u32[]{:S(2)}, u32[]{:S(2)}) collective-permute-start(f32[8,192]{1,0:T(8,128)S(1)} %stack.31.small_own), channel_id=1, source_target_pairs={{0,1},{1,0},{2,3},{3,2},{4,5},{5,4},{6,7},{7,6},{8,9},{9,8},{10,11... | collective-permute-start | bytes 18440 | tf_op jit(solution)/shard_map/ppermute | solution.py:403
  15.8 0.9 %copy-start.2 = (bf16[27,16,192]{2,1,0:T(8,128)(2,1)S(1)}, bf16[27,16,192]{2,1,0:T(8,128)(2,1)}, u32[]{:S(2)}) copy-start(bf16[27,16,192]{2,1,0:T(8,128)(2,1)} %stem_own.1) | copy-start | bytes 497668
  16.7 0.7 %copy-start.4 = (s32[8]{0:T(128)S(1)}, s32[8]{0:T(128)}, u32[]{:S(2)}) copy-start(s32[8]{0:T(128)} %counts.1) | copy-start | bytes 100
  18.7 16.5 %copy-start = (bf16[27,384,192]{1,2,0:T(8,128)(2,1)S(1)}, bf16[27,384,192]{1,2,0:T(8,128)(2,1)}, u32[]{:S(2)}) copy-start(bf16[27,384,192]{1,2,0:T(8,128)(2,1)} %param.24) | copy-start | bytes 11943940
  18.7 16.5 %copy-start.1 = (bf16[9,384,192]{1,2,0:T(8,128)(2,1)S(1)}, bf16[9,384,192]{1,2,0:T(8,128)(2,1)}, u32[]{:S(2)}) copy-start(bf16[9,384,192]{1,2,0:T(8,128)(2,1)} %param.26) | copy-start | bytes 3981316
  18.8 16.5 %copy-start.3 = (f32[192]{0:T(256)S(1)}, f32[192]{0:T(256)}, u32[]{:S(2)}) copy-start(f32[192]{0:T(256)} %param.27) | copy-start | bytes 2308
  33.6 1.6 %collective-permute-start.5 = (bf16[6,96,192]{2,1,0:T(8,128)(2,1)S(1)}, bf16[6,96,192]{2,1,0:T(8,128)(2,1)S(1)}, u32[]{:S(2)}, u32[]{:S(2)}) collective-permute-start(bf16[6,96,192]{2,1,0:T(8,128)(2,1)S(1)} %get-tuple-element.13.act_own), channel_id=1, source_target_pairs={{0,1},{1,0},{2,3},{3,2},{4,5},{5,4},{6,7},{7,6},{8,9},{9,8},{10,11... | collective-permute-start | bytes 663560 | tf_op jit(solution)/shard_map/ppermute | solution.py:459

commit v3 on v2

--- a/solution.py
+++ b/solution.py
@@ -48,6 +48,20 @@
     for block in range(ref.shape[0]):
         parts.append(ref[block, place, :][:, : channels - block * 128])
     return jnp.concatenate(parts, axis=1)
+
+
+def squares(ref, mean):
+    channels = mean.shape[1]
+    step = 64
+
+    def add(i, total):
+        spread = take(ref, pl.ds(pl.multiple_of(i * step, step), step), channels) - mean
+        return total + jnp.sum((spread * spread).reshape(step // 8, 8, channels), axis=0)
+
+    total = lax.fori_loop(
+        0, ref.shape[1] // step, add, jnp.zeros((8, channels), jnp.float32), unroll=2
+    )
+    return jnp.broadcast_to(jnp.sum(total, axis=0, keepdims=True), (8, channels))
 
 
 def times(lhs, weight, taps):
@@ -103,6 +117,7 @@
     vectors,
     small_own,
     weight_far,
+    unread,
     act_out,
     hidden_out,
     shifted,
@@ -122,7 +137,7 @@
     core = lax.axis_index("chan")
     full, half = vectors.shape[1], small_own.shape[1]
     frame_lanes = owners.shape[1] // F
-    zc = frame_lanes // H_PAD
+    zc = frame_lanes // H
     pieces = max(1, width // 16)
     rows = H // pieces
     cells = F * H * width
@@ -130,7 +145,9 @@
     for frame in range(F):
         lanes = slice(frame * frame_lanes, (frame + 1) * frame_lanes)
         chosen = jnp.dot(selection[...], owners[:, lanes], preferred_element_type=jnp.float32)
-        shifted[:, frame] = chosen.reshape(3, width, frame_lanes)
+        blank = jnp.zeros((3 * width, shifted.shape[3] - frame_lanes), jnp.float32)
+        chosen = pltpu.roll(jnp.concatenate([chosen, blank], axis=1), zc, axis=1)
+        shifted[:, frame] = chosen.reshape(3, width, shifted.shape[3])
 
     stem_bias = vectors[0:1]
     first_gain = vectors[1:2]
@@ -173,14 +190,7 @@
 
     per_group = full // GROUPS
     mean = group_mean(jnp.broadcast_to(sums[0:1, :], (8, full)), per_group, cells)
-    for frame in range(F):
-
-        def squares(row):
-            spread = take(hidden, span(frame, row), full) - mean
-            sums[1:2, :] += jnp.sum(spread * spread, axis=0, keepdims=True)
-
-        over_pieces(squares)
-    variance = group_mean(jnp.broadcast_to(sums[1:2, :], (8, full)), per_group, cells)
+    variance = group_mean(squares(hidden, mean), per_group, cells)
     scale = lax.rsqrt(variance + EPSILON) * first_gain
 
     spot = lax.broadcasted_iota(jnp.int32, (1, width, full), 1) + leftmost
@@ -193,17 +203,20 @@
             acts[e, frame, H + 1] = zero_row
     for frame in range(F):
 
-        def activate(row):
-            spread = take(hidden, span(frame, row), full) - mean
-            value = silu(spread * scale + first_shift).reshape(rows, width, full)
+        def activate(i, _):
+            row = i * 2
+            place = pl.ds(pl.multiple_of((frame * H + row) * width, 16), 2 * width)
+            spread = take(hidden, place, full) - mean
+            value = silu(spread * scale + first_shift).reshape(2, width, full)
             left = jnp.where(spot == 0, 0.0, pltpu.roll(value, 1, axis=1))
             right = jnp.where(spot == width - 1, 0.0, pltpu.roll(value, width - 1, axis=1))
-            place = pl.ds(row + 1, rows)
+            place = pl.ds(row + 1, 2)
             acts[0, frame, place] = left.astype(jnp.bfloat16)
             acts[1, frame, place] = value.astype(jnp.bfloat16)
             acts[2, frame, place] = right.astype(jnp.bfloat16)
-
-        over_pieces(activate)
+            return _
+
+        lax.fori_loop(0, H // 2, activate, 0, unroll=2)
 
     fetch.wait()
     first_bias = small_own[4:5]
@@ -228,14 +241,7 @@
         over_pieces(convolve)
 
     mean = group_mean(jnp.broadcast_to(sums[2:3, 0:half], (8, half)), per_group, cells)
-    for frame in range(F):
-
-        def squares_again(row):
-            spread = take(produced, span(frame, row), half) - mean
-            sums[3:4, 0:half] += jnp.sum(spread * spread, axis=0, keepdims=True)
-
-        over_pieces(squares_again)
-    variance = group_mean(jnp.broadcast_to(sums[3:4, 0:half], (8, half)), per_group, cells)
+    variance = group_mean(squares(produced, mean), per_group, cells)
     scale = lax.rsqrt(variance + EPSILON) * small_own[5:6]
     second_shift = small_own[6:7]
     for spot_at in range(W_DEV + 2 * HALO):
@@ -256,7 +262,7 @@
     act_other,
     hidden_in,
     weight_own,
-    weight_far,
+    weight_other,
     vectors,
     up_weight,
     up_bias,
@@ -264,11 +270,7 @@
     slots,
     taps,
     flat,
-    weight_other,
-    arrival,
 ):
-    fetch = pltpu.make_async_copy(weight_far, weight_other, arrival)
-    fetch.start()
     width = tile_count * W_DEV
     me = lax.axis_index("tile")
     core = lax.axis_index("chan")
@@ -309,7 +311,6 @@
         return times(lhs, weight, range(27))
 
     mine = convolve(weight_own)
-    fetch.wait()
     theirs = convolve(weight_other)
     second_out = joined(mine, theirs, core) + vectors[3:4]
     hidden = hidden_in[...].astype(jnp.float32) + second_out.reshape(inner, rows, full)
@@ -319,11 +320,19 @@
 
     line = lax.broadcasted_iota(jnp.int32, (inner * frames, H, half), 1)
     upper, lower = [], []
+    pad = jnp.zeros((256 - half % 256, full), jnp.bfloat16)
+    rhs = jnp.concatenate(
+        [part for tap in range(9) for part in (up_weight[tap], pad)], axis=0
+    )
+    spread = rhs.shape[0] // 9
+    every = lax.dot_general(
+        hidden, rhs, (((1,), (1,)), ((), ())), preferred_element_type=jnp.float32
+    )
     for e in range(3):
-        made = [
-            times(hidden, up_weight, [3 * b + e]).reshape(inner * frames, H, half)
-            for b in range(3)
-        ]
+        made = []
+        for b in range(3):
+            at = (3 * b + e) * spread
+            made.append(every[:, at : at + half].reshape(inner * frames, H, half))
         above = jnp.where(line == 0, 0.0, pltpu.roll(made[0], 1, axis=1))
         below = jnp.where(line == H - 1, 0.0, pltpu.roll(made[2], H - 1, axis=1))
         upper.append((above + made[1] + made[2]).reshape(inner, frames, H, half))
@@ -344,16 +353,10 @@
     out[...] = take(flat, slice(None), out.shape[-1]).astype(jnp.bfloat16).reshape(out.shape)
 
 
-def gathered(block, axis):
-    count = lax.axis_size(axis)
-    if count & (count - 1):
-        return lax.all_gather(block, axis, axis=0, tiled=True), False
-    step = 1
-    while step < count:
-        moved = lax.ppermute(block, axis, [(i, i ^ step) for i in range(count)])
-        block = jnp.concatenate([block, moved], axis=0)
-        step *= 2
-    return block, True
+def exchanged(block, step):
+    count = lax.axis_size("tile")
+    moved = lax.ppermute(block, "tile", [(i, i ^ step) for i in range(count)])
+    return jnp.concatenate([block, moved], axis=0)
 
 
 def on_device(
@@ -384,10 +387,7 @@
     swap = [(0, 1), (1, 0)]
     frames = F // 2
 
-    padded = owner_latent.reshape(1, slot_count, F, H, zc)
-    padded = jnp.pad(
-        padded, ((0, 0), (0, PITCH - slot_count), (0, 0), (1, H_PAD - H - 1), (0, 0))
-    ).reshape(1, PITCH, F * H_PAD * zc)
+    padded = jnp.pad(owner_latent, ((0, 0), (0, PITCH - slot_count), (0, 0)))
     small = jnp.stack(
         [
             stem_bias,
@@ -400,34 +400,54 @@
             jnp.zeros_like(stem_bias),
         ]
     )
-    small_other = lax.ppermute(small, "chan", swap)
-    stem_other = lax.ppermute(stem_weight, "chan", swap)
-    second_other = lax.ppermute(second_weight, "chan", swap)
-    owners, power = gathered(padded, "tile")
-    owners = owners.reshape(tile_count * PITCH, F * H_PAD * zc)
-
     window = W_DEV + 2 * HALO
     vmem = pl.BlockSpec(memory_space=pltpu.VMEM)
     far = pl.BlockSpec(memory_space=pltpu.HBM)
-    selection, stem_full, vectors = pl.pallas_call(
-        functools.partial(prepare_kernel, power),
-        out_shape=(
-            jax.ShapeDtypeStruct((3 * width, PITCH * tile_count), jnp.bfloat16),
-            jax.ShapeDtypeStruct((3, 256, full), jnp.bfloat16),
-            jax.ShapeDtypeStruct((small.shape[0], full), jnp.float32),
-        ),
-        in_specs=[pl.BlockSpec(memory_space=pltpu.SMEM)] + [vmem] * 4,
-        out_specs=(vmem,) * 3,
-        cost_estimate=pl.CostEstimate(flops=10**8, bytes_accessed=10**6, transcendentals=0),
-        compiler_params=pltpu.CompilerParams(vmem_limit_bytes=8 * 1024 * 1024),
-    )(tile_counts, stem_weight, stem_other, small, small_other)
+
+    def prepare(small, small_other, stem_other, power):
+        return pl.pallas_call(
+            functools.partial(prepare_kernel, power),
+            out_shape=(
+                jax.ShapeDtypeStruct((3 * width, PITCH * tile_count), jnp.bfloat16),
+                jax.ShapeDtypeStruct((3, 256, full), jnp.bfloat16),
+                jax.ShapeDtypeStruct((small.shape[0], full), jnp.float32),
+            ),
+            in_specs=[pl.BlockSpec(memory_space=pltpu.SMEM)] + [vmem] * 4,
+            out_specs=(vmem,) * 3,
+            cost_estimate=pl.CostEstimate(flops=10**8, bytes_accessed=10**6, transcendentals=0),
+            compiler_params=pltpu.CompilerParams(vmem_limit_bytes=8 * 1024 * 1024),
+        )(tile_counts, stem_weight, stem_other, small, small_other)
+
+    stem_other = lax.ppermute(stem_weight, "chan", swap)
+    power = tile_count & (tile_count - 1) == 0 and tile_count >= 4
+    if power:
+        owners = exchanged(padded, 1)
+        small_other = lax.ppermute(small, "chan", swap)
+        owners, small_other, stem_other, second_far = lax.optimization_barrier(
+            (owners, small_other, stem_other, second_weight)
+        )
+        second_other = lax.ppermute(second_far, "chan", swap)
+        owners = exchanged(owners, 2)
+        prepared = prepare(small, small_other, stem_other, power)
+        owners, prepared = lax.optimization_barrier((owners, prepared))
+        step = 4
+        while step < tile_count:
+            owners = exchanged(owners, step)
+            step *= 2
+    else:
+        small_other = lax.ppermute(small, "chan", swap)
+        second_other = lax.ppermute(second_weight, "chan", swap)
+        owners = lax.all_gather(padded, "tile", axis=0, tiled=True)
+        prepared = prepare(small, small_other, stem_other, power)
+    selection, stem_full, vectors = prepared
+    owners = owners.reshape(tile_count * PITCH, F * H * zc)
     act, hidden = pl.pallas_call(
         first_kernel,
         out_shape=(
             jax.ShapeDtypeStruct((window, F * H, half), jnp.bfloat16),
             jax.ShapeDtypeStruct((window - 2, frames * H, full), jnp.bfloat16),
         ),
-        in_specs=[vmem] * 5 + [far],
+        in_specs=[vmem] * 5 + [far, pl.BlockSpec(memory_space=pl.ANY)],
         out_specs=(vmem, vmem),
         scratch_shapes=[
             pltpu.VMEM((3, F, width, H_PAD * zc), jnp.float32),
@@ -454,6 +474,7 @@
         vectors,
         small,
         pltpu.with_memory_space_constraint(first_weight, pltpu.HBM),
+        second_other,
     )
 
     act_other = lax.ppermute(act, "chan", swap)
@@ -461,14 +482,12 @@
     out = pl.pallas_call(
         functools.partial(second_kernel, tile_count),
         out_shape=jax.ShapeDtypeStruct((frames, 2 * H, 2 * W_DEV, out_channels), jnp.bfloat16),
-        in_specs=[vmem] * 4 + [far] + [vmem] * 3,
+        in_specs=[vmem] * 8,
         out_specs=vmem,
         scratch_shapes=[
             pltpu.VMEM((window, 2 * frames * 32 + 8, full), jnp.float32),
             pltpu.VMEM((9, window, frames * H, full), jnp.bfloat16),
             pltpu.VMEM((pl.cdiv(out_channels, 128), frames * 2 * H * 2 * W_DEV, 128), jnp.float32),
-            pltpu.VMEM(second_weight.shape, jnp.bfloat16),
-            pltpu.SemaphoreType.DMA,
         ],
         cost_estimate=pl.CostEstimate(
             flops=2 * 4 * 48 * 27 * full * full,
@@ -481,7 +500,7 @@
         act_other,
         hidden,
         second_weight,
-        pltpu.with_memory_space_constraint(second_other, pltpu.HBM),
+        second_other,
         vectors,
         upsample_weight,
         upsample_bias.reshape(1, -1),

time: 43.6 us -> 36.9 us (0.85)
  Pallas kernels: 23.6 us -> 17.3 us
  local copies, waits for them, and re-layouts: 3.66 us -> 3.16 us
    pallas_call x1, Pallas kernels: 8.01 us -> 3.91 us  [on_device(): pl.pallas_call(functools.partial(second_kernel, tile_count), out_shape=ja...]
    pallas_call x1, Pallas kernels: 14.8 us -> 12.7 us  [on_device(): pl.pallas_call(first_kernel, out_shape=(jax.ShapeDtypeStruct((window, F *...]
    reshape x2 -> x0, local copies, waits for them, and re-layouts: 1.2 us -> none  [the longest x1 0.88 us: on_device(): padded = owner_latent.reshape(1, slot_count, F, H, zc)]
    ppermute x1, waiting for transfers between devices: 1.16 us -> 0.23 us  [on_device(): small_other = lax.ppermute(small, 'chan', swap)]
    pad x1, local copies, waits for them, and re-layouts: 0.05 us -> 0.74 us  [on_device(): padded = jnp.pad(owner_latent, ((0, 0), (0, PITCH - slot_count), (0, 0)))]
    ppermute x1, waiting for transfers between devices: 0.01 us -> 0.65 us  [on_device(): stem_other = lax.ppermute(stem_weight, 'chan', swap)]
    ppermute x1, starting transfers between devices: 0.01 us -> 0.5 us  [on_device(): stem_other = lax.ppermute(stem_weight, 'chan', swap)]
  transfers between devices with their start and end apart: 7 -> 7, of which waited for: 5 -> 6; matrix products, arithmetic and copies ran while one was open for 5% -> 2% of each run, Pallas kernels for 36% -> 2%
where the time goes in v3:
time: 36.9 us; the launch traced here: 36.7 us
  Pallas kernels  17.3 us (47%)
  starting transfers between devices  8.23 us (22%)
  waiting for transfers between devices  7.87 us (21%)
  local copies, waits for them, and re-layouts  3.16 us (9%)
    pallas_call x1, Pallas kernels, on_device(): pl.pallas_call(first_kernel, out_shape=(jax.ShapeDtypeStruct((window, F *...  12.7 us
    ppermute x3, starting transfers between devices, exchanged(): moved = lax.ppermute(block, 'tile', [(i, i ^ step) for i in range(count)])  7.23 us
    ppermute x3, waiting for transfers between devices, exchanged(): moved = lax.ppermute(block, 'tile', [(i, i ^ step) for i in range(count)])  5.42 us
    pallas_call x1, Pallas kernels, on_device(): pl.pallas_call(functools.partial(second_kernel, tile_count), out_shape=ja...  3.91 us
    unnamed x10, local copies, waits for them, and re-layouts  1.61 us
    ppermute x1, waiting for transfers between devices, on_device(): act_other = lax.ppermute(act, 'chan', swap)  1.57 us
    another operation x2, local copies, waits for them, and re-layouts, on_device(): jnp.stack([stem_bias, first_gain, first_shift, second_bias, first_bias, s...  0.8 us
    pad x1, local copies, waits for them, and re-layouts, on_device(): padded = jnp.pad(owner_latent, ((0, 0), (0, PITCH - slot_count), (0, 0)))  0.74 us
  transfers between devices with their start and end apart: 7, of which 6 were waited for; matrix products, arithmetic and copies ran while one was open for 2% of the time, Pallas kernels for 2%

profile of v3, /device:TPU:0, one launch (start us, length us, event | category | flops | bytes accessed | tf_op | source)
XLA Modules:
  0.0 36.7 jit_solution(9995409042293269073)
XLA Ops:
  0.0 0.7 %pad.4 = bf16[1,8,1536]{2,1,0:T(8,128)(2,1)S(1)} pad(bf16[1,5,1536]{2,1,0:T(8,128)(2,1)} %param.14, bf16[]{:T(256)} %constant.1.clone.1), padding=0_0x0_3x0_0 | pad | bytes 39938 | tf_op jit(solution)/shard_map/jit(_pad)/pad | solution.py:390
  0.7 3.0 %collective-permute-start = (bf16[1,8,1536]{2,1,0:T(8,128)(2,1)S(1)}, bf16[1,8,1536]{2,1,0:T(8,128)(2,1)S(1)}, u32[]{:S(2)}, u32[]{:S(2)}) collective-permute-start(bf16[1,8,1536]{2,1,0:T(8,128)(2,1)S(1)} %pad.4), channel_id=1, source_target_pairs={{0,2},{2,0},{4,6},{6,4},{8,10},{10,8},{12,14},{14,12},{1,3},{3,1},... | collective-permute-start | bytes 73736 | tf_op jit(solution)/shard_map/ppermute | solution.py:358
  3.7 0.8 %stack.31.small_own = f32[8,192]{1,0:T(8,128)S(1)} concatenate(f32[1,192]{1,0:T(1,128)} %bitcast.17, f32[1,192]{1,0:T(1,128)} %bitcast.18, f32[1,192]{1,0:T(1,128)} %bitcast.19, f32[1,192]{1,0:T(1,128)} %bitcast.20, f32[1,192]{1,0:T(1,128)} %bitcast.21, f32[1,192]{1,0:T(1,128)} %bitcast.22, f32[1,192]{1,0:T(1,128)} %bitcast.23, f32[1,192]{1,0:T(1,128)S(1)} %stack_broadcast_in_dim.3), dimensions={0} | concatenate | bytes 12288 | tf_op jit(solution)/shard_map/stack | solution.py:391
  4.5 0.1 collective-permute-start.1
  4.6 0.5 %collective-permute-start.2 = (bf16[27,16,192]{2,1,0:T(8,128)(2,1)}, bf16[27,16,192]{2,1,0:T(8,128)(2,1)S(1)}, u32[]{:S(2)}, u32[]{:S(2)}) collective-permute-start(bf16[27,16,192]{2,1,0:T(8,128)(2,1)} %stem_own.1), channel_id=1, source_target_pairs={{0,1},{1,0},{2,3},{3,2},{4,5},{5,4},{6,7},{7,6},{8,9},{9,8},{10,11... | collective-permute-start | bytes 497672 | tf_op jit(solution)/shard_map/ppermute | solution.py:421
  5.1 0.4 %collective-permute-done = bf16[1,8,1536]{2,1,0:T(8,128)(2,1)S(1)} collective-permute-done((bf16[1,8,1536]{2,1,0:T(8,128)(2,1)S(1)}, bf16[1,8,1536]{2,1,0:T(8,128)(2,1)S(1)}, u32[]{:S(2)}, u32[]{:S(2)}) %collective-permute-start) | collective-permute-done | bytes 24608 | tf_op jit(solution)/shard_map/ppermute | solution.py:358
  5.6 0.2 collective-permute-done.1.small_other
  5.8 0.7 %collective-permute-done.2.stem_other = bf16[27,16,192]{2,1,0:T(8,128)(2,1)S(1)} collective-permute-done((bf16[27,16,192]{2,1,0:T(8,128)(2,1)}, bf16[27,16,192]{2,1,0:T(8,128)(2,1)S(1)}, u32[]{:S(2)}, u32[]{:S(2)}) %collective-permute-start.2) | collective-permute-done | bytes 165920 | tf_op jit(solution)/shard_map/ppermute | solution.py:421
  6.4 0.4 %collective-permute-start.5 = (bf16[27,192,384]{2,1,0:T(8,128)(2,1)}, bf16[27,192,384]{2,1,0:T(8,128)(2,1)S(1)}, u32[]{:S(2)}, u32[]{:S(2)}) collective-permute-start(bf16[27,192,384]{2,1,0:T(8,128)(2,1)} %bitcast.13), channel_id=1, source_target_pairs={{0,1},{1,0},{2,3},{3,2},{4,5},{5,4},{6,7},{7,6},{8,9},{9,8},{10,11... | collective-permute-start | bytes 11943944 | tf_op jit(solution)/shard_map/ppermute | solution.py:429
  6.8 1.6 %collective-permute-start.3 = (bf16[2,8,1536]{2,1,0:T(8,128)(2,1)S(1)}, bf16[2,8,1536]{2,1,0:T(8,128)(2,1)S(1)}, u32[]{:S(2)}, u32[]{:S(2)}) collective-permute-start(bf16[2,8,1536]{2,1,0:T(8,128)(2,1)S(1)} %pad_maximum_fusion.1), channel_id=1, source_target_pairs={{0,4},{2,6},{4,0},{6,2},{8,12},{10,14},{12,8},{14,10},{1,5},{3,7},... | collective-permute-start | bytes 147464 | tf_op jit(solution)/shard_map/ppermute | solution.py:358
  8.4 0.9 %copy-done.2 = bf16[27,16,192]{2,1,0:T(8,128)(2,1)S(1)} copy-done((bf16[27,16,192]{2,1,0:T(8,128)(2,1)S(1)}, bf16[27,16,192]{2,1,0:T(8,128)(2,1)}, u32[]{:S(2)}) %copy-start.2) | copy-done | bytes 165912
  9.3 0.7 %copy-done.4 = s32[8]{0:T(128)S(1)} copy-done((s32[8]{0:T(128)S(1)}, s32[8]{0:T(128)}, u32[]{:S(2)}) %copy-start.4) | copy-done | bytes 56
  10.0 0.7 %shard_map.136 = (bf16[48,64]{1,0:T(8,128)(2,1)S(1)}, bf16[3,256,384]{2,1,0:T(8,128)(2,1)S(1)}, f32[8,384]{1,0:T(8,128)S(1)}) custom-call(s32[8]{0:T(128)S(1)} %copy-done.4, bf16[27,16,192]{2,1,0:T(8,128)(2,1)S(1)} %copy-done.2, bf16[27,16,192]{2,1,0:T(8,128)(2,1)S(1)} %collective-permute-done.2.stem_other, f32[8,192]{1,0:T(8,128)S(1)} %stack.31.small_own, ...), custom_call_target="tpu_custom_call" | custom-call | flops 100000000 | bytes 1000000 | tf_op jit(solution)/shard_map/pallas_call | solution.py:408
  10.7 0.2 collective-permute-done.3
  10.9 2.7 %collective-permute-start.4 = (bf16[4,8,1536]{2,1,0:T(8,128)(2,1)S(1)}, bf16[4,8,1536]{2,1,0:T(8,128)(2,1)S(1)}, u32[]{:S(2)}, u32[]{:S(2)}) collective-permute-start(bf16[4,8,1536]{2,1,0:T(8,128)(2,1)S(1)} %pad_maximum_fusion), channel_id=1, source_target_pairs={{0,8},{2,10},{4,12},{6,14},{8,0},{10,2},{12,4},{14,6},{1,9},{3,11}... | collective-permute-start | bytes 294920 | tf_op jit(solution)/shard_map/ppermute | solution.py:358
  13.6 4.8 %collective-permute-done.4 = bf16[4,8,1536]{2,1,0:T(8,128)(2,1)S(1)} collective-permute-done((bf16[4,8,1536]{2,1,0:T(8,128)(2,1)S(1)}, bf16[4,8,1536]{2,1,0:T(8,128)(2,1)S(1)}, u32[]{:S(2)}, u32[]{:S(2)}) %collective-permute-start.4) | collective-permute-done | bytes 98336 | tf_op jit(solution)/shard_map/ppermute | solution.py:358
  18.4 0.0 collective-permute-done.5.unread.weight_other
  18.4 0.0 copy-start
  18.4 0.0 copy-start.1
  18.4 0.0 copy-start.3
  18.4 12.7 %shard_map.137 = (bf16[6,96,192]{2,1,0:T(8,128)(2,1)S(1)}, bf16[4,48,384]{2,1,0:T(8,128)(2,1)S(1)}) custom-call(bf16[64,1536]{1,0:T(8,128)(2,1)S(1)} %maximum_bitcast_fusion.owners, bf16[48,64]{1,0:T(8,128)(2,1)S(1)} %get-tuple-element.25.selection, bf16[3,256,384]{2,1,0:T(8,128)(2,1)S(1)} %get-tuple-element.26.stem_full, ...), custom_call_target="tpu_custom_call" | custom-call | flops 4586471424 | bytes 3981312 | tf_op jit(solution)/shard_map/pallas_call | solution.py:444
  31.1 0.1 collective-permute-start.6
  31.2 1.6 %collective-permute-done.6.act_other = bf16[6,96,192]{2,1,0:T(8,128)(2,1)S(1)} collective-permute-done((bf16[6,96,192]{2,1,0:T(8,128)(2,1)S(1)}, bf16[6,96,192]{2,1,0:T(8,128)(2,1)S(1)}, u32[]{:S(2)}, u32[]{:S(2)}) %collective-permute-start.6) | collective-permute-done | bytes 221216 | tf_op jit(solution)/shard_map/ppermute | solution.py:480
  32.8 3.9 %shard_map.138 = bf16[2,48,4,192]{3,2,1,0:T(4,128)(2,1)} custom-call(bf16[6,96,192]{2,1,0:T(8,128)(2,1)S(1)} %get-tuple-element.29.act_own, bf16[6,96,192]{2,1,0:T(8,128)(2,1)S(1)} %collective-permute-done.6.act_other, bf16[4,48,384]{2,1,0:T(8,128)(2,1)S(1)} %get-tuple-element.30.hidden_in, bf16[27,192,384]{2,1,0:T(8,128)(2,1)S(1)} %bitcast.14, ...), custom_call_target="tpu_custom_call" | custom-call | flops 1528823808 | bytes 7962624 | tf_op jit(solution)/shard_map/pallas_call | solution.py:482
  (9 shorter events, 0.0 us)
Async XLA Ops:
  0.7 4.8 %collective-permute-start = (bf16[1,8,1536]{2,1,0:T(8,128)(2,1)S(1)}, bf16[1,8,1536]{2,1,0:T(8,128)(2,1)S(1)}, u32[]{:S(2)}, u32[]{:S(2)}) collective-permute-start(bf16[1,8,1536]{2,1,0:T(8,128)(2,1)S(1)} %pad.4), channel_id=1, source_target_pairs={{0,2},{2,0},{4,6},{6,4},{8,10},{10,8},{12,14},{14,12},{1,3},{3,1},... | collective-permute-start | bytes 73736 | tf_op jit(solution)/shard_map/ppermute | solution.py:358
  4.5 1.2 %collective-permute-start.1 = (f32[8,192]{1,0:T(8,128)S(1)}, f32[8,192]{1,0:T(8,128)S(1)}, u32[]{:S(2)}, u32[]{:S(2)}) collective-permute-start(f32[8,192]{1,0:T(8,128)S(1)} %stack.31.small_own), channel_id=1, source_target_pairs={{0,1},{1,0},{2,3},{3,2},{4,5},{5,4},{6,7},{7,6},{8,9},{9,8},{10,11... | collective-permute-start | bytes 18440 | tf_op jit(solution)/shard_map/ppermute | solution.py:425
  4.6 1.8 %collective-permute-start.2 = (bf16[27,16,192]{2,1,0:T(8,128)(2,1)}, bf16[27,16,192]{2,1,0:T(8,128)(2,1)S(1)}, u32[]{:S(2)}, u32[]{:S(2)}) collective-permute-start(bf16[27,16,192]{2,1,0:T(8,128)(2,1)} %stem_own.1), channel_id=1, source_target_pairs={{0,1},{1,0},{2,3},{3,2},{4,5},{5,4},{6,7},{7,6},{8,9},{9,8},{10,11... | collective-permute-start | bytes 497672 | tf_op jit(solution)/shard_map/ppermute | solution.py:421
  6.4 12.0 %collective-permute-start.5 = (bf16[27,192,384]{2,1,0:T(8,128)(2,1)}, bf16[27,192,384]{2,1,0:T(8,128)(2,1)S(1)}, u32[]{:S(2)}, u32[]{:S(2)}) collective-permute-start(bf16[27,192,384]{2,1,0:T(8,128)(2,1)} %bitcast.13), channel_id=1, source_target_pairs={{0,1},{1,0},{2,3},{3,2},{4,5},{5,4},{6,7},{7,6},{8,9},{9,8},{10,11... | collective-permute-start | bytes 11943944 | tf_op jit(solution)/shard_map/ppermute | solution.py:429
  6.8 4.1 %collective-permute-start.3 = (bf16[2,8,1536]{2,1,0:T(8,128)(2,1)S(1)}, bf16[2,8,1536]{2,1,0:T(8,128)(2,1)S(1)}, u32[]{:S(2)}, u32[]{:S(2)}) collective-permute-start(bf16[2,8,1536]{2,1,0:T(8,128)(2,1)S(1)} %pad_maximum_fusion.1), channel_id=1, source_target_pairs={{0,4},{2,6},{4,0},{6,2},{8,12},{10,14},{12,8},{14,10},{1,5},{3,7},... | collective-permute-start | bytes 147464 | tf_op jit(solution)/shard_map/ppermute | solution.py:358
  8.4 0.9 %copy-start.2 = (bf16[27,16,192]{2,1,0:T(8,128)(2,1)S(1)}, bf16[27,16,192]{2,1,0:T(8,128)(2,1)}, u32[]{:S(2)}) copy-start(bf16[27,16,192]{2,1,0:T(8,128)(2,1)} %stem_own.1) | copy-start | bytes 497668
  9.3 0.7 %copy-start.4 = (s32[8]{0:T(128)S(1)}, s32[8]{0:T(128)}, u32[]{:S(2)}) copy-start(s32[8]{0:T(128)} %counts.1) | copy-start | bytes 100
  10.9 7.5 %collective-permute-start.4 = (bf16[4,8,1536]{2,1,0:T(8,128)(2,1)S(1)}, bf16[4,8,1536]{2,1,0:T(8,128)(2,1)S(1)}, u32[]{:S(2)}, u32[]{:S(2)}) collective-permute-start(bf16[4,8,1536]{2,1,0:T(8,128)(2,1)S(1)} %pad_maximum_fusion), channel_id=1, source_target_pairs={{0,8},{2,10},{4,12},{6,14},{8,0},{10,2},{12,4},{14,6},{1,9},{3,11}... | collective-permute-start | bytes 294920 | tf_op jit(solution)/shard_map/ppermute | solution.py:358
  18.4 14.4 %copy-start = (bf16[27,384,192]{1,2,0:T(8,128)(2,1)S(1)}, bf16[27,384,192]{1,2,0:T(8,128)(2,1)}, u32[]{:S(2)}) copy-start(bf16[27,384,192]{1,2,0:T(8,128)(2,1)} %param.24) | copy-start | bytes 11943940
  18.4 14.4 %copy-start.1 = (bf16[9,384,192]{1,2,0:T(8,128)(2,1)S(1)}, bf16[9,384,192]{1,2,0:T(8,128)(2,1)}, u32[]{:S(2)}) copy-start(bf16[9,384,192]{1,2,0:T(8,128)(2,1)} %param.26) | copy-start | bytes 3981316
  18.4 14.4 %copy-start.3 = (f32[192]{0:T(256)S(1)}, f32[192]{0:T(256)}, u32[]{:S(2)}) copy-start(f32[192]{0:T(256)} %param.27) | copy-start | bytes 2308
  31.1 1.6 %collective-permute-start.6 = (bf16[6,96,192]{2,1,0:T(8,128)(2,1)S(1)}, bf16[6,96,192]{2,1,0:T(8,128)(2,1)S(1)}, u32[]{:S(2)}, u32[]{:S(2)}) collective-permute-start(bf16[6,96,192]{2,1,0:T(8,128)(2,1)S(1)} %get-tuple-element.29.act_own), channel_id=1, source_target_pairs={{0,1},{1,0},{2,3},{3,2},{4,5},{5,4},{6,7},{7,6},{8,9},{9,8},{10,11... | collective-permute-start | bytes 663560 | tf_op jit(solution)/shard_map/ppermute | solution.py:480

commit v4 on v3

--- a/solution.py
+++ b/solution.py
@@ -91,7 +91,11 @@
     held = jnp.full((3 * width, slots), -5, jnp.int32)
     start = jnp.int32(0)
     for owner in range(tile_count):
-        place = (me ^ owner) if power else jnp.int32(owner)
+        place = jnp.int32(owner)
+        if power:
+            bits = tile_count.bit_length() - 1
+            apart = me ^ owner
+            place = sum(((apart >> bit) & 1) << (bits - 1 - bit) for bit in range(bits))
         count = counts[owner]
         held = jnp.where((owner_at == place) & (slot_at < count), start + slot_at, held)
         start = start + count
@@ -421,19 +425,20 @@
     stem_other = lax.ppermute(stem_weight, "chan", swap)
     power = tile_count & (tile_count - 1) == 0 and tile_count >= 4
     if power:
-        owners = exchanged(padded, 1)
+        step = tile_count // 2
+        owners = exchanged(padded, step)
         small_other = lax.ppermute(small, "chan", swap)
         owners, small_other, stem_other, second_far = lax.optimization_barrier(
             (owners, small_other, stem_other, second_weight)
         )
         second_other = lax.ppermute(second_far, "chan", swap)
-        owners = exchanged(owners, 2)
+        step //= 2
+        owners = exchanged(owners, step)
         prepared = prepare(small, small_other, stem_other, power)
         owners, prepared = lax.optimization_barrier((owners, prepared))
-        step = 4
-        while step < tile_count:
+        while step > 1:
+            step //= 2
             owners = exchanged(owners, step)
-            step *= 2
     else:
         small_other = lax.ppermute(small, "chan", swap)
         second_other = lax.ppermute(second_weight, "chan", swap)

time: 36.9 us -> 35.2 us (0.954)
  waiting for transfers between devices: 7.87 us -> 6.17 us
    ppermute x3, waiting for transfers between devices: 5.42 us -> 3.73 us  [exchanged(): moved = lax.ppermute(block, 'tile', [(i, i ^ step) for i in range(count)])]
where the time goes in v4:
time: 35.2 us; the launch traced here: 35 us
  Pallas kernels  17.3 us (49%)
  starting transfers between devices  8.23 us (23%)
  waiting for transfers between devices  6.17 us (18%)
  local copies, waits for them, and re-layouts  3.16 us (9%)
    pallas_call x1, Pallas kernels, on_device(): pl.pallas_call(first_kernel, out_shape=(jax.ShapeDtypeStruct((window, F *...  12.7 us
    ppermute x3, starting transfers between devices, exchanged(): moved = lax.ppermute(block, 'tile', [(i, i ^ step) for i in range(count)])  7.23 us
    pallas_call x1, Pallas kernels, on_device(): pl.pallas_call(functools.partial(second_kernel, tile_count), out_shape=ja...  3.91 us
    ppermute x3, waiting for transfers between devices, exchanged(): moved = lax.ppermute(block, 'tile', [(i, i ^ step) for i in range(count)])  3.73 us
    unnamed x10, local copies, waits for them, and re-layouts  1.61 us
    ppermute x1, waiting for transfers between devices, on_device(): act_other = lax.ppermute(act, 'chan', swap)  1.57 us
    another operation x2, local copies, waits for them, and re-layouts, on_device(): jnp.stack([stem_bias, first_gain, first_shift, second_bias, first_bias, s...  0.8 us
    pad x1, local copies, waits for them, and re-layouts, on_device(): padded = jnp.pad(owner_latent, ((0, 0), (0, PITCH - slot_count), (0, 0)))  0.74 us
  transfers between devices with their start and end apart: 7, of which 6 were waited for; matrix products, arithmetic and copies ran while one was open for 2% of the time, Pallas kernels for 2%

profile of v4, /device:TPU:0, one launch (start us, length us, event | category | flops | bytes accessed | tf_op | source)
XLA Modules:
  0.0 35.0 jit_solution(10725175865320199351)
XLA Ops:
  0.0 0.7 %pad.4 = bf16[1,8,1536]{2,1,0:T(8,128)(2,1)S(1)} pad(bf16[1,5,1536]{2,1,0:T(8,128)(2,1)} %param.14, bf16[]{:T(256)} %constant.1.clone.1), padding=0_0x0_3x0_0 | pad | bytes 39938 | tf_op jit(solution)/shard_map/jit(_pad)/pad | solution.py:394
  0.7 4.1 %collective-permute-start = (bf16[1,8,1536]{2,1,0:T(8,128)(2,1)S(1)}, bf16[1,8,1536]{2,1,0:T(8,128)(2,1)S(1)}, u32[]{:S(2)}, u32[]{:S(2)}) collective-permute-start(bf16[1,8,1536]{2,1,0:T(8,128)(2,1)S(1)} %pad.4), channel_id=1, source_target_pairs={{0,8},{2,10},{4,12},{6,14},{8,0},{10,2},{12,4},{14,6},{1,9},{3,11}... | collective-permute-start | bytes 73736 | tf_op jit(solution)/shard_map/ppermute | solution.py:362
  4.8 0.8 %stack.31.small_own = f32[8,192]{1,0:T(8,128)S(1)} concatenate(f32[1,192]{1,0:T(1,128)} %bitcast.17, f32[1,192]{1,0:T(1,128)} %bitcast.18, f32[1,192]{1,0:T(1,128)} %bitcast.19, f32[1,192]{1,0:T(1,128)} %bitcast.20, f32[1,192]{1,0:T(1,128)} %bitcast.21, f32[1,192]{1,0:T(1,128)} %bitcast.22, f32[1,192]{1,0:T(1,128)} %bitcast.23, f32[1,192]{1,0:T(1,128)S(1)} %stack_broadcast_in_dim.3), dimensions={0} | concatenate | bytes 12288 | tf_op jit(solution)/shard_map/stack | solution.py:395
  5.6 0.1 collective-permute-start.1
  5.7 0.5 %collective-permute-start.2 = (bf16[27,16,192]{2,1,0:T(8,128)(2,1)}, bf16[27,16,192]{2,1,0:T(8,128)(2,1)S(1)}, u32[]{:S(2)}, u32[]{:S(2)}) collective-permute-start(bf16[27,16,192]{2,1,0:T(8,128)(2,1)} %stem_own.1), channel_id=1, source_target_pairs={{0,1},{1,0},{2,3},{3,2},{4,5},{5,4},{6,7},{7,6},{8,9},{9,8},{10,11... | collective-permute-start | bytes 497672 | tf_op jit(solution)/shard_map/ppermute | solution.py:425
  6.2 0.4 %collective-permute-done = bf16[1,8,1536]{2,1,0:T(8,128)(2,1)S(1)} collective-permute-done((bf16[1,8,1536]{2,1,0:T(8,128)(2,1)S(1)}, bf16[1,8,1536]{2,1,0:T(8,128)(2,1)S(1)}, u32[]{:S(2)}, u32[]{:S(2)}) %collective-permute-start) | collective-permute-done | bytes 24608 | tf_op jit(solution)/shard_map/ppermute | solution.py:362
  6.6 0.2 collective-permute-done.1.small_other
  6.8 0.7 %collective-permute-done.2.stem_other = bf16[27,16,192]{2,1,0:T(8,128)(2,1)S(1)} collective-permute-done((bf16[27,16,192]{2,1,0:T(8,128)(2,1)}, bf16[27,16,192]{2,1,0:T(8,128)(2,1)S(1)}, u32[]{:S(2)}, u32[]{:S(2)}) %collective-permute-start.2) | collective-permute-done | bytes 165920 | tf_op jit(solution)/shard_map/ppermute | solution.py:425
  7.5 0.4 %collective-permute-start.5 = (bf16[27,192,384]{2,1,0:T(8,128)(2,1)}, bf16[27,192,384]{2,1,0:T(8,128)(2,1)S(1)}, u32[]{:S(2)}, u32[]{:S(2)}) collective-permute-start(bf16[27,192,384]{2,1,0:T(8,128)(2,1)} %bitcast.13), channel_id=1, source_target_pairs={{0,1},{1,0},{2,3},{3,2},{4,5},{5,4},{6,7},{7,6},{8,9},{9,8},{10,11... | collective-permute-start | bytes 11943944 | tf_op jit(solution)/shard_map/ppermute | solution.py:434
  7.9 1.6 %collective-permute-start.3 = (bf16[2,8,1536]{2,1,0:T(8,128)(2,1)S(1)}, bf16[2,8,1536]{2,1,0:T(8,128)(2,1)S(1)}, u32[]{:S(2)}, u32[]{:S(2)}) collective-permute-start(bf16[2,8,1536]{2,1,0:T(8,128)(2,1)S(1)} %pad_maximum_fusion.1), channel_id=1, source_target_pairs={{0,4},{2,6},{4,0},{6,2},{8,12},{10,14},{12,8},{14,10},{1,5},{3,7},... | collective-permute-start | bytes 147464 | tf_op jit(solution)/shard_map/ppermute | solution.py:362
  9.5 0.9 %copy-done.2 = bf16[27,16,192]{2,1,0:T(8,128)(2,1)S(1)} copy-done((bf16[27,16,192]{2,1,0:T(8,128)(2,1)S(1)}, bf16[27,16,192]{2,1,0:T(8,128)(2,1)}, u32[]{:S(2)}) %copy-start.2) | copy-done | bytes 165912
  10.4 0.7 %copy-done.4 = s32[8]{0:T(128)S(1)} copy-done((s32[8]{0:T(128)S(1)}, s32[8]{0:T(128)}, u32[]{:S(2)}) %copy-start.4) | copy-done | bytes 56
  11.0 0.7 %shard_map.136 = (bf16[48,64]{1,0:T(8,128)(2,1)S(1)}, bf16[3,256,384]{2,1,0:T(8,128)(2,1)S(1)}, f32[8,384]{1,0:T(8,128)S(1)}) custom-call(s32[8]{0:T(128)S(1)} %copy-done.4, bf16[27,16,192]{2,1,0:T(8,128)(2,1)S(1)} %copy-done.2, bf16[27,16,192]{2,1,0:T(8,128)(2,1)S(1)} %collective-permute-done.2.stem_other, f32[8,192]{1,0:T(8,128)S(1)} %stack.31.small_own, ...), custom_call_target="tpu_custom_call" | custom-call | flops 100000000 | bytes 1000000 | tf_op jit(solution)/shard_map/pallas_call | solution.py:412
  11.8 0.2 collective-permute-done.3
  12.0 1.6 %collective-permute-start.4 = (bf16[4,8,1536]{2,1,0:T(8,128)(2,1)S(1)}, bf16[4,8,1536]{2,1,0:T(8,128)(2,1)S(1)}, u32[]{:S(2)}, u32[]{:S(2)}) collective-permute-start(bf16[4,8,1536]{2,1,0:T(8,128)(2,1)S(1)} %pad_maximum_fusion), channel_id=1, source_target_pairs={{0,2},{2,0},{4,6},{6,4},{8,10},{10,8},{12,14},{14,12},{1,3},{3,1},... | collective-permute-start | bytes 294920 | tf_op jit(solution)/shard_map/ppermute | solution.py:362
  13.6 3.1 %collective-permute-done.4 = bf16[4,8,1536]{2,1,0:T(8,128)(2,1)S(1)} collective-permute-done((bf16[4,8,1536]{2,1,0:T(8,128)(2,1)S(1)}, bf16[4,8,1536]{2,1,0:T(8,128)(2,1)S(1)}, u32[]{:S(2)}, u32[]{:S(2)}) %collective-permute-start.4) | collective-permute-done | bytes 98336 | tf_op jit(solution)/shard_map/ppermute | solution.py:362
  16.7 0.0 collective-permute-done.5.unread.weight_other
  16.7 0.0 copy-start
  16.7 0.0 copy-start.1
  16.7 0.0 copy-start.3
  16.7 12.7 %shard_map.137 = (bf16[6,96,192]{2,1,0:T(8,128)(2,1)S(1)}, bf16[4,48,384]{2,1,0:T(8,128)(2,1)S(1)}) custom-call(bf16[64,1536]{1,0:T(8,128)(2,1)S(1)} %maximum_bitcast_fusion.owners, bf16[48,64]{1,0:T(8,128)(2,1)S(1)} %get-tuple-element.25.selection, bf16[3,256,384]{2,1,0:T(8,128)(2,1)S(1)} %get-tuple-element.26.stem_full, ...), custom_call_target="tpu_custom_call" | custom-call | flops 4586471424 | bytes 3981312 | tf_op jit(solution)/shard_map/pallas_call | solution.py:449
  29.4 0.1 collective-permute-start.6
  29.5 1.6 %collective-permute-done.6.act_other = bf16[6,96,192]{2,1,0:T(8,128)(2,1)S(1)} collective-permute-done((bf16[6,96,192]{2,1,0:T(8,128)(2,1)S(1)}, bf16[6,96,192]{2,1,0:T(8,128)(2,1)S(1)}, u32[]{:S(2)}, u32[]{:S(2)}) %collective-permute-start.6) | collective-permute-done | bytes 221216 | tf_op jit(solution)/shard_map/ppermute | solution.py:485
  31.1 3.9 %shard_map.138 = bf16[2,48,4,192]{3,2,1,0:T(4,128)(2,1)} custom-call(bf16[6,96,192]{2,1,0:T(8,128)(2,1)S(1)} %get-tuple-element.29.act_own, bf16[6,96,192]{2,1,0:T(8,128)(2,1)S(1)} %collective-permute-done.6.act_other, bf16[4,48,384]{2,1,0:T(8,128)(2,1)S(1)} %get-tuple-element.30.hidden_in, bf16[27,192,384]{2,1,0:T(8,128)(2,1)S(1)} %bitcast.14, ...), custom_call_target="tpu_custom_call" | custom-call | flops 1528823808 | bytes 7962624 | tf_op jit(solution)/shard_map/pallas_call | solution.py:487
  (9 shorter events, 0.0 us)
Async XLA Ops:
  0.7 5.9 %collective-permute-start = (bf16[1,8,1536]{2,1,0:T(8,128)(2,1)S(1)}, bf16[1,8,1536]{2,1,0:T(8,128)(2,1)S(1)}, u32[]{:S(2)}, u32[]{:S(2)}) collective-permute-start(bf16[1,8,1536]{2,1,0:T(8,128)(2,1)S(1)} %pad.4), channel_id=1, source_target_pairs={{0,8},{2,10},{4,12},{6,14},{8,0},{10,2},{12,4},{14,6},{1,9},{3,11}... | collective-permute-start | bytes 73736 | tf_op jit(solution)/shard_map/ppermute | solution.py:362
  5.6 1.2 %collective-permute-start.1 = (f32[8,192]{1,0:T(8,128)S(1)}, f32[8,192]{1,0:T(8,128)S(1)}, u32[]{:S(2)}, u32[]{:S(2)}) collective-permute-start(f32[8,192]{1,0:T(8,128)S(1)} %stack.31.small_own), channel_id=1, source_target_pairs={{0,1},{1,0},{2,3},{3,2},{4,5},{5,4},{6,7},{7,6},{8,9},{9,8},{10,11... | collective-permute-start | bytes 18440 | tf_op jit(solution)/shard_map/ppermute | solution.py:430
  5.7 1.8 %collective-permute-start.2 = (bf16[27,16,192]{2,1,0:T(8,128)(2,1)}, bf16[27,16,192]{2,1,0:T(8,128)(2,1)S(1)}, u32[]{:S(2)}, u32[]{:S(2)}) collective-permute-start(bf16[27,16,192]{2,1,0:T(8,128)(2,1)} %stem_own.1), channel_id=1, source_target_pairs={{0,1},{1,0},{2,3},{3,2},{4,5},{5,4},{6,7},{7,6},{8,9},{9,8},{10,11... | collective-permute-start | bytes 497672 | tf_op jit(solution)/shard_map/ppermute | solution.py:425
  7.5 9.2 %collective-permute-start.5 = (bf16[27,192,384]{2,1,0:T(8,128)(2,1)}, bf16[27,192,384]{2,1,0:T(8,128)(2,1)S(1)}, u32[]{:S(2)}, u32[]{:S(2)}) collective-permute-start(bf16[27,192,384]{2,1,0:T(8,128)(2,1)} %bitcast.13), channel_id=1, source_target_pairs={{0,1},{1,0},{2,3},{3,2},{4,5},{5,4},{6,7},{7,6},{8,9},{9,8},{10,11... | collective-permute-start | bytes 11943944 | tf_op jit(solution)/shard_map/ppermute | solution.py:434
  7.9 4.1 %collective-permute-start.3 = (bf16[2,8,1536]{2,1,0:T(8,128)(2,1)S(1)}, bf16[2,8,1536]{2,1,0:T(8,128)(2,1)S(1)}, u32[]{:S(2)}, u32[]{:S(2)}) collective-permute-start(bf16[2,8,1536]{2,1,0:T(8,128)(2,1)S(1)} %pad_maximum_fusion.1), channel_id=1, source_target_pairs={{0,4},{2,6},{4,0},{6,2},{8,12},{10,14},{12,8},{14,10},{1,5},{3,7},... | collective-permute-start | bytes 147464 | tf_op jit(solution)/shard_map/ppermute | solution.py:362
  9.5 0.9 %copy-start.2 = (bf16[27,16,192]{2,1,0:T(8,128)(2,1)S(1)}, bf16[27,16,192]{2,1,0:T(8,128)(2,1)}, u32[]{:S(2)}) copy-start(bf16[27,16,192]{2,1,0:T(8,128)(2,1)} %stem_own.1) | copy-start | bytes 497668
  10.4 0.7 %copy-start.4 = (s32[8]{0:T(128)S(1)}, s32[8]{0:T(128)}, u32[]{:S(2)}) copy-start(s32[8]{0:T(128)} %counts.1) | copy-start | bytes 100
  12.0 4.7 %collective-permute-start.4 = (bf16[4,8,1536]{2,1,0:T(8,128)(2,1)S(1)}, bf16[4,8,1536]{2,1,0:T(8,128)(2,1)S(1)}, u32[]{:S(2)}, u32[]{:S(2)}) collective-permute-start(bf16[4,8,1536]{2,1,0:T(8,128)(2,1)S(1)} %pad_maximum_fusion), channel_id=1, source_target_pairs={{0,2},{2,0},{4,6},{6,4},{8,10},{10,8},{12,14},{14,12},{1,3},{3,1},... | collective-permute-start | bytes 294920 | tf_op jit(solution)/shard_map/ppermute | solution.py:362
  16.7 14.4 %copy-start = (bf16[27,384,192]{1,2,0:T(8,128)(2,1)S(1)}, bf16[27,384,192]{1,2,0:T(8,128)(2,1)}, u32[]{:S(2)}) copy-start(bf16[27,384,192]{1,2,0:T(8,128)(2,1)} %param.24) | copy-start | bytes 11943940
  16.7 14.4 %copy-start.1 = (bf16[9,384,192]{1,2,0:T(8,128)(2,1)S(1)}, bf16[9,384,192]{1,2,0:T(8,128)(2,1)}, u32[]{:S(2)}) copy-start(bf16[9,384,192]{1,2,0:T(8,128)(2,1)} %param.26) | copy-start | bytes 3981316
  16.7 14.4 %copy-start.3 = (f32[192]{0:T(256)S(1)}, f32[192]{0:T(256)}, u32[]{:S(2)}) copy-start(f32[192]{0:T(256)} %param.27) | copy-start | bytes 2308
  29.4 1.6 %collective-permute-start.6 = (bf16[6,96,192]{2,1,0:T(8,128)(2,1)S(1)}, bf16[6,96,192]{2,1,0:T(8,128)(2,1)S(1)}, u32[]{:S(2)}, u32[]{:S(2)}) collective-permute-start(bf16[6,96,192]{2,1,0:T(8,128)(2,1)S(1)} %get-tuple-element.29.act_own), channel_id=1, source_target_pairs={{0,1},{1,0},{2,3},{3,2},{4,5},{5,4},{6,7},{7,6},{8,9},{9,8},{10,11... | collective-permute-start | bytes 663560 | tf_op jit(solution)/shard_map/ppermute | solution.py:485

commit v5 on v4

--- a/solution.py
+++ b/solution.py
@@ -12,7 +12,7 @@
 H = 24
 W_DEV = 2
 HALO = 2
-PITCH = 8
+PACKED = 64
 H_PAD = 32
 EPSILON = 1e-06
 
@@ -84,27 +84,37 @@
     zc = stem_own.shape[1]
     leftmost = me * W_DEV - HALO
 
-    slots = PITCH * tile_count
-    lane = lax.broadcasted_iota(jnp.int32, (3 * width, slots), 1)
-    owner_at = lane // PITCH
-    slot_at = lane - owner_at * PITCH
-    held = jnp.full((3 * width, slots), -5, jnp.int32)
+    blocks = selection.shape[0] // (3 * width)
+    packed_rows = tile_count * PACKED
+    lane = lax.broadcasted_iota(jnp.int32, (8, packed_rows), 1)
+    place_at = lane // PACKED
+    row_at = lane - place_at * PACKED
+    slot_at = jnp.floor((row_at.astype(jnp.float32) + 0.5) * (1.0 / blocks)).astype(jnp.int32)
+    held = jnp.full((8, packed_rows), -5, jnp.int32)
     start = jnp.int32(0)
+    bits = tile_count.bit_length() - 1
     for owner in range(tile_count):
         place = jnp.int32(owner)
         if power:
-            bits = tile_count.bit_length() - 1
             apart = me ^ owner
-            place = sum(((apart >> bit) & 1) << (bits - 1 - bit) for bit in range(bits))
+            far = apart >> (bits - 2)
+            place = jnp.where(far == 2, 1 + 2 * core, jnp.where(far == 1, 3 - 2 * core, far))
+            place = jnp.where(far == 3, 2, place)
+            for bit in range(bits - 2):
+                place += ((apart >> bit) & 1) << (bits - 1 - bit)
         count = counts[owner]
-        held = jnp.where((owner_at == place) & (slot_at < count), start + slot_at, held)
+        held = jnp.where((place_at == place) & (slot_at < count), start + slot_at, held)
         start = start + count
-    position = lax.broadcasted_iota(jnp.int32, (3 * width, slots), 0)
+    code = (held * 16 + row_at - slot_at * blocks)[0:1]
+    position = lax.broadcasted_iota(jnp.int32, (3 * width, packed_rows), 0)
     shift = (position >= width).astype(jnp.int32) + (position >= 2 * width).astype(jnp.int32)
     column = position - shift * width + leftmost
     column = jnp.where(column < 0, column + width, column)
     column = jnp.where(column >= width, column - width, column)
-    selection[...] = (held == column + shift - 1).astype(jnp.bfloat16)
+    wanted = (column + shift - 1) * 16
+    for block in range(blocks):
+        rows = slice(block * 3 * width, (block + 1) * 3 * width)
+        selection[rows, :] = (wanted + block == code).astype(jnp.bfloat16)
 
     stem_full[...] = jnp.zeros(stem_full.shape, jnp.bfloat16)
     for tap in range(27):
@@ -124,6 +134,7 @@
     unread,
     act_out,
     hidden_out,
+    packed,
     shifted,
     patches,
     hidden,
@@ -135,22 +146,32 @@
 ):
     fetch = pltpu.make_async_copy(weight_far, weight, arrival)
     fetch.start()
-    tile_count = owners.shape[0] // PITCH
+    tile_count = owners.shape[0]
     width = tile_count * W_DEV
     me = lax.axis_index("tile")
     core = lax.axis_index("chan")
     full, half = vectors.shape[1], small_own.shape[1]
-    frame_lanes = owners.shape[1] // F
+    blocks = selection.shape[0] // (3 * width)
+    frame_blocks = blocks // F
+    frame_lanes = frame_blocks * 128
     zc = frame_lanes // H
     pieces = max(1, width // 16)
     rows = H // pieces
     cells = F * H * width
     leftmost = me * W_DEV - HALO
+    packed[...] = jnp.zeros(packed.shape, jnp.bfloat16)
+    packed[:, 0 : owners.shape[1], :] = owners[...]
+    every = jnp.dot(
+        selection[...],
+        packed[...].reshape(tile_count * PACKED, 128),
+        preferred_element_type=jnp.float32,
+    )
+    blank = jnp.zeros((3 * width, shifted.shape[3] - frame_lanes), jnp.float32)
     for frame in range(F):
-        lanes = slice(frame * frame_lanes, (frame + 1) * frame_lanes)
-        chosen = jnp.dot(selection[...], owners[:, lanes], preferred_element_type=jnp.float32)
-        blank = jnp.zeros((3 * width, shifted.shape[3] - frame_lanes), jnp.float32)
-        chosen = pltpu.roll(jnp.concatenate([chosen, blank], axis=1), zc, axis=1)
+        parts = []
+        for block in range(frame * frame_blocks, (frame + 1) * frame_blocks):
+            parts.append(every[block * 3 * width : (block + 1) * 3 * width])
+        chosen = pltpu.roll(jnp.concatenate(parts + [blank], axis=1), zc, axis=1)
         shifted[:, frame] = chosen.reshape(3, width, shifted.shape[3])
 
     stem_bias = vectors[0:1]
@@ -391,7 +412,8 @@
     swap = [(0, 1), (1, 0)]
     frames = F // 2
 
-    padded = jnp.pad(owner_latent, ((0, 0), (0, PITCH - slot_count), (0, 0)))
+    block_rows = slot_count * row_length // 128
+    latents = owner_latent.reshape(1, block_rows, 128)
     small = jnp.stack(
         [
             stem_bias,
@@ -412,40 +434,48 @@
         return pl.pallas_call(
             functools.partial(prepare_kernel, power),
             out_shape=(
-                jax.ShapeDtypeStruct((3 * width, PITCH * tile_count), jnp.bfloat16),
+                jax.ShapeDtypeStruct((row_length // 128 * 3 * width, PACKED * tile_count), jnp.bfloat16),
                 jax.ShapeDtypeStruct((3, 256, full), jnp.bfloat16),
                 jax.ShapeDtypeStruct((small.shape[0], full), jnp.float32),
             ),
             in_specs=[pl.BlockSpec(memory_space=pltpu.SMEM)] + [vmem] * 4,
             out_specs=(vmem,) * 3,
             cost_estimate=pl.CostEstimate(flops=10**8, bytes_accessed=10**6, transcendentals=0),
-            compiler_params=pltpu.CompilerParams(vmem_limit_bytes=8 * 1024 * 1024),
+            compiler_params=pltpu.CompilerParams(
+                vmem_limit_bytes=(6 + 2 * width // 16) * 1024 * 1024
+            ),
         )(tile_counts, stem_weight, stem_other, small, small_other)
 
     stem_other = lax.ppermute(stem_weight, "chan", swap)
     power = tile_count & (tile_count - 1) == 0 and tile_count >= 4
     if power:
-        step = tile_count // 2
-        owners = exchanged(padded, step)
+        away, near = tile_count // 2, tile_count // 4
+        pairs = [
+            (2 * i + c, 2 * (i ^ (near if c else away)) + c)
+            for i in range(tile_count)
+            for c in range(2)
+        ]
+        one = lax.ppermute(latents, ("tile", "chan"), pairs)
+        both = [(i, i ^ away ^ near) for i in range(tile_count)]
+        two = lax.ppermute(latents, "tile", both)
         small_other = lax.ppermute(small, "chan", swap)
+        three = lax.ppermute(one, "chan", swap)
+        owners = jnp.concatenate([latents, one, two, three], axis=0)
         owners, small_other, stem_other, second_far = lax.optimization_barrier(
             (owners, small_other, stem_other, second_weight)
         )
         second_other = lax.ppermute(second_far, "chan", swap)
-        step //= 2
-        owners = exchanged(owners, step)
-        prepared = prepare(small, small_other, stem_other, power)
-        owners, prepared = lax.optimization_barrier((owners, prepared))
+        step = near
         while step > 1:
             step //= 2
             owners = exchanged(owners, step)
+        prepared = prepare(small, small_other, stem_other, power)
     else:
         small_other = lax.ppermute(small, "chan", swap)
         second_other = lax.ppermute(second_weight, "chan", swap)
-        owners = lax.all_gather(padded, "tile", axis=0, tiled=True)
+        owners = lax.all_gather(latents, "tile", axis=0, tiled=True)
         prepared = prepare(small, small_other, stem_other, power)
     selection, stem_full, vectors = prepared
-    owners = owners.reshape(tile_count * PITCH, F * H * zc)
     act, hidden = pl.pallas_call(
         first_kernel,
         out_shape=(
@@ -455,6 +485,7 @@
         in_specs=[vmem] * 5 + [far, pl.BlockSpec(memory_space=pl.ANY)],
         out_specs=(vmem, vmem),
         scratch_shapes=[
+            pltpu.VMEM((tile_count, PACKED, 128), jnp.bfloat16),
             pltpu.VMEM((3, F, width, H_PAD * zc), jnp.float32),
             pltpu.VMEM((F, H, width, 256), jnp.bfloat16),
             pltpu.VMEM((full // 128, F * H * width, 128), jnp.float32),

time: 35.2 us -> 36.2 us (1.028)
  waiting for transfers between devices: 6.17 us -> 7.29 us
    ppermute x3 -> x1, starting transfers between devices: 7.23 us -> 1.58 us  [exchanged(): moved = lax.ppermute(block, 'tile', [(i, i ^ step) for i in range(count)])]
    ppermute x0 -> x3, starting transfers between devices: none -> 4.99 us  [the longest x1 3.64 us: on_device(): one = lax.ppermute(latents, ('tile', 'chan'), pairs)]
    ppermute x3 -> x1, waiting for transfers between devices: 3.73 us -> 0.49 us  [exchanged(): moved = lax.ppermute(block, 'tile', [(i, i ^ step) for i in range(count)])]
    ppermute x0 -> x3, waiting for transfers between devices: none -> 2.81 us  [the longest x1 2.44 us: on_device(): two = lax.ppermute(latents, 'tile', both)]
    ppermute x1, waiting for transfers between devices: 0.01 us -> 2.54 us  [on_device(): second_other = lax.ppermute(second_far, 'chan', swap)]
    reshape x0 -> x1, local copies, waits for them, and re-layouts: none -> 0.77 us  [on_device(): latents = owner_latent.reshape(1, block_rows, 128)]
    pad x1 -> x0, local copies, waits for them, and re-layouts: 0.74 us -> none  [on_device(): padded = jnp.pad(owner_latent, ((0, 0), (0, PITCH - slot_count), (0, 0)))]
    ppermute x1, waiting for transfers between devices: 0.65 us -> 0.01 us  [on_device(): stem_other = lax.ppermute(stem_weight, 'chan', swap)]
  transfers between devices with their start and end apart: 7 -> 8, of which waited for: 6 -> 5; matrix products, arithmetic and copies ran while one was open for 2% -> 4% of each run, Pallas kernels for 2% -> 2%
where the time goes in v5:
time: 36.2 us; the launch traced here: 36 us
  Pallas kernels  17.5 us (48%)
  starting transfers between devices  7.91 us (22%)
  waiting for transfers between devices  7.29 us (20%)
  local copies, waits for them, and re-layouts  3.18 us (9%)
    pallas_call x1, Pallas kernels, on_device(): pl.pallas_call(first_kernel, out_shape=(jax.ShapeDtypeStruct((window, F *...  12.8 us
    pallas_call x1, Pallas kernels, on_device(): pl.pallas_call(functools.partial(second_kernel, tile_count), out_shape=ja...  3.92 us
    ppermute x1, starting transfers between devices, on_device(): one = lax.ppermute(latents, ('tile', 'chan'), pairs)  3.64 us
    ppermute x1, waiting for transfers between devices, on_device(): second_other = lax.ppermute(second_far, 'chan', swap)  2.54 us
    ppermute x1, waiting for transfers between devices, on_device(): two = lax.ppermute(latents, 'tile', both)  2.44 us
    unnamed x10, local copies, waits for them, and re-layouts  1.6 us
    ppermute x1, starting transfers between devices, exchanged(): moved = lax.ppermute(block, 'tile', [(i, i ^ step) for i in range(count)])  1.58 us
    ppermute x1, waiting for transfers between devices, on_device(): act_other = lax.ppermute(act, 'chan', swap)  1.44 us
  transfers between devices with their start and end apart: 8, of which 5 were waited for; matrix products, arithmetic and copies ran while one was open for 4% of the time, Pallas kernels for 2%

profile of v5, /device:TPU:0, one launch (start us, length us, event | category | flops | bytes accessed | tf_op | source)
XLA Modules:
  0.0 36.0 jit_solution(1683589746530404542)
XLA Ops:
  0.0 0.5 %collective-permute-start.4 = (bf16[27,16,192]{2,1,0:T(8,128)(2,1)}, bf16[27,16,192]{2,1,0:T(8,128)(2,1)S(1)}, u32[]{:S(2)}, u32[]{:S(2)}) collective-permute-start(bf16[27,16,192]{2,1,0:T(8,128)(2,1)} %stem_own.1), channel_id=1, source_target_pairs={{0,1},{1,0},{2,3},{3,2},{4,5},{5,4},{6,7},{7,6},{8,9},{9,8},{10,11... | collective-permute-start | bytes 497672 | tf_op jit(solution)/shard_map/ppermute | solution.py:449
  0.5 0.8 %reshape.6 = bf16[1,60,128]{2,1,0:T(8,128)(2,1)S(1)} reshape(bf16[1,5,1536]{2,1,0:T(8,128)(2,1)} %param.14) | data formatting | bytes 30720 | tf_op jit(solution)/shard_map/reshape | solution.py:416
  1.3 3.6 %collective-permute-start = (bf16[1,60,128]{2,1,0:T(8,128)(2,1)S(1)}, bf16[1,60,128]{2,1,0:T(8,128)(2,1)S(1)}, u32[]{:S(2)}, u32[]{:S(2)}) collective-permute-start(bf16[1,60,128]{2,1,0:T(8,128)(2,1)S(1)} %reshape.6), channel_id=1, source_target_pairs={{0,8},{1,5},{2,10},{3,7},{4,12},{5,1},{6,14},{7,3},{8,0},{9,13},{1... | collective-permute-start | bytes 46088 | tf_op jit(solution)/shard_map/ppermute | solution.py:458
  4.9 1.3 %collective-permute-start.1 = (bf16[1,60,128]{2,1,0:T(8,128)(2,1)S(1)}, bf16[1,60,128]{2,1,0:T(8,128)(2,1)S(1)}, u32[]{:S(2)}, u32[]{:S(2)}) collective-permute-start(bf16[1,60,128]{2,1,0:T(8,128)(2,1)S(1)} %reshape.6), channel_id=1, source_target_pairs={{0,12},{2,14},{4,8},{6,10},{8,4},{10,6},{12,0},{14,2},{1,13},{3,15... | collective-permute-start | bytes 46088 | tf_op jit(solution)/shard_map/ppermute | solution.py:460
  6.3 0.4 %collective-permute-done = bf16[1,60,128]{2,1,0:T(8,128)(2,1)S(1)} collective-permute-done((bf16[1,60,128]{2,1,0:T(8,128)(2,1)S(1)}, bf16[1,60,128]{2,1,0:T(8,128)(2,1)S(1)}, u32[]{:S(2)}, u32[]{:S(2)}) %collective-permute-start) | collective-permute-done | bytes 15392 | tf_op jit(solution)/shard_map/ppermute | solution.py:458
  6.6 0.0 collective-permute-start.2
  6.6 0.8 %stack.31.small_own = f32[8,192]{1,0:T(8,128)S(1)} concatenate(f32[1,192]{1,0:T(1,128)} %bitcast.15, f32[1,192]{1,0:T(1,128)} %bitcast.16, f32[1,192]{1,0:T(1,128)} %bitcast.17, f32[1,192]{1,0:T(1,128)} %bitcast.18, f32[1,192]{1,0:T(1,128)} %bitcast.19, f32[1,192]{1,0:T(1,128)} %bitcast.20, f32[1,192]{1,0:T(1,128)} %bitcast.21, f32[1,192]{1,0:T(1,128)S(1)} %stack_broadcast_in_dim.3), dimensions={0} | concatenate | bytes 12288 | tf_op jit(solution)/shard_map/stack | solution.py:417
  7.4 0.6 %collective-permute-start.3 = (f32[8,192]{1,0:T(8,128)S(1)}, f32[8,192]{1,0:T(8,128)S(1)}, u32[]{:S(2)}, u32[]{:S(2)}) collective-permute-start(f32[8,192]{1,0:T(8,128)S(1)} %stack.31.small_own), channel_id=1, source_target_pairs={{0,1},{1,0},{2,3},{3,2},{4,5},{5,4},{6,7},{7,6},{8,9},{9,8},{10,11... | collective-permute-start | bytes 18440 | tf_op jit(solution)/shard_map/ppermute | solution.py:461
  8.0 2.4 %collective-permute-done.1 = bf16[1,60,128]{2,1,0:T(8,128)(2,1)S(1)} collective-permute-done((bf16[1,60,128]{2,1,0:T(8,128)(2,1)S(1)}, bf16[1,60,128]{2,1,0:T(8,128)(2,1)S(1)}, u32[]{:S(2)}, u32[]{:S(2)}) %collective-permute-start.1) | collective-permute-done | bytes 15392 | tf_op jit(solution)/shard_map/ppermute | solution.py:460
  10.4 0.0 collective-permute-done.2
  10.5 0.0 collective-permute-done.3.small_other
  10.5 0.0 collective-permute-done.4.stem_other
  10.5 0.1 collective-permute-start.6
  10.6 1.6 %collective-permute-start.5 = (bf16[4,60,128]{2,1,0:T(8,128)(2,1)S(1)}, bf16[4,60,128]{2,1,0:T(8,128)(2,1)S(1)}, u32[]{:S(2)}, u32[]{:S(2)}) collective-permute-start(bf16[4,60,128]{2,1,0:T(8,128)(2,1)S(1)} %pad_maximum_fusion.1), channel_id=1, source_target_pairs={{0,2},{2,0},{4,6},{6,4},{8,10},{10,8},{12,14},{14,12},{1,3},{3,1},... | collective-permute-start | bytes 184328 | tf_op jit(solution)/shard_map/ppermute | solution.py:383
  12.2 0.9 %copy-done.2 = bf16[27,16,192]{2,1,0:T(8,128)(2,1)S(1)} copy-done((bf16[27,16,192]{2,1,0:T(8,128)(2,1)S(1)}, bf16[27,16,192]{2,1,0:T(8,128)(2,1)}, u32[]{:S(2)}) %copy-start.2) | copy-done | bytes 165912
  13.1 0.7 %copy-done.4 = s32[8]{0:T(128)S(1)} copy-done((s32[8]{0:T(128)S(1)}, s32[8]{0:T(128)}, u32[]{:S(2)}) %copy-start.4) | copy-done | bytes 56
  13.7 0.8 %shard_map.136 = (bf16[576,512]{1,0:T(8,128)(2,1)S(1)}, bf16[3,256,384]{2,1,0:T(8,128)(2,1)S(1)}, f32[8,384]{1,0:T(8,128)S(1)}) custom-call(s32[8]{0:T(128)S(1)} %copy-done.4, bf16[27,16,192]{2,1,0:T(8,128)(2,1)S(1)} %copy-done.2, bf16[27,16,192]{2,1,0:T(8,128)(2,1)S(1)} %collective-permute-done.4.stem_other, f32[8,192]{1,0:T(8,128)S(1)} %stack.31.small_own, ...), custom_call_target="tpu_custom_call" | custom-call | flops 100000000 | bytes 1000000 | tf_op jit(solution)/shard_map/pallas_call | solution.py:434
  14.6 0.5 %collective-permute-done.5 = bf16[4,60,128]{2,1,0:T(8,128)(2,1)S(1)} collective-permute-done((bf16[4,60,128]{2,1,0:T(8,128)(2,1)S(1)}, bf16[4,60,128]{2,1,0:T(8,128)(2,1)S(1)}, u32[]{:S(2)}, u32[]{:S(2)}) %collective-permute-start.5) | collective-permute-done | bytes 61472 | tf_op jit(solution)/shard_map/ppermute | solution.py:383
  15.1 2.5 %collective-permute-done.6.unread.weight_other = bf16[27,192,384]{2,1,0:T(8,128)(2,1)S(1)} collective-permute-done((bf16[27,192,384]{2,1,0:T(8,128)(2,1)}, bf16[27,192,384]{2,1,0:T(8,128)(2,1)S(1)}, u32[]{:S(2)}, u32[]{:S(2)}) %collective-permute-start.6) | collective-permute-done | bytes 3981344 | tf_op jit(solution)/shard_map/ppermute | solution.py:467
  17.6 12.8 %shard_map.137 = (bf16[6,96,192]{2,1,0:T(8,128)(2,1)S(1)}, bf16[4,48,384]{2,1,0:T(8,128)(2,1)S(1)}) custom-call(bf16[8,60,128]{2,1,0:T(8,128)(2,1)S(1)} %pad_maximum_fusion.owners, bf16[576,512]{1,0:T(8,128)(2,1)S(1)} %get-tuple-element.17.selection, bf16[3,256,384]{2,1,0:T(8,128)(2,1)S(1)} %get-tuple-element.18.stem_full, ...), custom_call_target="tpu_custom_call" | custom-call | flops 4586471424 | bytes 3981312 | tf_op jit(solution)/shard_map/pallas_call | solution.py:479
  30.4 0.2 collective-permute-start.7
  30.6 1.4 %collective-permute-done.7.act_other = bf16[6,96,192]{2,1,0:T(8,128)(2,1)S(1)} collective-permute-done((bf16[6,96,192]{2,1,0:T(8,128)(2,1)S(1)}, bf16[6,96,192]{2,1,0:T(8,128)(2,1)S(1)}, u32[]{:S(2)}, u32[]{:S(2)}) %collective-permute-start.7) | collective-permute-done | bytes 221216 | tf_op jit(solution)/shard_map/ppermute | solution.py:516
  32.1 0.0 copy-done
  32.1 3.9 %shard_map.138 = bf16[2,48,4,192]{3,2,1,0:T(4,128)(2,1)} custom-call(bf16[6,96,192]{2,1,0:T(8,128)(2,1)S(1)} %get-tuple-element.21.act_own, bf16[6,96,192]{2,1,0:T(8,128)(2,1)S(1)} %collective-permute-done.7.act_other, bf16[4,48,384]{2,1,0:T(8,128)(2,1)S(1)} %get-tuple-element.22.hidden_in, bf16[27,192,384]{2,1,0:T(8,128)(2,1)S(1)} %bitcast.12, ...), custom_call_target="tpu_custom_call" | custom-call | flops 1528823808 | bytes 7962624 | tf_op jit(solution)/shard_map/pallas_call | solution.py:518
  (10 shorter events, 0.0 us)
Async XLA Ops:
  0.0 10.5 %collective-permute-start.4 = (bf16[27,16,192]{2,1,0:T(8,128)(2,1)}, bf16[27,16,192]{2,1,0:T(8,128)(2,1)S(1)}, u32[]{:S(2)}, u32[]{:S(2)}) collective-permute-start(bf16[27,16,192]{2,1,0:T(8,128)(2,1)} %stem_own.1), channel_id=1, source_target_pairs={{0,1},{1,0},{2,3},{3,2},{4,5},{5,4},{6,7},{7,6},{8,9},{9,8},{10,11... | collective-permute-start | bytes 497672 | tf_op jit(solution)/shard_map/ppermute | solution.py:449
  1.3 5.4 %collective-permute-start = (bf16[1,60,128]{2,1,0:T(8,128)(2,1)S(1)}, bf16[1,60,128]{2,1,0:T(8,128)(2,1)S(1)}, u32[]{:S(2)}, u32[]{:S(2)}) collective-permute-start(bf16[1,60,128]{2,1,0:T(8,128)(2,1)S(1)} %reshape.6), channel_id=1, source_target_pairs={{0,8},{1,5},{2,10},{3,7},{4,12},{5,1},{6,14},{7,3},{8,0},{9,13},{1... | collective-permute-start | bytes 46088 | tf_op jit(solution)/shard_map/ppermute | solution.py:458
  4.9 5.5 %collective-permute-start.1 = (bf16[1,60,128]{2,1,0:T(8,128)(2,1)S(1)}, bf16[1,60,128]{2,1,0:T(8,128)(2,1)S(1)}, u32[]{:S(2)}, u32[]{:S(2)}) collective-permute-start(bf16[1,60,128]{2,1,0:T(8,128)(2,1)S(1)} %reshape.6), channel_id=1, source_target_pairs={{0,12},{2,14},{4,8},{6,10},{8,4},{10,6},{12,0},{14,2},{1,13},{3,15... | collective-permute-start | bytes 46088 | tf_op jit(solution)/shard_map/ppermute | solution.py:460
  6.6 3.8 %collective-permute-start.2 = (bf16[1,60,128]{2,1,0:T(8,128)(2,1)S(1)}, bf16[1,60,128]{2,1,0:T(8,128)(2,1)S(1)}, u32[]{:S(2)}, u32[]{:S(2)}) collective-permute-start(bf16[1,60,128]{2,1,0:T(8,128)(2,1)S(1)} %collective-permute-done), channel_id=1, source_target_pairs={{0,1},{1,0},{2,3},{3,2},{4,5},{5,4},{6,7},{7,6},{8,9},{9,8},{10,11... | collective-permute-start | bytes 46088 | tf_op jit(solution)/shard_map/ppermute | solution.py:462
  7.4 3.0 %collective-permute-start.3 = (f32[8,192]{1,0:T(8,128)S(1)}, f32[8,192]{1,0:T(8,128)S(1)}, u32[]{:S(2)}, u32[]{:S(2)}) collective-permute-start(f32[8,192]{1,0:T(8,128)S(1)} %stack.31.small_own), channel_id=1, source_target_pairs={{0,1},{1,0},{2,3},{3,2},{4,5},{5,4},{6,7},{7,6},{8,9},{9,8},{10,11... | collective-permute-start | bytes 18440 | tf_op jit(solution)/shard_map/ppermute | solution.py:461
  10.5 7.1 %collective-permute-start.6 = (bf16[27,192,384]{2,1,0:T(8,128)(2,1)}, bf16[27,192,384]{2,1,0:T(8,128)(2,1)S(1)}, u32[]{:S(2)}, u32[]{:S(2)}) collective-permute-start(bf16[27,192,384]{2,1,0:T(8,128)(2,1)} %bitcast.11), channel_id=1, source_target_pairs={{0,1},{1,0},{2,3},{3,2},{4,5},{5,4},{6,7},{7,6},{8,9},{9,8},{10,11... | collective-permute-start | bytes 11943944 | tf_op jit(solution)/shard_map/ppermute | solution.py:467
  10.6 4.5 %collective-permute-start.5 = (bf16[4,60,128]{2,1,0:T(8,128)(2,1)S(1)}, bf16[4,60,128]{2,1,0:T(8,128)(2,1)S(1)}, u32[]{:S(2)}, u32[]{:S(2)}) collective-permute-start(bf16[4,60,128]{2,1,0:T(8,128)(2,1)S(1)} %pad_maximum_fusion.1), channel_id=1, source_target_pairs={{0,2},{2,0},{4,6},{6,4},{8,10},{10,8},{12,14},{14,12},{1,3},{3,1},... | collective-permute-start | bytes 184328 | tf_op jit(solution)/shard_map/ppermute | solution.py:383
  12.2 0.9 %copy-start.2 = (bf16[27,16,192]{2,1,0:T(8,128)(2,1)S(1)}, bf16[27,16,192]{2,1,0:T(8,128)(2,1)}, u32[]{:S(2)}) copy-start(bf16[27,16,192]{2,1,0:T(8,128)(2,1)} %stem_own.1) | copy-start | bytes 497668
  13.1 0.7 %copy-start.4 = (s32[8]{0:T(128)S(1)}, s32[8]{0:T(128)}, u32[]{:S(2)}) copy-start(s32[8]{0:T(128)} %counts.1) | copy-start | bytes 100
  17.6 14.5 %copy-start = (bf16[27,384,192]{1,2,0:T(8,128)(2,1)S(1)}, bf16[27,384,192]{1,2,0:T(8,128)(2,1)}, u32[]{:S(2)}) copy-start(bf16[27,384,192]{1,2,0:T(8,128)(2,1)} %param.24) | copy-start | bytes 11943940
  17.6 14.5 %copy-start.1 = (bf16[9,384,192]{1,2,0:T(8,128)(2,1)S(1)}, bf16[9,384,192]{1,2,0:T(8,128)(2,1)}, u32[]{:S(2)}) copy-start(bf16[9,384,192]{1,2,0:T(8,128)(2,1)} %param.26) | copy-start | bytes 3981316
  17.6 14.5 %copy-start.3 = (f32[192]{0:T(256)S(1)}, f32[192]{0:T(256)}, u32[]{:S(2)}) copy-start(f32[192]{0:T(256)} %param.27) | copy-start | bytes 2308
  30.4 1.6 %collective-permute-start.7 = (bf16[6,96,192]{2,1,0:T(8,128)(2,1)S(1)}, bf16[6,96,192]{2,1,0:T(8,128)(2,1)S(1)}, u32[]{:S(2)}, u32[]{:S(2)}) collective-permute-start(bf16[6,96,192]{2,1,0:T(8,128)(2,1)S(1)} %get-tuple-element.21.act_own), channel_id=1, source_target_pairs={{0,1},{1,0},{2,3},{3,2},{4,5},{5,4},{6,7},{7,6},{8,9},{9,8},{10,11... | collective-permute-start | bytes 663560 | tf_op jit(solution)/shard_map/ppermute | solution.py:516

commit v6 on v5

--- a/solution.py
+++ b/solution.py
@@ -6,6 +6,7 @@
 from jax.experimental import pallas as pl
 from jax.experimental.pallas import tpu as pltpu
 from jax.sharding import PartitionSpec as P
+
 
 GROUPS = 32
 F = 4
@@ -447,6 +448,7 @@
         )(tile_counts, stem_weight, stem_other, small, small_other)
 
     stem_other = lax.ppermute(stem_weight, "chan", swap)
+    second_other = lax.ppermute(second_weight, "chan", swap)
     power = tile_count & (tile_count - 1) == 0 and tile_count >= 4
     if power:
         away, near = tile_count // 2, tile_count // 4
@@ -461,10 +463,9 @@
         small_other = lax.ppermute(small, "chan", swap)
         three = lax.ppermute(one, "chan", swap)
         owners = jnp.concatenate([latents, one, two, three], axis=0)
-        owners, small_other, stem_other, second_far = lax.optimization_barrier(
-            (owners, small_other, stem_other, second_weight)
+        owners, small_other, stem_other = lax.optimization_barrier(
+            (owners, small_other, stem_other)
         )
-        second_other = lax.ppermute(second_far, "chan", swap)
         step = near
         while step > 1:
             step //= 2
@@ -472,7 +473,6 @@
         prepared = prepare(small, small_other, stem_other, power)
     else:
         small_other = lax.ppermute(small, "chan", swap)
-        second_other = lax.ppermute(second_weight, "chan", swap)
         owners = lax.all_gather(latents, "tile", axis=0, tiled=True)
         prepared = prepare(small, small_other, stem_other, power)
     selection, stem_full, vectors = prepared
@@ -561,6 +561,7 @@
         P(),
         P(),
     )
+
     return jax.shard_map(
         on_device,
         mesh=mesh,

time: 36.2 us -> 36.2 us (level)
  waiting for transfers between devices: 7.29 us -> 4.72 us
  Pallas kernels: 17.5 us -> 19.7 us
    ppermute x1, waiting for transfers between devices: 2.54 us -> 0.01 us  [on_device(): second_other = lax.ppermute(second_weight, 'chan', swap)]
    pallas_call x1, Pallas kernels: 3.92 us -> 6.05 us  [on_device(): pl.pallas_call(functools.partial(second_kernel, tile_count), out_shape=ja...]
    ppermute x1, starting transfers between devices: 3.64 us -> 4.13 us  [on_device(): one = lax.ppermute(latents, ('tile', 'chan'), pairs)]
    ppermute x1, starting transfers between devices: 0.49 us -> 0.02 us  [on_device(): stem_other = lax.ppermute(stem_weight, 'chan', swap)]
    ppermute x1, starting transfers between devices: 0.07 us -> 0.49 us  [on_device(): second_other = lax.ppermute(second_weight, 'chan', swap)]
  transfers between devices with their start and end apart: 8 -> 8, of which waited for: 5 -> 4; matrix products, arithmetic and copies ran while one was open for 4% -> 4% of each run, Pallas kernels for 2% -> 2%
where the time goes in v6:
time: 36.2 us; the launch traced here: 35.9 us
  Pallas kernels  19.7 us (54%)
  starting transfers between devices  8.21 us (23%)
  waiting for transfers between devices  4.72 us (13%)
  local copies, waits for them, and re-layouts  3.19 us (9%)
    pallas_call x1, Pallas kernels, on_device(): pl.pallas_call(first_kernel, out_shape=(jax.ShapeDtypeStruct((window, F *...  12.8 us
    pallas_call x1, Pallas kernels, on_device(): pl.pallas_call(functools.partial(second_kernel, tile_count), out_shape=ja...  6.05 us
    ppermute x1, starting transfers between devices, on_device(): one = lax.ppermute(latents, ('tile', 'chan'), pairs)  4.13 us
    ppermute x1, waiting for transfers between devices, on_device(): two = lax.ppermute(latents, 'tile', both)  2.44 us
    unnamed x10, local copies, waits for them, and re-layouts  1.61 us
    ppermute x1, starting transfers between devices, exchanged(): moved = lax.ppermute(block, 'tile', [(i, i ^ step) for i in range(count)])  1.58 us
    ppermute x1, waiting for transfers between devices, on_device(): act_other = lax.ppermute(act, 'chan', swap)  1.57 us
    ppermute x1, starting transfers between devices, on_device(): two = lax.ppermute(latents, 'tile', both)  1.35 us
  transfers between devices with their start and end apart: 8, of which 4 were waited for; matrix products, arithmetic and copies ran while one was open for 4% of the time, Pallas kernels for 2%

profile of v6, /device:TPU:0, one launch (start us, length us, event | category | flops | bytes accessed | tf_op | source)
XLA Modules:
  0.0 35.9 jit_solution(6594450531081840272)
XLA Ops:
  0.0 0.5 %collective-permute-start.6 = (bf16[27,192,384]{2,1,0:T(8,128)(2,1)}, bf16[27,192,384]{2,1,0:T(8,128)(2,1)}, u32[]{:S(2)}, u32[]{:S(2)}) collective-permute-start(bf16[27,192,384]{2,1,0:T(8,128)(2,1)} %bitcast.11), channel_id=1, source_target_pairs={{0,1},{1,0},{2,3},{3,2},{4,5},{5,4},{6,7},{7,6},{8,9},{9,8},{10,11... | collective-permute-start | bytes 11943944 | tf_op jit(solution)/shard_map/ppermute | solution.py:451
  0.5 0.0 collective-permute-start.4
  0.5 0.8 %reshape.6 = bf16[1,60,128]{2,1,0:T(8,128)(2,1)S(1)} reshape(bf16[1,5,1536]{2,1,0:T(8,128)(2,1)} %param.14) | data formatting | bytes 30720 | tf_op jit(solution)/shard_map/reshape | solution.py:417
  1.3 4.1 %collective-permute-start = (bf16[1,60,128]{2,1,0:T(8,128)(2,1)S(1)}, bf16[1,60,128]{2,1,0:T(8,128)(2,1)S(1)}, u32[]{:S(2)}, u32[]{:S(2)}) collective-permute-start(bf16[1,60,128]{2,1,0:T(8,128)(2,1)S(1)} %reshape.6), channel_id=1, source_target_pairs={{0,8},{1,5},{2,10},{3,7},{4,12},{5,1},{6,14},{7,3},{8,0},{9,13},{1... | collective-permute-start | bytes 46088 | tf_op jit(solution)/shard_map/ppermute | solution.py:460
  5.4 1.3 %collective-permute-start.1 = (bf16[1,60,128]{2,1,0:T(8,128)(2,1)S(1)}, bf16[1,60,128]{2,1,0:T(8,128)(2,1)S(1)}, u32[]{:S(2)}, u32[]{:S(2)}) collective-permute-start(bf16[1,60,128]{2,1,0:T(8,128)(2,1)S(1)} %reshape.6), channel_id=1, source_target_pairs={{0,12},{2,14},{4,8},{6,10},{8,4},{10,6},{12,0},{14,2},{1,13},{3,15... | collective-permute-start | bytes 46088 | tf_op jit(solution)/shard_map/ppermute | solution.py:462
  6.8 0.4 %collective-permute-done = bf16[1,60,128]{2,1,0:T(8,128)(2,1)S(1)} collective-permute-done((bf16[1,60,128]{2,1,0:T(8,128)(2,1)S(1)}, bf16[1,60,128]{2,1,0:T(8,128)(2,1)S(1)}, u32[]{:S(2)}, u32[]{:S(2)}) %collective-permute-start) | collective-permute-done | bytes 15392 | tf_op jit(solution)/shard_map/ppermute | solution.py:460
  7.1 0.0 collective-permute-start.2
  7.1 0.8 %stack.31.small_own = f32[8,192]{1,0:T(8,128)S(1)} concatenate(f32[1,192]{1,0:T(1,128)} %bitcast.15, f32[1,192]{1,0:T(1,128)} %bitcast.16, f32[1,192]{1,0:T(1,128)} %bitcast.17, f32[1,192]{1,0:T(1,128)} %bitcast.18, f32[1,192]{1,0:T(1,128)} %bitcast.19, f32[1,192]{1,0:T(1,128)} %bitcast.20, f32[1,192]{1,0:T(1,128)} %bitcast.21, f32[1,192]{1,0:T(1,128)S(1)} %stack_broadcast_in_dim.3), dimensions={0} | concatenate | bytes 12288 | tf_op jit(solution)/shard_map/stack | solution.py:418
  7.9 0.6 %collective-permute-start.3 = (f32[8,192]{1,0:T(8,128)S(1)}, f32[8,192]{1,0:T(8,128)S(1)}, u32[]{:S(2)}, u32[]{:S(2)}) collective-permute-start(f32[8,192]{1,0:T(8,128)S(1)} %stack.31.small_own), channel_id=1, source_target_pairs={{0,1},{1,0},{2,3},{3,2},{4,5},{5,4},{6,7},{7,6},{8,9},{9,8},{10,11... | collective-permute-start | bytes 18440 | tf_op jit(solution)/shard_map/ppermute | solution.py:463
  8.5 2.4 %collective-permute-done.1 = bf16[1,60,128]{2,1,0:T(8,128)(2,1)S(1)} collective-permute-done((bf16[1,60,128]{2,1,0:T(8,128)(2,1)S(1)}, bf16[1,60,128]{2,1,0:T(8,128)(2,1)S(1)}, u32[]{:S(2)}, u32[]{:S(2)}) %collective-permute-start.1) | collective-permute-done | bytes 15392 | tf_op jit(solution)/shard_map/ppermute | solution.py:462
  11.0 0.0 collective-permute-done.2
  11.0 0.0 collective-permute-done.3.small_other
  11.0 1.6 %collective-permute-start.5 = (bf16[4,60,128]{2,1,0:T(8,128)(2,1)S(1)}, bf16[4,60,128]{2,1,0:T(8,128)(2,1)S(1)}, u32[]{:S(2)}, u32[]{:S(2)}) collective-permute-start(bf16[4,60,128]{2,1,0:T(8,128)(2,1)S(1)} %pad_maximum_fusion.1), channel_id=1, source_target_pairs={{0,2},{2,0},{4,6},{6,4},{8,10},{10,8},{12,14},{14,12},{1,3},{3,1},... | collective-permute-start | bytes 184328 | tf_op jit(solution)/shard_map/ppermute | solution.py:384
  12.6 0.9 %copy-done.2 = bf16[27,16,192]{2,1,0:T(8,128)(2,1)S(1)} copy-done((bf16[27,16,192]{2,1,0:T(8,128)(2,1)S(1)}, bf16[27,16,192]{2,1,0:T(8,128)(2,1)}, u32[]{:S(2)}) %copy-start.2) | copy-done | bytes 165912
  13.5 0.7 %copy-done.4 = s32[8]{0:T(128)S(1)} copy-done((s32[8]{0:T(128)S(1)}, s32[8]{0:T(128)}, u32[]{:S(2)}) %copy-start.4) | copy-done | bytes 56
  14.2 0.8 %shard_map.136 = (bf16[576,512]{1,0:T(8,128)(2,1)S(1)}, bf16[3,256,384]{2,1,0:T(8,128)(2,1)S(1)}, f32[8,384]{1,0:T(8,128)S(1)}) custom-call(s32[8]{0:T(128)S(1)} %copy-done.4, bf16[27,16,192]{2,1,0:T(8,128)(2,1)S(1)} %copy-done.2, bf16[27,16,192]{2,1,0:T(8,128)(2,1)S(1)} %collective-permute-done.4.stem_other, f32[8,192]{1,0:T(8,128)S(1)} %stack.31.small_own, ...), custom_call_target="tpu_custom_call" | custom-call | flops 100000000 | bytes 1000000 | tf_op jit(solution)/shard_map/pallas_call | solution.py:435
  15.0 0.3 collective-permute-done.5
  15.4 0.0 copy-start
  15.4 0.0 copy-start.1
  15.4 0.0 copy-start.3
  15.4 12.8 %shard_map.137 = (bf16[6,96,192]{2,1,0:T(8,128)(2,1)S(1)}, bf16[4,48,384]{2,1,0:T(8,128)(2,1)S(1)}) custom-call(bf16[8,60,128]{2,1,0:T(8,128)(2,1)S(1)} %pad_maximum_fusion.owners, bf16[576,512]{1,0:T(8,128)(2,1)S(1)} %get-tuple-element.16.selection, bf16[3,256,384]{2,1,0:T(8,128)(2,1)S(1)} %get-tuple-element.17.stem_full, ...), custom_call_target="tpu_custom_call" | custom-call | flops 4586471424 | bytes 3981312 | tf_op jit(solution)/shard_map/pallas_call | solution.py:479
  28.2 0.1 collective-permute-start.7
  28.3 1.6 %collective-permute-done.7.act_other = bf16[6,96,192]{2,1,0:T(8,128)(2,1)S(1)} collective-permute-done((bf16[6,96,192]{2,1,0:T(8,128)(2,1)S(1)}, bf16[6,96,192]{2,1,0:T(8,128)(2,1)S(1)}, u32[]{:S(2)}, u32[]{:S(2)}) %collective-permute-start.7) | collective-permute-done | bytes 221216 | tf_op jit(solution)/shard_map/ppermute | solution.py:516
  29.9 6.0 %shard_map.138 = bf16[2,48,4,192]{3,2,1,0:T(4,128)(2,1)} custom-call(bf16[6,96,192]{2,1,0:T(8,128)(2,1)S(1)} %get-tuple-element.19.act_own, bf16[6,96,192]{2,1,0:T(8,128)(2,1)S(1)} %collective-permute-done.7.act_other, bf16[4,48,384]{2,1,0:T(8,128)(2,1)S(1)} %get-tuple-element.20.hidden_in, bf16[27,192,384]{2,1,0:T(8,128)(2,1)S(1)} %bitcast.12, ...), custom_call_target="tpu_custom_call" | custom-call | flops 1528823808 | bytes 7962624 | tf_op jit(solution)/shard_map/pallas_call | solution.py:518
  (10 shorter events, 0.0 us)
Async XLA Ops:
  0.0 15.4 %collective-permute-start.6 = (bf16[27,192,384]{2,1,0:T(8,128)(2,1)}, bf16[27,192,384]{2,1,0:T(8,128)(2,1)}, u32[]{:S(2)}, u32[]{:S(2)}) collective-permute-start(bf16[27,192,384]{2,1,0:T(8,128)(2,1)} %bitcast.11), channel_id=1, source_target_pairs={{0,1},{1,0},{2,3},{3,2},{4,5},{5,4},{6,7},{7,6},{8,9},{9,8},{10,11... | collective-permute-start | bytes 11943944 | tf_op jit(solution)/shard_map/ppermute | solution.py:451
  0.5 10.5 %collective-permute-start.4 = (bf16[27,16,192]{2,1,0:T(8,128)(2,1)}, bf16[27,16,192]{2,1,0:T(8,128)(2,1)S(1)}, u32[]{:S(2)}, u32[]{:S(2)}) collective-permute-start(bf16[27,16,192]{2,1,0:T(8,128)(2,1)} %stem_own.1), channel_id=1, source_target_pairs={{0,1},{1,0},{2,3},{3,2},{4,5},{5,4},{6,7},{7,6},{8,9},{9,8},{10,11... | collective-permute-start | bytes 497672 | tf_op jit(solution)/shard_map/ppermute | solution.py:450
  1.3 5.8 %collective-permute-start = (bf16[1,60,128]{2,1,0:T(8,128)(2,1)S(1)}, bf16[1,60,128]{2,1,0:T(8,128)(2,1)S(1)}, u32[]{:S(2)}, u32[]{:S(2)}) collective-permute-start(bf16[1,60,128]{2,1,0:T(8,128)(2,1)S(1)} %reshape.6), channel_id=1, source_target_pairs={{0,8},{1,5},{2,10},{3,7},{4,12},{5,1},{6,14},{7,3},{8,0},{9,13},{1... | collective-permute-start | bytes 46088 | tf_op jit(solution)/shard_map/ppermute | solution.py:460
  5.4 5.5 %collective-permute-start.1 = (bf16[1,60,128]{2,1,0:T(8,128)(2,1)S(1)}, bf16[1,60,128]{2,1,0:T(8,128)(2,1)S(1)}, u32[]{:S(2)}, u32[]{:S(2)}) collective-permute-start(bf16[1,60,128]{2,1,0:T(8,128)(2,1)S(1)} %reshape.6), channel_id=1, source_target_pairs={{0,12},{2,14},{4,8},{6,10},{8,4},{10,6},{12,0},{14,2},{1,13},{3,15... | collective-permute-start | bytes 46088 | tf_op jit(solution)/shard_map/ppermute | solution.py:462
  7.1 3.8 %collective-permute-start.2 = (bf16[1,60,128]{2,1,0:T(8,128)(2,1)S(1)}, bf16[1,60,128]{2,1,0:T(8,128)(2,1)S(1)}, u32[]{:S(2)}, u32[]{:S(2)}) collective-permute-start(bf16[1,60,128]{2,1,0:T(8,128)(2,1)S(1)} %collective-permute-done), channel_id=1, source_target_pairs={{0,1},{1,0},{2,3},{3,2},{4,5},{5,4},{6,7},{7,6},{8,9},{9,8},{10,11... | collective-permute-start | bytes 46088 | tf_op jit(solution)/shard_map/ppermute | solution.py:464
  7.9 3.0 %collective-permute-start.3 = (f32[8,192]{1,0:T(8,128)S(1)}, f32[8,192]{1,0:T(8,128)S(1)}, u32[]{:S(2)}, u32[]{:S(2)}) collective-permute-start(f32[8,192]{1,0:T(8,128)S(1)} %stack.31.small_own), channel_id=1, source_target_pairs={{0,1},{1,0},{2,3},{3,2},{4,5},{5,4},{6,7},{7,6},{8,9},{9,8},{10,11... | collective-permute-start | bytes 18440 | tf_op jit(solution)/shard_map/ppermute | solution.py:463
  11.0 4.3 %collective-permute-start.5 = (bf16[4,60,128]{2,1,0:T(8,128)(2,1)S(1)}, bf16[4,60,128]{2,1,0:T(8,128)(2,1)S(1)}, u32[]{:S(2)}, u32[]{:S(2)}) collective-permute-start(bf16[4,60,128]{2,1,0:T(8,128)(2,1)S(1)} %pad_maximum_fusion.1), channel_id=1, source_target_pairs={{0,2},{2,0},{4,6},{6,4},{8,10},{10,8},{12,14},{14,12},{1,3},{3,1},... | collective-permute-start | bytes 184328 | tf_op jit(solution)/shard_map/ppermute | solution.py:384
  12.6 0.9 %copy-start.2 = (bf16[27,16,192]{2,1,0:T(8,128)(2,1)S(1)}, bf16[27,16,192]{2,1,0:T(8,128)(2,1)}, u32[]{:S(2)}) copy-start(bf16[27,16,192]{2,1,0:T(8,128)(2,1)} %stem_own.1) | copy-start | bytes 497668
  13.5 0.7 %copy-start.4 = (s32[8]{0:T(128)S(1)}, s32[8]{0:T(128)}, u32[]{:S(2)}) copy-start(s32[8]{0:T(128)} %counts.1) | copy-start | bytes 100
  15.4 14.5 %copy-start = (bf16[27,384,192]{1,2,0:T(8,128)(2,1)S(1)}, bf16[27,384,192]{1,2,0:T(8,128)(2,1)}, u32[]{:S(2)}) copy-start(bf16[27,384,192]{1,2,0:T(8,128)(2,1)} %param.24) | copy-start | bytes 11943940
  15.4 14.5 %copy-start.1 = (bf16[9,384,192]{1,2,0:T(8,128)(2,1)S(1)}, bf16[9,384,192]{1,2,0:T(8,128)(2,1)}, u32[]{:S(2)}) copy-start(bf16[9,384,192]{1,2,0:T(8,128)(2,1)} %param.26) | copy-start | bytes 3981316
  15.4 14.5 %copy-start.3 = (f32[192]{0:T(256)S(1)}, f32[192]{0:T(256)}, u32[]{:S(2)}) copy-start(f32[192]{0:T(256)} %param.27) | copy-start | bytes 2308
  28.2 1.6 %collective-permute-start.7 = (bf16[6,96,192]{2,1,0:T(8,128)(2,1)S(1)}, bf16[6,96,192]{2,1,0:T(8,128)(2,1)S(1)}, u32[]{:S(2)}, u32[]{:S(2)}) collective-permute-start(bf16[6,96,192]{2,1,0:T(8,128)(2,1)S(1)} %get-tuple-element.19.act_own), channel_id=1, source_target_pairs={{0,1},{1,0},{2,3},{3,2},{4,5},{5,4},{6,7},{7,6},{8,9},{9,8},{10,11... | collective-permute-start | bytes 663560 | tf_op jit(solution)/shard_map/ppermute | solution.py:516

commit v7 on v6

--- a/solution.py
+++ b/solution.py
@@ -132,9 +132,10 @@
     vectors,
     small_own,
     weight_far,
-    unread,
+    next_far,
     act_out,
     hidden_out,
+    next_near,
     packed,
     shifted,
     patches,
@@ -144,6 +145,7 @@
     sums,
     weight,
     arrival,
+    next_arrival,
 ):
     fetch = pltpu.make_async_copy(weight_far, weight, arrival)
     fetch.start()
@@ -245,6 +247,8 @@
         lax.fori_loop(0, H // 2, activate, 0, unroll=2)
 
     fetch.wait()
+    carry = pltpu.make_async_copy(next_far, next_near, next_arrival)
+    carry.start()
     first_bias = small_own[4:5]
     for frame in range(F):
 
@@ -280,6 +284,7 @@
         begin = core * (frames * H * width) + spot_at
         value = take(hidden, pl.ds(begin, frames * H, stride=width), full)
         hidden_out[spot_at - 1] = value.astype(jnp.bfloat16)
+    carry.wait()
 
 
 def second_kernel(
@@ -476,14 +481,15 @@
         owners = lax.all_gather(latents, "tile", axis=0, tiled=True)
         prepared = prepare(small, small_other, stem_other, power)
     selection, stem_full, vectors = prepared
-    act, hidden = pl.pallas_call(
+    act, hidden, second_near = pl.pallas_call(
         first_kernel,
         out_shape=(
             jax.ShapeDtypeStruct((window, F * H, half), jnp.bfloat16),
             jax.ShapeDtypeStruct((window - 2, frames * H, full), jnp.bfloat16),
+            jax.ShapeDtypeStruct(second_weight.shape, jnp.bfloat16),
         ),
-        in_specs=[vmem] * 5 + [far, pl.BlockSpec(memory_space=pl.ANY)],
-        out_specs=(vmem, vmem),
+        in_specs=[vmem] * 5 + [far, far],
+        out_specs=(vmem, vmem, vmem),
         scratch_shapes=[
             pltpu.VMEM((tile_count, PACKED, 128), jnp.bfloat16),
             pltpu.VMEM((3, F, width, H_PAD * zc), jnp.float32),
@@ -493,6 +499,7 @@
             pltpu.VMEM((pl.cdiv(half, 128), F * H * width, 128), jnp.float32),
             pltpu.VMEM((8, full), jnp.float32),
             pltpu.VMEM(first_weight.shape, jnp.bfloat16),
+            pltpu.SemaphoreType.DMA,
             pltpu.SemaphoreType.DMA,
         ],
         cost_estimate=pl.CostEstimate(
@@ -510,7 +517,7 @@
         vectors,
         small,
         pltpu.with_memory_space_constraint(first_weight, pltpu.HBM),
-        second_other,
+        pltpu.with_memory_space_constraint(second_other, pltpu.HBM),
     )
 
     act_other = lax.ppermute(act, "chan", swap)
@@ -536,7 +543,7 @@
         act_other,
         hidden,
         second_weight,
-        second_other,
+        second_near,
         vectors,
         upsample_weight,
         upsample_bias.reshape(1, -1),

time: 36.2 us -> 34.1 us (0.942)
  Pallas kernels: 19.7 us -> 17.6 us
    pallas_call x1, Pallas kernels: 6.05 us -> 4.02 us  [on_device(): pl.pallas_call(functools.partial(second_kernel, tile_count), out_shape=ja...]
  transfers between devices with their start and end apart: 8 -> 8, of which waited for: 4 -> 4; matrix products, arithmetic and copies ran while one was open for 4% -> 5% of each run, Pallas kernels for 2% -> 2%
where the time goes in v7:
time: 34.1 us; the launch traced here: 33.9 us
  Pallas kernels  17.6 us (52%)
  starting transfers between devices  8.21 us (24%)
  waiting for transfers between devices  4.72 us (14%)
  local copies, waits for them, and re-layouts  3.19 us (9%)
    pallas_call x1, Pallas kernels, on_device(): pl.pallas_call(first_kernel, out_shape=(jax.ShapeDtypeStruct((window, F *...  12.8 us
    ppermute x1, starting transfers between devices, on_device(): one = lax.ppermute(latents, ('tile', 'chan'), pairs)  4.13 us
    pallas_call x1, Pallas kernels, on_device(): pl.pallas_call(functools.partial(second_kernel, tile_count), out_shape=ja...  4.02 us
    ppermute x1, waiting for transfers between devices, on_device(): two = lax.ppermute(latents, 'tile', both)  2.44 us
    unnamed x10, local copies, waits for them, and re-layouts  1.61 us
    ppermute x1, starting transfers between devices, exchanged(): moved = lax.ppermute(block, 'tile', [(i, i ^ step) for i in range(count)])  1.58 us
    ppermute x1, waiting for transfers between devices, on_device(): act_other = lax.ppermute(act, 'chan', swap)  1.57 us
    ppermute x1, starting transfers between devices, on_device(): two = lax.ppermute(latents, 'tile', both)  1.35 us
  transfers between devices with their start and end apart: 8, of which 4 were waited for; matrix products, arithmetic and copies ran while one was open for 5% of the time, Pallas kernels for 2%

profile of v7, /device:TPU:0, one launch (start us, length us, event | category | flops | bytes accessed | tf_op | source)
XLA Modules:
  0.0 33.9 jit_solution(11399972540561137124)
XLA Ops:
  0.0 0.5 %collective-permute-start.6 = (bf16[27,192,384]{2,1,0:T(8,128)(2,1)}, bf16[27,192,384]{2,1,0:T(8,128)(2,1)}, u32[]{:S(2)}, u32[]{:S(2)}) collective-permute-start(bf16[27,192,384]{2,1,0:T(8,128)(2,1)} %bitcast.11), channel_id=1, source_target_pairs={{0,1},{1,0},{2,3},{3,2},{4,5},{5,4},{6,7},{7,6},{8,9},{9,8},{10,11... | collective-permute-start | bytes 11943944 | tf_op jit(solution)/shard_map/ppermute | solution.py:456
  0.5 0.0 collective-permute-start.4
  0.5 0.8 %reshape.6 = bf16[1,60,128]{2,1,0:T(8,128)(2,1)S(1)} reshape(bf16[1,5,1536]{2,1,0:T(8,128)(2,1)} %param.14) | data formatting | bytes 30720 | tf_op jit(solution)/shard_map/reshape | solution.py:422
  1.3 4.1 %collective-permute-start = (bf16[1,60,128]{2,1,0:T(8,128)(2,1)S(1)}, bf16[1,60,128]{2,1,0:T(8,128)(2,1)S(1)}, u32[]{:S(2)}, u32[]{:S(2)}) collective-permute-start(bf16[1,60,128]{2,1,0:T(8,128)(2,1)S(1)} %reshape.6), channel_id=1, source_target_pairs={{0,8},{1,5},{2,10},{3,7},{4,12},{5,1},{6,14},{7,3},{8,0},{9,13},{1... | collective-permute-start | bytes 46088 | tf_op jit(solution)/shard_map/ppermute | solution.py:465
  5.4 1.3 %collective-permute-start.1 = (bf16[1,60,128]{2,1,0:T(8,128)(2,1)S(1)}, bf16[1,60,128]{2,1,0:T(8,128)(2,1)S(1)}, u32[]{:S(2)}, u32[]{:S(2)}) collective-permute-start(bf16[1,60,128]{2,1,0:T(8,128)(2,1)S(1)} %reshape.6), channel_id=1, source_target_pairs={{0,12},{2,14},{4,8},{6,10},{8,4},{10,6},{12,0},{14,2},{1,13},{3,15... | collective-permute-start | bytes 46088 | tf_op jit(solution)/shard_map/ppermute | solution.py:467
  6.8 0.4 %collective-permute-done = bf16[1,60,128]{2,1,0:T(8,128)(2,1)S(1)} collective-permute-done((bf16[1,60,128]{2,1,0:T(8,128)(2,1)S(1)}, bf16[1,60,128]{2,1,0:T(8,128)(2,1)S(1)}, u32[]{:S(2)}, u32[]{:S(2)}) %collective-permute-start) | collective-permute-done | bytes 15392 | tf_op jit(solution)/shard_map/ppermute | solution.py:465
  7.1 0.0 collective-permute-start.2
  7.1 0.8 %stack.31.small_own = f32[8,192]{1,0:T(8,128)S(1)} concatenate(f32[1,192]{1,0:T(1,128)} %bitcast.15, f32[1,192]{1,0:T(1,128)} %bitcast.16, f32[1,192]{1,0:T(1,128)} %bitcast.17, f32[1,192]{1,0:T(1,128)} %bitcast.18, f32[1,192]{1,0:T(1,128)} %bitcast.19, f32[1,192]{1,0:T(1,128)} %bitcast.20, f32[1,192]{1,0:T(1,128)} %bitcast.21, f32[1,192]{1,0:T(1,128)S(1)} %stack_broadcast_in_dim.3), dimensions={0} | concatenate | bytes 12288 | tf_op jit(solution)/shard_map/stack | solution.py:423
  7.9 0.6 %collective-permute-start.3 = (f32[8,192]{1,0:T(8,128)S(1)}, f32[8,192]{1,0:T(8,128)S(1)}, u32[]{:S(2)}, u32[]{:S(2)}) collective-permute-start(f32[8,192]{1,0:T(8,128)S(1)} %stack.31.small_own), channel_id=1, source_target_pairs={{0,1},{1,0},{2,3},{3,2},{4,5},{5,4},{6,7},{7,6},{8,9},{9,8},{10,11... | collective-permute-start | bytes 18440 | tf_op jit(solution)/shard_map/ppermute | solution.py:468
  8.5 2.4 %collective-permute-done.1 = bf16[1,60,128]{2,1,0:T(8,128)(2,1)S(1)} collective-permute-done((bf16[1,60,128]{2,1,0:T(8,128)(2,1)S(1)}, bf16[1,60,128]{2,1,0:T(8,128)(2,1)S(1)}, u32[]{:S(2)}, u32[]{:S(2)}) %collective-permute-start.1) | collective-permute-done | bytes 15392 | tf_op jit(solution)/shard_map/ppermute | solution.py:467
  11.0 0.0 collective-permute-done.2
  11.0 0.0 collective-permute-done.3.small_other
  11.0 1.6 %collective-permute-start.5 = (bf16[4,60,128]{2,1,0:T(8,128)(2,1)S(1)}, bf16[4,60,128]{2,1,0:T(8,128)(2,1)S(1)}, u32[]{:S(2)}, u32[]{:S(2)}) collective-permute-start(bf16[4,60,128]{2,1,0:T(8,128)(2,1)S(1)} %pad_maximum_fusion.1), channel_id=1, source_target_pairs={{0,2},{2,0},{4,6},{6,4},{8,10},{10,8},{12,14},{14,12},{1,3},{3,1},... | collective-permute-start | bytes 184328 | tf_op jit(solution)/shard_map/ppermute | solution.py:389
  12.6 0.9 %copy-done.2 = bf16[27,16,192]{2,1,0:T(8,128)(2,1)S(1)} copy-done((bf16[27,16,192]{2,1,0:T(8,128)(2,1)S(1)}, bf16[27,16,192]{2,1,0:T(8,128)(2,1)}, u32[]{:S(2)}) %copy-start.2) | copy-done | bytes 165912
  13.5 0.7 %copy-done.4 = s32[8]{0:T(128)S(1)} copy-done((s32[8]{0:T(128)S(1)}, s32[8]{0:T(128)}, u32[]{:S(2)}) %copy-start.4) | copy-done | bytes 56
  14.2 0.8 %shard_map.136 = (bf16[576,512]{1,0:T(8,128)(2,1)S(1)}, bf16[3,256,384]{2,1,0:T(8,128)(2,1)S(1)}, f32[8,384]{1,0:T(8,128)S(1)}) custom-call(s32[8]{0:T(128)S(1)} %copy-done.4, bf16[27,16,192]{2,1,0:T(8,128)(2,1)S(1)} %copy-done.2, bf16[27,16,192]{2,1,0:T(8,128)(2,1)S(1)} %collective-permute-done.4.stem_other, f32[8,192]{1,0:T(8,128)S(1)} %stack.31.small_own, ...), custom_call_target="tpu_custom_call" | custom-call | flops 100000000 | bytes 1000000 | tf_op jit(solution)/shard_map/pallas_call | solution.py:440
  15.0 0.3 collective-permute-done.5
  15.4 0.0 copy-start
  15.4 0.0 copy-start.1
  15.4 0.0 copy-start.3
  15.4 12.8 %shard_map.137 = (bf16[6,96,192]{2,1,0:T(8,128)(2,1)S(1)}, bf16[4,48,384]{2,1,0:T(8,128)(2,1)S(1)}, bf16[27,192,384]{2,1,0:T(8,128)(2,1)S(1)}) custom-call(bf16[8,60,128]{2,1,0:T(8,128)(2,1)S(1)} %pad_maximum_fusion.owners, bf16[576,512]{1,0:T(8,128)(2,1)S(1)} %get-tuple-element.17.selection, bf16[3,256,384]{2,1,0:T(8,128)(2,1)S(1)} %get-tuple-element.18.stem_full, ...), custom_call_target="tpu_custom_call" | custom-call | flops 4586471424 | bytes 3981312 | tf_op jit(solution)/shard_map/pallas_call | solution.py:484
  28.2 0.1 collective-permute-start.7
  28.3 1.6 %collective-permute-done.7.act_other = bf16[6,96,192]{2,1,0:T(8,128)(2,1)S(1)} collective-permute-done((bf16[6,96,192]{2,1,0:T(8,128)(2,1)S(1)}, bf16[6,96,192]{2,1,0:T(8,128)(2,1)S(1)}, u32[]{:S(2)}, u32[]{:S(2)}) %collective-permute-start.7) | collective-permute-done | bytes 221216 | tf_op jit(solution)/shard_map/ppermute | solution.py:523
  29.9 4.0 %shard_map.138 = bf16[2,48,4,192]{3,2,1,0:T(4,128)(2,1)} custom-call(bf16[6,96,192]{2,1,0:T(8,128)(2,1)S(1)} %get-tuple-element.20.act_own, bf16[6,96,192]{2,1,0:T(8,128)(2,1)S(1)} %collective-permute-done.7.act_other, bf16[4,48,384]{2,1,0:T(8,128)(2,1)S(1)} %get-tuple-element.21.hidden_in, bf16[27,192,384]{2,1,0:T(8,128)(2,1)S(1)} %bitcast.12, ...), custom_call_target="tpu_custom_call" | custom-call | flops 1528823808 | bytes 7962624 | tf_op jit(solution)/shard_map/pallas_call | solution.py:525
  (10 shorter events, 0.0 us)
Async XLA Ops:
  0.0 15.4 %collective-permute-start.6 = (bf16[27,192,384]{2,1,0:T(8,128)(2,1)}, bf16[27,192,384]{2,1,0:T(8,128)(2,1)}, u32[]{:S(2)}, u32[]{:S(2)}) collective-permute-start(bf16[27,192,384]{2,1,0:T(8,128)(2,1)} %bitcast.11), channel_id=1, source_target_pairs={{0,1},{1,0},{2,3},{3,2},{4,5},{5,4},{6,7},{7,6},{8,9},{9,8},{10,11... | collective-permute-start | bytes 11943944 | tf_op jit(solution)/shard_map/ppermute | solution.py:456
  0.5 10.5 %collective-permute-start.4 = (bf16[27,16,192]{2,1,0:T(8,128)(2,1)}, bf16[27,16,192]{2,1,0:T(8,128)(2,1)S(1)}, u32[]{:S(2)}, u32[]{:S(2)}) collective-permute-start(bf16[27,16,192]{2,1,0:T(8,128)(2,1)} %stem_own.1), channel_id=1, source_target_pairs={{0,1},{1,0},{2,3},{3,2},{4,5},{5,4},{6,7},{7,6},{8,9},{9,8},{10,11... | collective-permute-start | bytes 497672 | tf_op jit(solution)/shard_map/ppermute | solution.py:455
  1.3 5.8 %collective-permute-start = (bf16[1,60,128]{2,1,0:T(8,128)(2,1)S(1)}, bf16[1,60,128]{2,1,0:T(8,128)(2,1)S(1)}, u32[]{:S(2)}, u32[]{:S(2)}) collective-permute-start(bf16[1,60,128]{2,1,0:T(8,128)(2,1)S(1)} %reshape.6), channel_id=1, source_target_pairs={{0,8},{1,5},{2,10},{3,7},{4,12},{5,1},{6,14},{7,3},{8,0},{9,13},{1... | collective-permute-start | bytes 46088 | tf_op jit(solution)/shard_map/ppermute | solution.py:465
  5.4 5.5 %collective-permute-start.1 = (bf16[1,60,128]{2,1,0:T(8,128)(2,1)S(1)}, bf16[1,60,128]{2,1,0:T(8,128)(2,1)S(1)}, u32[]{:S(2)}, u32[]{:S(2)}) collective-permute-start(bf16[1,60,128]{2,1,0:T(8,128)(2,1)S(1)} %reshape.6), channel_id=1, source_target_pairs={{0,12},{2,14},{4,8},{6,10},{8,4},{10,6},{12,0},{14,2},{1,13},{3,15... | collective-permute-start | bytes 46088 | tf_op jit(solution)/shard_map/ppermute | solution.py:467
  7.1 3.8 %collective-permute-start.2 = (bf16[1,60,128]{2,1,0:T(8,128)(2,1)S(1)}, bf16[1,60,128]{2,1,0:T(8,128)(2,1)S(1)}, u32[]{:S(2)}, u32[]{:S(2)}) collective-permute-start(bf16[1,60,128]{2,1,0:T(8,128)(2,1)S(1)} %collective-permute-done), channel_id=1, source_target_pairs={{0,1},{1,0},{2,3},{3,2},{4,5},{5,4},{6,7},{7,6},{8,9},{9,8},{10,11... | collective-permute-start | bytes 46088 | tf_op jit(solution)/shard_map/ppermute | solution.py:469
  7.9 3.0 %collective-permute-start.3 = (f32[8,192]{1,0:T(8,128)S(1)}, f32[8,192]{1,0:T(8,128)S(1)}, u32[]{:S(2)}, u32[]{:S(2)}) collective-permute-start(f32[8,192]{1,0:T(8,128)S(1)} %stack.31.small_own), channel_id=1, source_target_pairs={{0,1},{1,0},{2,3},{3,2},{4,5},{5,4},{6,7},{7,6},{8,9},{9,8},{10,11... | collective-permute-start | bytes 18440 | tf_op jit(solution)/shard_map/ppermute | solution.py:468
  11.0 4.3 %collective-permute-start.5 = (bf16[4,60,128]{2,1,0:T(8,128)(2,1)S(1)}, bf16[4,60,128]{2,1,0:T(8,128)(2,1)S(1)}, u32[]{:S(2)}, u32[]{:S(2)}) collective-permute-start(bf16[4,60,128]{2,1,0:T(8,128)(2,1)S(1)} %pad_maximum_fusion.1), channel_id=1, source_target_pairs={{0,2},{2,0},{4,6},{6,4},{8,10},{10,8},{12,14},{14,12},{1,3},{3,1},... | collective-permute-start | bytes 184328 | tf_op jit(solution)/shard_map/ppermute | solution.py:389
  12.6 0.9 %copy-start.2 = (bf16[27,16,192]{2,1,0:T(8,128)(2,1)S(1)}, bf16[27,16,192]{2,1,0:T(8,128)(2,1)}, u32[]{:S(2)}) copy-start(bf16[27,16,192]{2,1,0:T(8,128)(2,1)} %stem_own.1) | copy-start | bytes 497668
  13.5 0.7 %copy-start.4 = (s32[8]{0:T(128)S(1)}, s32[8]{0:T(128)}, u32[]{:S(2)}) copy-start(s32[8]{0:T(128)} %counts.1) | copy-start | bytes 100
  15.4 14.5 %copy-start = (bf16[27,384,192]{1,2,0:T(8,128)(2,1)S(1)}, bf16[27,384,192]{1,2,0:T(8,128)(2,1)}, u32[]{:S(2)}) copy-start(bf16[27,384,192]{1,2,0:T(8,128)(2,1)} %param.24) | copy-start | bytes 11943940
  15.4 14.5 %copy-start.1 = (bf16[9,384,192]{1,2,0:T(8,128)(2,1)S(1)}, bf16[9,384,192]{1,2,0:T(8,128)(2,1)}, u32[]{:S(2)}) copy-start(bf16[9,384,192]{1,2,0:T(8,128)(2,1)} %param.26) | copy-start | bytes 3981316
  15.4 14.5 %copy-start.3 = (f32[192]{0:T(256)S(1)}, f32[192]{0:T(256)}, u32[]{:S(2)}) copy-start(f32[192]{0:T(256)} %param.27) | copy-start | bytes 2308
  28.2 1.6 %collective-permute-start.7 = (bf16[6,96,192]{2,1,0:T(8,128)(2,1)S(1)}, bf16[6,96,192]{2,1,0:T(8,128)(2,1)S(1)}, u32[]{:S(2)}, u32[]{:S(2)}) collective-permute-start(bf16[6,96,192]{2,1,0:T(8,128)(2,1)S(1)} %get-tuple-element.20.act_own), channel_id=1, source_target_pairs={{0,1},{1,0},{2,3},{3,2},{4,5},{5,4},{6,7},{7,6},{8,9},{9,8},{10,11... | collective-permute-start | bytes 663560 | tf_op jit(solution)/shard_map/ppermute | solution.py:523

commit v8 on v6

--- a/solution.py
+++ b/solution.py
@@ -76,8 +76,24 @@
 
 
 def prepare_kernel(
-    power, counts, stem_own, stem_other, small_own, small_other, selection, stem_full, vectors
+    power,
+    counts_far,
+    stem_far,
+    stem_other,
+    small_own,
+    small_other,
+    selection,
+    stem_full,
+    vectors,
+    counts,
+    stem_own,
+    counts_arrival,
+    stem_arrival,
 ):
+    counts_fetch = pltpu.make_async_copy(counts_far, counts, counts_arrival)
+    counts_fetch.start()
+    stem_fetch = pltpu.make_async_copy(stem_far, stem_own, stem_arrival)
+    stem_fetch.start()
     tile_count = counts.shape[0]
     width = tile_count * W_DEV
     me = lax.axis_index("tile")
@@ -92,6 +108,7 @@
     row_at = lane - place_at * PACKED
     slot_at = jnp.floor((row_at.astype(jnp.float32) + 0.5) * (1.0 / blocks)).astype(jnp.int32)
     held = jnp.full((8, packed_rows), -5, jnp.int32)
+    counts_fetch.wait()
     start = jnp.int32(0)
     bits = tile_count.bit_length() - 1
     for owner in range(tile_count):
@@ -118,6 +135,7 @@
         selection[rows, :] = (wanted + block == code).astype(jnp.bfloat16)
 
     stem_full[...] = jnp.zeros(stem_full.shape, jnp.bfloat16)
+    stem_fetch.wait()
     for tap in range(27):
         a, b, e = tap // 9, tap // 3 % 3, tap % 3
         at = e * 4 * zc + b * zc
@@ -132,9 +150,14 @@
     vectors,
     small_own,
     weight_far,
-    unread,
+    others_far,
+    own_far,
+    up_far,
     act_out,
     hidden_out,
+    others_near,
+    own_near,
+    up_near,
     packed,
     shifted,
     patches,
@@ -144,6 +167,7 @@
     sums,
     weight,
     arrival,
+    next_arrivals,
 ):
     fetch = pltpu.make_async_copy(weight_far, weight, arrival)
     fetch.start()
@@ -245,6 +269,14 @@
         lax.fori_loop(0, H // 2, activate, 0, unroll=2)
 
     fetch.wait()
+    carries = [
+        pltpu.make_async_copy(source, target, next_arrivals.at[at])
+        for at, (source, target) in enumerate(
+            ((own_far, own_near), (others_far, others_near), (up_far, up_near))
+        )
+    ]
+    for carry in carries:
+        carry.start()
     first_bias = small_own[4:5]
     for frame in range(F):
 
@@ -280,6 +312,8 @@
         begin = core * (frames * H * width) + spot_at
         value = take(hidden, pl.ds(begin, frames * H, stride=width), full)
         hidden_out[spot_at - 1] = value.astype(jnp.bfloat16)
+    for carry in carries:
+        carry.wait()
 
 
 def second_kernel(
@@ -439,13 +473,25 @@
                 jax.ShapeDtypeStruct((3, 256, full), jnp.bfloat16),
                 jax.ShapeDtypeStruct((small.shape[0], full), jnp.float32),
             ),
-            in_specs=[pl.BlockSpec(memory_space=pltpu.SMEM)] + [vmem] * 4,
+            in_specs=[far] * 2 + [vmem] * 3,
             out_specs=(vmem,) * 3,
+            scratch_shapes=[
+                pltpu.SMEM(tile_counts.shape, jnp.int32),
+                pltpu.VMEM(stem_weight.shape, jnp.bfloat16),
+                pltpu.SemaphoreType.DMA,
+                pltpu.SemaphoreType.DMA,
+            ],
             cost_estimate=pl.CostEstimate(flops=10**8, bytes_accessed=10**6, transcendentals=0),
             compiler_params=pltpu.CompilerParams(
                 vmem_limit_bytes=(6 + 2 * width // 16) * 1024 * 1024
             ),
-        )(tile_counts, stem_weight, stem_other, small, small_other)
+        )(
+            pltpu.with_memory_space_constraint(tile_counts, pltpu.HBM),
+            pltpu.with_memory_space_constraint(stem_weight, pltpu.HBM),
+            stem_other,
+            small,
+            small_other,
+        )
 
     stem_other = lax.ppermute(stem_weight, "chan", swap)
     second_other = lax.ppermute(second_weight, "chan", swap)
@@ -476,14 +522,17 @@
         owners = lax.all_gather(latents, "tile", axis=0, tiled=True)
         prepared = prepare(small, small_other, stem_other, power)
     selection, stem_full, vectors = prepared
-    act, hidden = pl.pallas_call(
+    act, hidden, other_near, own_near, up_near = pl.pallas_call(
         first_kernel,
         out_shape=(
             jax.ShapeDtypeStruct((window, F * H, half), jnp.bfloat16),
             jax.ShapeDtypeStruct((window - 2, frames * H, full), jnp.bfloat16),
+            jax.ShapeDtypeStruct(second_weight.shape, jnp.bfloat16),
+            jax.ShapeDtypeStruct(second_weight.shape, jnp.bfloat16),
+            jax.ShapeDtypeStruct(upsample_weight.shape, jnp.bfloat16),
         ),
-        in_specs=[vmem] * 5 + [far, pl.BlockSpec(memory_space=pl.ANY)],
-        out_specs=(vmem, vmem),
+        in_specs=[vmem] * 5 + [far] * 4,
+        out_specs=(vmem,) * 5,
         scratch_shapes=[
             pltpu.VMEM((tile_count, PACKED, 128), jnp.bfloat16),
             pltpu.VMEM((3, F, width, H_PAD * zc), jnp.float32),
@@ -494,6 +543,7 @@
             pltpu.VMEM((8, full), jnp.float32),
             pltpu.VMEM(first_weight.shape, jnp.bfloat16),
             pltpu.SemaphoreType.DMA,
+            pltpu.SemaphoreType.DMA((3,)),
         ],
         cost_estimate=pl.CostEstimate(
             flops=2 * F * H * width * 27 * full * half * 3 // 4,
@@ -510,7 +560,9 @@
         vectors,
         small,
         pltpu.with_memory_space_constraint(first_weight, pltpu.HBM),
-        second_other,
+        pltpu.with_memory_space_constraint(second_other, pltpu.HBM),
+        pltpu.with_memory_space_constraint(second_weight, pltpu.HBM),
+        pltpu.with_memory_space_constraint(upsample_weight, pltpu.HBM),
     )
 
     act_other = lax.ppermute(act, "chan", swap)
@@ -535,10 +587,10 @@
         act,
         act_other,
         hidden,
-        second_weight,
-        second_other,
+        own_near,
+        other_near,
         vectors,
-        upsample_weight,
+        up_near,
         upsample_bias.reshape(1, -1),
     )
     return out

time: 36.2 us -> 34.1 us (0.942)
  Pallas kernels: 19.7 us -> 18 us
  local copies, waits for them, and re-layouts: 3.19 us -> 1.58 us
  waiting for transfers between devices: 4.72 us -> 5.99 us
    pallas_call x1, Pallas kernels: 6.05 us -> 4.04 us  [on_device(): pl.pallas_call(functools.partial(second_kernel, tile_count), out_shape=ja...]
    unnamed x10 -> x2, local copies, waits for them, and re-layouts: 1.61 us -> 0.01 us
    ppermute x1, waiting for transfers between devices: 0.33 us -> 1.6 us  [exchanged(): moved = lax.ppermute(block, 'tile', [(i, i ^ step) for i in range(count)])]
  transfers between devices with their start and end apart: 8 -> 8, of which waited for: 4 -> 4; matrix products, arithmetic and copies ran while one was open for 4% -> 5% of each run, Pallas kernels for 2% -> 3%
where the time goes in v8:
time: 34.1 us; the launch traced here: 33.9 us
  Pallas kernels  18 us (53%)
  starting transfers between devices  8.21 us (24%)
  waiting for transfers between devices  5.99 us (18%)
  local copies, waits for them, and re-layouts  1.58 us (5%)
    pallas_call x1, Pallas kernels, on_device(): pl.pallas_call(first_kernel, out_shape=(jax.ShapeDtypeStruct((window, F *...  12.8 us
    ppermute x1, starting transfers between devices, on_device(): one = lax.ppermute(latents, ('tile', 'chan'), pairs)  4.13 us
    pallas_call x1, Pallas kernels, on_device(): pl.pallas_call(functools.partial(second_kernel, tile_count), out_shape=ja...  4.04 us
    ppermute x1, waiting for transfers between devices, on_device(): two = lax.ppermute(latents, 'tile', both)  2.44 us
    ppermute x1, waiting for transfers between devices, exchanged(): moved = lax.ppermute(block, 'tile', [(i, i ^ step) for i in range(count)])  1.6 us
    ppermute x1, starting transfers between devices, exchanged(): moved = lax.ppermute(block, 'tile', [(i, i ^ step) for i in range(count)])  1.58 us
    ppermute x1, waiting for transfers between devices, on_device(): act_other = lax.ppermute(act, 'chan', swap)  1.57 us
    ppermute x1, starting transfers between devices, on_device(): two = lax.ppermute(latents, 'tile', both)  1.35 us
  transfers between devices with their start and end apart: 8, of which 4 were waited for; matrix products, arithmetic and copies ran while one was open for 5% of the time, Pallas kernels for 3%

profile of v8, /device:TPU:0, one launch (start us, length us, event | category | flops | bytes accessed | tf_op | source)
XLA Modules:
  0.0 33.9 jit_solution(6460183846157333006)
XLA Ops:
  0.0 0.5 %collective-permute-start.6 = (bf16[27,192,384]{2,1,0:T(8,128)(2,1)}, bf16[27,192,384]{2,1,0:T(8,128)(2,1)}, u32[]{:S(2)}, u32[]{:S(2)}) collective-permute-start(bf16[27,192,384]{2,1,0:T(8,128)(2,1)} %bitcast.20), channel_id=1, source_target_pairs={{0,1},{1,0},{2,3},{3,2},{4,5},{5,4},{6,7},{7,6},{8,9},{9,8},{10,11... | collective-permute-start | bytes 11943944 | tf_op jit(solution)/shard_map/ppermute | solution.py:497
  0.5 0.0 collective-permute-start.4
  0.5 0.8 %reshape.6 = bf16[1,60,128]{2,1,0:T(8,128)(2,1)S(1)} reshape(bf16[1,5,1536]{2,1,0:T(8,128)(2,1)} %param.14) | data formatting | bytes 30720 | tf_op jit(solution)/shard_map/reshape | solution.py:451
  1.3 4.1 %collective-permute-start = (bf16[1,60,128]{2,1,0:T(8,128)(2,1)S(1)}, bf16[1,60,128]{2,1,0:T(8,128)(2,1)S(1)}, u32[]{:S(2)}, u32[]{:S(2)}) collective-permute-start(bf16[1,60,128]{2,1,0:T(8,128)(2,1)S(1)} %reshape.6), channel_id=1, source_target_pairs={{0,8},{1,5},{2,10},{3,7},{4,12},{5,1},{6,14},{7,3},{8,0},{9,13},{1... | collective-permute-start | bytes 46088 | tf_op jit(solution)/shard_map/ppermute | solution.py:506
  5.4 1.3 %collective-permute-start.1 = (bf16[1,60,128]{2,1,0:T(8,128)(2,1)S(1)}, bf16[1,60,128]{2,1,0:T(8,128)(2,1)S(1)}, u32[]{:S(2)}, u32[]{:S(2)}) collective-permute-start(bf16[1,60,128]{2,1,0:T(8,128)(2,1)S(1)} %reshape.6), channel_id=1, source_target_pairs={{0,12},{2,14},{4,8},{6,10},{8,4},{10,6},{12,0},{14,2},{1,13},{3,15... | collective-permute-start | bytes 46088 | tf_op jit(solution)/shard_map/ppermute | solution.py:508
  6.8 0.4 %collective-permute-done = bf16[1,60,128]{2,1,0:T(8,128)(2,1)S(1)} collective-permute-done((bf16[1,60,128]{2,1,0:T(8,128)(2,1)S(1)}, bf16[1,60,128]{2,1,0:T(8,128)(2,1)S(1)}, u32[]{:S(2)}, u32[]{:S(2)}) %collective-permute-start) | collective-permute-done | bytes 15392 | tf_op jit(solution)/shard_map/ppermute | solution.py:506
  7.1 0.0 collective-permute-start.2
  7.1 0.8 %stack.31.small_own = f32[8,192]{1,0:T(8,128)S(1)} concatenate(f32[1,192]{1,0:T(1,128)} %bitcast.12, f32[1,192]{1,0:T(1,128)} %bitcast.13, f32[1,192]{1,0:T(1,128)} %bitcast.14, f32[1,192]{1,0:T(1,128)} %bitcast.15, f32[1,192]{1,0:T(1,128)} %bitcast.16, f32[1,192]{1,0:T(1,128)} %bitcast.17, f32[1,192]{1,0:T(1,128)} %bitcast.18, f32[1,192]{1,0:T(1,128)S(1)} %stack_broadcast_in_dim.3), dimensions={0} | concatenate | bytes 12288 | tf_op jit(solution)/shard_map/stack | solution.py:452
  7.9 0.6 %collective-permute-start.3 = (f32[8,192]{1,0:T(8,128)S(1)}, f32[8,192]{1,0:T(8,128)S(1)}, u32[]{:S(2)}, u32[]{:S(2)}) collective-permute-start(f32[8,192]{1,0:T(8,128)S(1)} %stack.31.small_own), channel_id=1, source_target_pairs={{0,1},{1,0},{2,3},{3,2},{4,5},{5,4},{6,7},{7,6},{8,9},{9,8},{10,11... | collective-permute-start | bytes 18440 | tf_op jit(solution)/shard_map/ppermute | solution.py:509
  8.5 2.4 %collective-permute-done.1 = bf16[1,60,128]{2,1,0:T(8,128)(2,1)S(1)} collective-permute-done((bf16[1,60,128]{2,1,0:T(8,128)(2,1)S(1)}, bf16[1,60,128]{2,1,0:T(8,128)(2,1)S(1)}, u32[]{:S(2)}, u32[]{:S(2)}) %collective-permute-start.1) | collective-permute-done | bytes 15392 | tf_op jit(solution)/shard_map/ppermute | solution.py:508
  11.0 0.0 collective-permute-done.2
  11.0 0.0 collective-permute-done.3.small_other
  11.0 0.0 collective-permute-done.4.stem_other
  11.0 1.6 %collective-permute-start.5 = (bf16[4,60,128]{2,1,0:T(8,128)(2,1)S(1)}, bf16[4,60,128]{2,1,0:T(8,128)(2,1)S(1)}, u32[]{:S(2)}, u32[]{:S(2)}) collective-permute-start(bf16[4,60,128]{2,1,0:T(8,128)(2,1)S(1)} %pad_maximum_fusion.1), channel_id=1, source_target_pairs={{0,2},{2,0},{4,6},{6,4},{8,10},{10,8},{12,14},{14,12},{1,3},{3,1},... | collective-permute-start | bytes 184328 | tf_op jit(solution)/shard_map/ppermute | solution.py:418
  12.6 1.1 %shard_map.136 = (bf16[576,512]{1,0:T(8,128)(2,1)S(1)}, bf16[3,256,384]{2,1,0:T(8,128)(2,1)S(1)}, f32[8,384]{1,0:T(8,128)S(1)}) custom-call(s32[8]{0:T(128)} %counts_far.1, bf16[27,16,192]{2,1,0:T(8,128)(2,1)} %stem_far.1, bf16[27,16,192]{2,1,0:T(8,128)(2,1)S(1)} %collective-permute-done.4.stem_other, f32[8,192]{1,0:T(8,128)S(1)} %stack.31.small_own, ...), custom_call_target="tpu_custom_call" | custom-call | flops 100000000 | bytes 1000000 | tf_op jit(solution)/shard_map/pallas_call | solution.py:469
  13.7 1.6 %collective-permute-done.5 = bf16[4,60,128]{2,1,0:T(8,128)(2,1)S(1)} collective-permute-done((bf16[4,60,128]{2,1,0:T(8,128)(2,1)S(1)}, bf16[4,60,128]{2,1,0:T(8,128)(2,1)S(1)}, u32[]{:S(2)}, u32[]{:S(2)}) %collective-permute-start.5) | collective-permute-done | bytes 61472 | tf_op jit(solution)/shard_map/ppermute | solution.py:418
  15.3 0.0 collective-permute-done.6.others_far
  15.4 0.0 copy-start
  15.4 12.8 %shard_map.137 = (bf16[6,96,192]{2,1,0:T(8,128)(2,1)S(1)}, bf16[4,48,384]{2,1,0:T(8,128)(2,1)S(1)}, bf16[27,192,384]{2,1,0:T(8,128)(2,1)S(1)}, bf16[27,192,384]{2,1,0:T(8,128)(2,1)S(1)}, bf16[9,192,384]{2,1,0:T(8,128)(2,1)S(1)}) custom-call(bf16[8,60,128]{2,1,0:T(8,128)(2,1)S(1)} %pad_maximum_fusion.owners, ...), custom_call_target="tpu_custom_call" | custom-call | flops 4586471424 | bytes 3981312 | tf_op jit(solution)/shard_map/pallas_call | solution.py:525
  28.2 0.1 collective-permute-start.7
  28.3 1.6 %collective-permute-done.7.act_other = bf16[6,96,192]{2,1,0:T(8,128)(2,1)S(1)} collective-permute-done((bf16[6,96,192]{2,1,0:T(8,128)(2,1)S(1)}, bf16[6,96,192]{2,1,0:T(8,128)(2,1)S(1)}, u32[]{:S(2)}, u32[]{:S(2)}) %collective-permute-start.7) | collective-permute-done | bytes 221216 | tf_op jit(solution)/shard_map/ppermute | solution.py:568
  29.9 0.0 copy-done
  29.9 4.0 %shard_map.138 = bf16[2,48,4,192]{3,2,1,0:T(4,128)(2,1)} custom-call(bf16[6,96,192]{2,1,0:T(8,128)(2,1)S(1)} %get-tuple-element.22.act_own, bf16[6,96,192]{2,1,0:T(8,128)(2,1)S(1)} %collective-permute-done.7.act_other, bf16[4,48,384]{2,1,0:T(8,128)(2,1)S(1)} %get-tuple-element.23.hidden_in, bf16[27,192,384]{2,1,0:T(8,128)(2,1)S(1)} %get-tuple-element.24.weight_own, ...), custom_call_target="tpu_custom_call" | custom-call | flops 1528823808 | bytes 7962624 | tf_op jit(solution)/shard_map/pallas_call | solution.py:570
  (3 shorter events, 0.0 us)
Async XLA Ops:
  0.0 15.4 %collective-permute-start.6 = (bf16[27,192,384]{2,1,0:T(8,128)(2,1)}, bf16[27,192,384]{2,1,0:T(8,128)(2,1)}, u32[]{:S(2)}, u32[]{:S(2)}) collective-permute-start(bf16[27,192,384]{2,1,0:T(8,128)(2,1)} %bitcast.20), channel_id=1, source_target_pairs={{0,1},{1,0},{2,3},{3,2},{4,5},{5,4},{6,7},{7,6},{8,9},{9,8},{10,11... | collective-permute-start | bytes 11943944 | tf_op jit(solution)/shard_map/ppermute | solution.py:497
  0.5 10.5 %collective-permute-start.4 = (bf16[27,16,192]{2,1,0:T(8,128)(2,1)}, bf16[27,16,192]{2,1,0:T(8,128)(2,1)S(1)}, u32[]{:S(2)}, u32[]{:S(2)}) collective-permute-start(bf16[27,16,192]{2,1,0:T(8,128)(2,1)} %stem_far.1), channel_id=1, source_target_pairs={{0,1},{1,0},{2,3},{3,2},{4,5},{5,4},{6,7},{7,6},{8,9},{9,8},{10,11... | collective-permute-start | bytes 497672 | tf_op jit(solution)/shard_map/ppermute | solution.py:496
  1.3 5.8 %collective-permute-start = (bf16[1,60,128]{2,1,0:T(8,128)(2,1)S(1)}, bf16[1,60,128]{2,1,0:T(8,128)(2,1)S(1)}, u32[]{:S(2)}, u32[]{:S(2)}) collective-permute-start(bf16[1,60,128]{2,1,0:T(8,128)(2,1)S(1)} %reshape.6), channel_id=1, source_target_pairs={{0,8},{1,5},{2,10},{3,7},{4,12},{5,1},{6,14},{7,3},{8,0},{9,13},{1... | collective-permute-start | bytes 46088 | tf_op jit(solution)/shard_map/ppermute | solution.py:506
  5.4 5.5 %collective-permute-start.1 = (bf16[1,60,128]{2,1,0:T(8,128)(2,1)S(1)}, bf16[1,60,128]{2,1,0:T(8,128)(2,1)S(1)}, u32[]{:S(2)}, u32[]{:S(2)}) collective-permute-start(bf16[1,60,128]{2,1,0:T(8,128)(2,1)S(1)} %reshape.6), channel_id=1, source_target_pairs={{0,12},{2,14},{4,8},{6,10},{8,4},{10,6},{12,0},{14,2},{1,13},{3,15... | collective-permute-start | bytes 46088 | tf_op jit(solution)/shard_map/ppermute | solution.py:508
  7.1 3.8 %collective-permute-start.2 = (bf16[1,60,128]{2,1,0:T(8,128)(2,1)S(1)}, bf16[1,60,128]{2,1,0:T(8,128)(2,1)S(1)}, u32[]{:S(2)}, u32[]{:S(2)}) collective-permute-start(bf16[1,60,128]{2,1,0:T(8,128)(2,1)S(1)} %collective-permute-done), channel_id=1, source_target_pairs={{0,1},{1,0},{2,3},{3,2},{4,5},{5,4},{6,7},{7,6},{8,9},{9,8},{10,11... | collective-permute-start | bytes 46088 | tf_op jit(solution)/shard_map/ppermute | solution.py:510
  7.9 3.0 %collective-permute-start.3 = (f32[8,192]{1,0:T(8,128)S(1)}, f32[8,192]{1,0:T(8,128)S(1)}, u32[]{:S(2)}, u32[]{:S(2)}) collective-permute-start(f32[8,192]{1,0:T(8,128)S(1)} %stack.31.small_own), channel_id=1, source_target_pairs={{0,1},{1,0},{2,3},{3,2},{4,5},{5,4},{6,7},{7,6},{8,9},{9,8},{10,11... | collective-permute-start | bytes 18440 | tf_op jit(solution)/shard_map/ppermute | solution.py:509
  11.0 4.3 %collective-permute-start.5 = (bf16[4,60,128]{2,1,0:T(8,128)(2,1)S(1)}, bf16[4,60,128]{2,1,0:T(8,128)(2,1)S(1)}, u32[]{:S(2)}, u32[]{:S(2)}) collective-permute-start(bf16[4,60,128]{2,1,0:T(8,128)(2,1)S(1)} %pad_maximum_fusion.1), channel_id=1, source_target_pairs={{0,2},{2,0},{4,6},{6,4},{8,10},{10,8},{12,14},{14,12},{1,3},{3,1},... | collective-permute-start | bytes 184328 | tf_op jit(solution)/shard_map/ppermute | solution.py:418
  15.4 14.5 %copy-start = (f32[192]{0:T(256)S(1)}, f32[192]{0:T(256)}, u32[]{:S(2)}) copy-start(f32[192]{0:T(256)} %param.27) | copy-start | bytes 2308
  28.2 1.6 %collective-permute-start.7 = (bf16[6,96,192]{2,1,0:T(8,128)(2,1)S(1)}, bf16[6,96,192]{2,1,0:T(8,128)(2,1)S(1)}, u32[]{:S(2)}, u32[]{:S(2)}) collective-permute-start(bf16[6,96,192]{2,1,0:T(8,128)(2,1)S(1)} %get-tuple-element.22.act_own), channel_id=1, source_target_pairs={{0,1},{1,0},{2,3},{3,2},{4,5},{5,4},{6,7},{7,6},{8,9},{9,8},{10,11... | collective-permute-start | bytes 663560 | tf_op jit(solution)/shard_map/ppermute | solution.py:568

commit v9 on v8

--- a/solution.py
+++ b/solution.py
@@ -24,18 +24,23 @@
     return jnp.where(core == 0, low, high)
 
 
-def group_mean(column_sums, per_group, cells):
-    channels = column_sums.shape[1]
+def same_group(channels, per_group):
     row = lax.broadcasted_iota(jnp.int32, (channels, channels), 0).astype(jnp.float32)
     column = lax.broadcasted_iota(jnp.int32, (channels, channels), 1).astype(jnp.float32)
     same = jnp.floor((row + 0.5) / per_group) == jnp.floor((column + 0.5) / per_group)
-    total = jnp.dot(
-        column_sums,
-        same.astype(jnp.float32),
-        precision=lax.Precision.HIGHEST,
-        preferred_element_type=jnp.float32,
-    )
-    return total[0:1] * (1.0 / (cells * per_group))
+    return same.astype(jnp.bfloat16)
+
+
+def group_mean(column_sums, same, per_group, cells):
+    channels = column_sums.shape[1]
+    high = column_sums.astype(jnp.bfloat16).astype(jnp.float32)
+    rest = column_sums - high
+    middle = rest.astype(jnp.bfloat16).astype(jnp.float32)
+    terms = jnp.concatenate([high, middle, rest - middle], axis=0).astype(jnp.bfloat16)
+    totals = jnp.dot(
+        terms, same[0:channels, 0:channels], preferred_element_type=jnp.float32
+    )
+    return (totals[0:1] + totals[8:9] + totals[16:17]) * (1.0 / (cells * per_group))
 
 
 def put(ref, place, value):
@@ -85,6 +90,7 @@
     selection,
     stem_full,
     vectors,
+    same,
     counts,
     stem_own,
     counts_arrival,
@@ -141,6 +147,7 @@
         at = e * 4 * zc + b * zc
         stem_full[a, at : at + zc, :] = joined(stem_own[tap], stem_other[tap], core)
     vectors[...] = joined(small_own[...], small_other[...], core)
+    same[...] = same_group(same.shape[0], same.shape[0] // GROUPS)
 
 
 def first_kernel(
@@ -148,6 +155,7 @@
     selection,
     stem_full,
     vectors,
+    same,
     small_own,
     weight_far,
     others_far,
@@ -239,8 +247,8 @@
         over_pieces(stem)
 
     per_group = full // GROUPS
-    mean = group_mean(jnp.broadcast_to(sums[0:1, :], (8, full)), per_group, cells)
-    variance = group_mean(squares(hidden, mean), per_group, cells)
+    mean = group_mean(jnp.broadcast_to(sums[0:1, :], (8, full)), same, per_group, cells)
+    variance = group_mean(squares(hidden, mean), same, per_group, cells)
     scale = lax.rsqrt(variance + EPSILON) * first_gain
 
     spot = lax.broadcasted_iota(jnp.int32, (1, width, full), 1) + leftmost
@@ -298,8 +306,10 @@
 
         over_pieces(convolve)
 
-    mean = group_mean(jnp.broadcast_to(sums[2:3, 0:half], (8, half)), per_group, cells)
-    variance = group_mean(squares(produced, mean), per_group, cells)
+    mean = group_mean(
+        jnp.broadcast_to(sums[2:3, 0:half], (8, half)), same, per_group, cells
+    )
+    variance = group_mean(squares(produced, mean), same, per_group, cells)
     scale = lax.rsqrt(variance + EPSILON) * small_own[5:6]
     second_shift = small_own[6:7]
     for spot_at in range(W_DEV + 2 * HALO):
@@ -472,9 +482,10 @@
                 jax.ShapeDtypeStruct((row_length // 128 * 3 * width, PACKED * tile_count), jnp.bfloat16),
                 jax.ShapeDtypeStruct((3, 256, full), jnp.bfloat16),
                 jax.ShapeDtypeStruct((small.shape[0], full), jnp.float32),
+                jax.ShapeDtypeStruct((full, full), jnp.bfloat16),
             ),
             in_specs=[far] * 2 + [vmem] * 3,
-            out_specs=(vmem,) * 3,
+            out_specs=(vmem,) * 4,
             scratch_shapes=[
                 pltpu.SMEM(tile_counts.shape, jnp.int32),
                 pltpu.VMEM(stem_weight.shape, jnp.bfloat16),
@@ -521,7 +532,7 @@
         small_other = lax.ppermute(small, "chan", swap)
         owners = lax.all_gather(latents, "tile", axis=0, tiled=True)
         prepared = prepare(small, small_other, stem_other, power)
-    selection, stem_full, vectors = prepared
+    selection, stem_full, vectors, same = prepared
     act, hidden, other_near, own_near, up_near = pl.pallas_call(
         first_kernel,
         out_shape=(
@@ -531,7 +542,7 @@
             jax.ShapeDtypeStruct(second_weight.shape, jnp.bfloat16),
             jax.ShapeDtypeStruct(upsample_weight.shape, jnp.bfloat16),
         ),
-        in_specs=[vmem] * 5 + [far] * 4,
+        in_specs=[vmem] * 6 + [far] * 4,
         out_specs=(vmem,) * 5,
         scratch_shapes=[
             pltpu.VMEM((tile_count, PACKED, 128), jnp.bfloat16),
@@ -558,6 +569,7 @@
         selection,
         stem_full,
         vectors,
+        same,
         small,
         pltpu.with_memory_space_constraint(first_weight, pltpu.HBM),
         pltpu.with_memory_space_constraint(second_other, pltpu.HBM),

time: 34.1 us -> 33.4 us (0.979)
  Pallas kernels: 18 us -> 17.3 us
    pallas_call x1, Pallas kernels: 12.8 us -> 12.1 us  [on_device(): pl.pallas_call(first_kernel, out_shape=(jax.ShapeDtypeStruct((window, F *...]
  transfers between devices with their start and end apart: 8 -> 8, of which waited for: 4 -> 4; matrix products, arithmetic and copies ran while one was open for 5% -> 5% of each run, Pallas kernels for 3% -> 4%
where the time goes in v9:
time: 33.4 us; the launch traced here: 33.2 us
  Pallas kernels  17.3 us (52%)
  starting transfers between devices  8.21 us (25%)
  waiting for transfers between devices  5.96 us (18%)
  local copies, waits for them, and re-layouts  1.58 us (5%)
    pallas_call x1, Pallas kernels, on_device(): pl.pallas_call(first_kernel, out_shape=(jax.ShapeDtypeStruct((window, F *...  12.1 us
    ppermute x1, starting transfers between devices, on_device(): one = lax.ppermute(latents, ('tile', 'chan'), pairs)  4.13 us
    pallas_call x1, Pallas kernels, on_device(): pl.pallas_call(functools.partial(second_kernel, tile_count), out_shape=ja...  4.03 us
    ppermute x1, waiting for transfers between devices, on_device(): two = lax.ppermute(latents, 'tile', both)  2.44 us
    ppermute x1, starting transfers between devices, exchanged(): moved = lax.ppermute(block, 'tile', [(i, i ^ step) for i in range(count)])  1.58 us
    ppermute x1, waiting for transfers between devices, exchanged(): moved = lax.ppermute(block, 'tile', [(i, i ^ step) for i in range(count)])  1.57 us
    ppermute x1, waiting for transfers between devices, on_device(): act_other = lax.ppermute(act, 'chan', swap)  1.57 us
    ppermute x1, starting transfers between devices, on_device(): two = lax.ppermute(latents, 'tile', both)  1.35 us
  transfers between devices with their start and end apart: 8, of which 4 were waited for; matrix products, arithmetic and copies ran while one was open for 5% of the time, Pallas kernels for 4%

profile of v9, /device:TPU:0, one launch (start us, length us, event | category | flops | bytes accessed | tf_op | source)
XLA Modules:
  0.0 33.2 jit_solution(8260223788439236386)
XLA Ops:
  0.0 0.5 %collective-permute-start.6 = (bf16[27,192,384]{2,1,0:T(8,128)(2,1)}, bf16[27,192,384]{2,1,0:T(8,128)(2,1)}, u32[]{:S(2)}, u32[]{:S(2)}) collective-permute-start(bf16[27,192,384]{2,1,0:T(8,128)(2,1)} %bitcast.20), channel_id=1, source_target_pairs={{0,1},{1,0},{2,3},{3,2},{4,5},{5,4},{6,7},{7,6},{8,9},{9,8},{10,11... | collective-permute-start | bytes 11943944 | tf_op jit(solution)/shard_map/ppermute | solution.py:508
  0.5 0.0 collective-permute-start.4
  0.5 0.8 %reshape.6 = bf16[1,60,128]{2,1,0:T(8,128)(2,1)S(1)} reshape(bf16[1,5,1536]{2,1,0:T(8,128)(2,1)} %param.14) | data formatting | bytes 30720 | tf_op jit(solution)/shard_map/reshape | solution.py:461
  1.3 4.1 %collective-permute-start = (bf16[1,60,128]{2,1,0:T(8,128)(2,1)S(1)}, bf16[1,60,128]{2,1,0:T(8,128)(2,1)S(1)}, u32[]{:S(2)}, u32[]{:S(2)}) collective-permute-start(bf16[1,60,128]{2,1,0:T(8,128)(2,1)S(1)} %reshape.6), channel_id=1, source_target_pairs={{0,8},{1,5},{2,10},{3,7},{4,12},{5,1},{6,14},{7,3},{8,0},{9,13},{1... | collective-permute-start | bytes 46088 | tf_op jit(solution)/shard_map/ppermute | solution.py:517
  5.4 1.3 %collective-permute-start.1 = (bf16[1,60,128]{2,1,0:T(8,128)(2,1)S(1)}, bf16[1,60,128]{2,1,0:T(8,128)(2,1)S(1)}, u32[]{:S(2)}, u32[]{:S(2)}) collective-permute-start(bf16[1,60,128]{2,1,0:T(8,128)(2,1)S(1)} %reshape.6), channel_id=1, source_target_pairs={{0,12},{2,14},{4,8},{6,10},{8,4},{10,6},{12,0},{14,2},{1,13},{3,15... | collective-permute-start | bytes 46088 | tf_op jit(solution)/shard_map/ppermute | solution.py:519
  6.8 0.4 %collective-permute-done = bf16[1,60,128]{2,1,0:T(8,128)(2,1)S(1)} collective-permute-done((bf16[1,60,128]{2,1,0:T(8,128)(2,1)S(1)}, bf16[1,60,128]{2,1,0:T(8,128)(2,1)S(1)}, u32[]{:S(2)}, u32[]{:S(2)}) %collective-permute-start) | collective-permute-done | bytes 15392 | tf_op jit(solution)/shard_map/ppermute | solution.py:517
  7.1 0.0 collective-permute-start.2
  7.1 0.8 %stack.31.small_own = f32[8,192]{1,0:T(8,128)S(1)} concatenate(f32[1,192]{1,0:T(1,128)} %bitcast.12, f32[1,192]{1,0:T(1,128)} %bitcast.13, f32[1,192]{1,0:T(1,128)} %bitcast.14, f32[1,192]{1,0:T(1,128)} %bitcast.15, f32[1,192]{1,0:T(1,128)} %bitcast.16, f32[1,192]{1,0:T(1,128)} %bitcast.17, f32[1,192]{1,0:T(1,128)} %bitcast.18, f32[1,192]{1,0:T(1,128)S(1)} %stack_broadcast_in_dim.3), dimensions={0} | concatenate | bytes 12288 | tf_op jit(solution)/shard_map/stack | solution.py:462
  7.9 0.6 %collective-permute-start.3 = (f32[8,192]{1,0:T(8,128)S(1)}, f32[8,192]{1,0:T(8,128)S(1)}, u32[]{:S(2)}, u32[]{:S(2)}) collective-permute-start(f32[8,192]{1,0:T(8,128)S(1)} %stack.31.small_own), channel_id=1, source_target_pairs={{0,1},{1,0},{2,3},{3,2},{4,5},{5,4},{6,7},{7,6},{8,9},{9,8},{10,11... | collective-permute-start | bytes 18440 | tf_op jit(solution)/shard_map/ppermute | solution.py:520
  8.5 2.4 %collective-permute-done.1 = bf16[1,60,128]{2,1,0:T(8,128)(2,1)S(1)} collective-permute-done((bf16[1,60,128]{2,1,0:T(8,128)(2,1)S(1)}, bf16[1,60,128]{2,1,0:T(8,128)(2,1)S(1)}, u32[]{:S(2)}, u32[]{:S(2)}) %collective-permute-start.1) | collective-permute-done | bytes 15392 | tf_op jit(solution)/shard_map/ppermute | solution.py:519
  11.0 0.0 collective-permute-done.2
  11.0 0.0 collective-permute-done.3.small_other
  11.0 0.0 collective-permute-done.4.stem_other
  11.0 1.6 %collective-permute-start.5 = (bf16[4,60,128]{2,1,0:T(8,128)(2,1)S(1)}, bf16[4,60,128]{2,1,0:T(8,128)(2,1)S(1)}, u32[]{:S(2)}, u32[]{:S(2)}) collective-permute-start(bf16[4,60,128]{2,1,0:T(8,128)(2,1)S(1)} %pad_maximum_fusion.1), channel_id=1, source_target_pairs={{0,2},{2,0},{4,6},{6,4},{8,10},{10,8},{12,14},{14,12},{1,3},{3,1},... | collective-permute-start | bytes 184328 | tf_op jit(solution)/shard_map/ppermute | solution.py:428
  12.6 1.2 %shard_map.136 = (bf16[576,512]{1,0:T(8,128)(2,1)S(1)}, bf16[3,256,384]{2,1,0:T(8,128)(2,1)S(1)}, f32[8,384]{1,0:T(8,128)S(1)}, bf16[384,384]{1,0:T(8,128)(2,1)S(1)}) custom-call(s32[8]{0:T(128)} %counts_far.1, bf16[27,16,192]{2,1,0:T(8,128)(2,1)} %stem_far.1, bf16[27,16,192]{2,1,0:T(8,128)(2,1)S(1)} %collective-permute-done.4.stem_other, ...), custom_call_target="tpu_custom_call" | custom-call | flops 100000000 | bytes 1000000 | tf_op jit(solution)/shard_map/pallas_call | solution.py:479
  13.8 1.6 %collective-permute-done.5 = bf16[4,60,128]{2,1,0:T(8,128)(2,1)S(1)} collective-permute-done((bf16[4,60,128]{2,1,0:T(8,128)(2,1)S(1)}, bf16[4,60,128]{2,1,0:T(8,128)(2,1)S(1)}, u32[]{:S(2)}, u32[]{:S(2)}) %collective-permute-start.5) | collective-permute-done | bytes 61472 | tf_op jit(solution)/shard_map/ppermute | solution.py:428
  15.3 0.0 collective-permute-done.6.others_far
  15.4 0.0 copy-start
  15.4 12.1 %shard_map.137 = (bf16[6,96,192]{2,1,0:T(8,128)(2,1)S(1)}, bf16[4,48,384]{2,1,0:T(8,128)(2,1)S(1)}, bf16[27,192,384]{2,1,0:T(8,128)(2,1)S(1)}, bf16[27,192,384]{2,1,0:T(8,128)(2,1)S(1)}, bf16[9,192,384]{2,1,0:T(8,128)(2,1)S(1)}) custom-call(bf16[8,60,128]{2,1,0:T(8,128)(2,1)S(1)} %pad_maximum_fusion.owners, ...), custom_call_target="tpu_custom_call" | custom-call | flops 4586471424 | bytes 3981312 | tf_op jit(solution)/shard_map/pallas_call | solution.py:536
  27.5 0.1 collective-permute-start.7
  27.6 1.6 %collective-permute-done.7.act_other = bf16[6,96,192]{2,1,0:T(8,128)(2,1)S(1)} collective-permute-done((bf16[6,96,192]{2,1,0:T(8,128)(2,1)S(1)}, bf16[6,96,192]{2,1,0:T(8,128)(2,1)S(1)}, u32[]{:S(2)}, u32[]{:S(2)}) %collective-permute-start.7) | collective-permute-done | bytes 221216 | tf_op jit(solution)/shard_map/ppermute | solution.py:580
  29.2 0.0 copy-done
  29.2 4.0 %shard_map.138 = bf16[2,48,4,192]{3,2,1,0:T(4,128)(2,1)} custom-call(bf16[6,96,192]{2,1,0:T(8,128)(2,1)S(1)} %get-tuple-element.24.act_own, bf16[6,96,192]{2,1,0:T(8,128)(2,1)S(1)} %collective-permute-done.7.act_other, bf16[4,48,384]{2,1,0:T(8,128)(2,1)S(1)} %get-tuple-element.25.hidden_in, bf16[27,192,384]{2,1,0:T(8,128)(2,1)S(1)} %get-tuple-element.26.weight_own, ...), custom_call_target="tpu_custom_call" | custom-call | flops 1528823808 | bytes 7962624 | tf_op jit(solution)/shard_map/pallas_call | solution.py:582
  (3 shorter events, 0.0 us)
Async XLA Ops:
  0.0 15.4 %collective-permute-start.6 = (bf16[27,192,384]{2,1,0:T(8,128)(2,1)}, bf16[27,192,384]{2,1,0:T(8,128)(2,1)}, u32[]{:S(2)}, u32[]{:S(2)}) collective-permute-start(bf16[27,192,384]{2,1,0:T(8,128)(2,1)} %bitcast.20), channel_id=1, source_target_pairs={{0,1},{1,0},{2,3},{3,2},{4,5},{5,4},{6,7},{7,6},{8,9},{9,8},{10,11... | collective-permute-start | bytes 11943944 | tf_op jit(solution)/shard_map/ppermute | solution.py:508
  0.5 10.5 %collective-permute-start.4 = (bf16[27,16,192]{2,1,0:T(8,128)(2,1)}, bf16[27,16,192]{2,1,0:T(8,128)(2,1)S(1)}, u32[]{:S(2)}, u32[]{:S(2)}) collective-permute-start(bf16[27,16,192]{2,1,0:T(8,128)(2,1)} %stem_far.1), channel_id=1, source_target_pairs={{0,1},{1,0},{2,3},{3,2},{4,5},{5,4},{6,7},{7,6},{8,9},{9,8},{10,11... | collective-permute-start | bytes 497672 | tf_op jit(solution)/shard_map/ppermute | solution.py:507
  1.3 5.8 %collective-permute-start = (bf16[1,60,128]{2,1,0:T(8,128)(2,1)S(1)}, bf16[1,60,128]{2,1,0:T(8,128)(2,1)S(1)}, u32[]{:S(2)}, u32[]{:S(2)}) collective-permute-start(bf16[1,60,128]{2,1,0:T(8,128)(2,1)S(1)} %reshape.6), channel_id=1, source_target_pairs={{0,8},{1,5},{2,10},{3,7},{4,12},{5,1},{6,14},{7,3},{8,0},{9,13},{1... | collective-permute-start | bytes 46088 | tf_op jit(solution)/shard_map/ppermute | solution.py:517
  5.4 5.5 %collective-permute-start.1 = (bf16[1,60,128]{2,1,0:T(8,128)(2,1)S(1)}, bf16[1,60,128]{2,1,0:T(8,128)(2,1)S(1)}, u32[]{:S(2)}, u32[]{:S(2)}) collective-permute-start(bf16[1,60,128]{2,1,0:T(8,128)(2,1)S(1)} %reshape.6), channel_id=1, source_target_pairs={{0,12},{2,14},{4,8},{6,10},{8,4},{10,6},{12,0},{14,2},{1,13},{3,15... | collective-permute-start | bytes 46088 | tf_op jit(solution)/shard_map/ppermute | solution.py:519
  7.1 3.8 %collective-permute-start.2 = (bf16[1,60,128]{2,1,0:T(8,128)(2,1)S(1)}, bf16[1,60,128]{2,1,0:T(8,128)(2,1)S(1)}, u32[]{:S(2)}, u32[]{:S(2)}) collective-permute-start(bf16[1,60,128]{2,1,0:T(8,128)(2,1)S(1)} %collective-permute-done), channel_id=1, source_target_pairs={{0,1},{1,0},{2,3},{3,2},{4,5},{5,4},{6,7},{7,6},{8,9},{9,8},{10,11... | collective-permute-start | bytes 46088 | tf_op jit(solution)/shard_map/ppermute | solution.py:521
  7.9 3.0 %collective-permute-start.3 = (f32[8,192]{1,0:T(8,128)S(1)}, f32[8,192]{1,0:T(8,128)S(1)}, u32[]{:S(2)}, u32[]{:S(2)}) collective-permute-start(f32[8,192]{1,0:T(8,128)S(1)} %stack.31.small_own), channel_id=1, source_target_pairs={{0,1},{1,0},{2,3},{3,2},{4,5},{5,4},{6,7},{7,6},{8,9},{9,8},{10,11... | collective-permute-start | bytes 18440 | tf_op jit(solution)/shard_map/ppermute | solution.py:520
  11.0 4.3 %collective-permute-start.5 = (bf16[4,60,128]{2,1,0:T(8,128)(2,1)S(1)}, bf16[4,60,128]{2,1,0:T(8,128)(2,1)S(1)}, u32[]{:S(2)}, u32[]{:S(2)}) collective-permute-start(bf16[4,60,128]{2,1,0:T(8,128)(2,1)S(1)} %pad_maximum_fusion.1), channel_id=1, source_target_pairs={{0,2},{2,0},{4,6},{6,4},{8,10},{10,8},{12,14},{14,12},{1,3},{3,1},... | collective-permute-start | bytes 184328 | tf_op jit(solution)/shard_map/ppermute | solution.py:428
  15.4 13.8 %copy-start = (f32[192]{0:T(256)S(1)}, f32[192]{0:T(256)}, u32[]{:S(2)}) copy-start(f32[192]{0:T(256)} %param.27) | copy-start | bytes 2308
  27.5 1.6 %collective-permute-start.7 = (bf16[6,96,192]{2,1,0:T(8,128)(2,1)S(1)}, bf16[6,96,192]{2,1,0:T(8,128)(2,1)S(1)}, u32[]{:S(2)}, u32[]{:S(2)}) collective-permute-start(bf16[6,96,192]{2,1,0:T(8,128)(2,1)S(1)} %get-tuple-element.24.act_own), channel_id=1, source_target_pairs={{0,1},{1,0},{2,3},{3,2},{4,5},{5,4},{6,7},{7,6},{8,9},{9,8},{10,11... | collective-permute-start | bytes 663560 | tf_op jit(solution)/shard_map/ppermute | solution.py:580

commit v10 on v9

--- a/solution.py
+++ b/solution.py
@@ -65,7 +65,7 @@
         return total + jnp.sum((spread * spread).reshape(step // 8, 8, channels), axis=0)
 
     total = lax.fori_loop(
-        0, ref.shape[1] // step, add, jnp.zeros((8, channels), jnp.float32), unroll=2
+        0, ref.shape[1] // step, add, jnp.zeros((8, channels), jnp.float32), unroll=8
     )
     return jnp.broadcast_to(jnp.sum(total, axis=0, keepdims=True), (8, channels))
 
@@ -274,7 +274,7 @@
             acts[2, frame, place] = right.astype(jnp.bfloat16)
             return _
 
-        lax.fori_loop(0, H // 2, activate, 0, unroll=2)
+        lax.fori_loop(0, H // 2, activate, 0, unroll=3)
 
     fetch.wait()
     carries = [
@@ -286,14 +286,21 @@
     for carry in carries:
         carry.start()
     first_bias = small_own[4:5]
-    for frame in range(F):
+    together = (tuple(range(2, F)), (1,), (0,))
+    for group in together if pieces == 1 else [(frame,) for frame in range(F)]:
 
         def convolve(row):
-            used = range(max(0, 2 - frame) * 9, 27)
+            used = range(max(0, 2 - group[0]) * 9, 27)
             lhs = jnp.concatenate(
                 [
-                    acts[tap % 3, frame + tap // 9 - 2, pl.ds(row + tap // 3 % 3, rows)].reshape(
-                        rows * width, full
+                    jnp.concatenate(
+                        [
+                            acts[
+                                tap % 3, frame + tap // 9 - 2, pl.ds(row + tap // 3 % 3, rows)
+                            ].reshape(rows * width, full)
+                            for frame in group
+                        ],
+                        axis=0,
                     )
                     for tap in used
                 ],
@@ -301,7 +308,9 @@
             )
             total = times(lhs, weight, used)
             value = (total + first_bias).astype(jnp.bfloat16).astype(jnp.float32)
-            put(produced, span(frame, row), value)
+            for at, frame in enumerate(group):
+                part = value[at * rows * width : (at + 1) * rows * width]
+                put(produced, span(frame, row), part)
             sums[2:3, 0:half] += jnp.sum(value, axis=0, keepdims=True)
 
         over_pieces(convolve)

time: 33.4 us -> 32.3 us (0.967)
  Pallas kernels: 17.3 us -> 16.2 us
    pallas_call x1, Pallas kernels: 12.1 us -> 11 us  [on_device(): pl.pallas_call(first_kernel, out_shape=(jax.ShapeDtypeStruct((window, F *...]
where the time goes in v10:
time: 32.3 us; the launch traced here: 32.1 us
  Pallas kernels  16.2 us (50%)
  starting transfers between devices  8.21 us (25%)
  waiting for transfers between devices  5.96 us (18%)
  local copies, waits for them, and re-layouts  1.58 us (5%)
    pallas_call x1, Pallas kernels, on_device(): pl.pallas_call(first_kernel, out_shape=(jax.ShapeDtypeStruct((window, F *...  11 us
    ppermute x1, starting transfers between devices, on_device(): one = lax.ppermute(latents, ('tile', 'chan'), pairs)  4.13 us
    pallas_call x1, Pallas kernels, on_device(): pl.pallas_call(functools.partial(second_kernel, tile_count), out_shape=ja...  4.04 us
    ppermute x1, waiting for transfers between devices, on_device(): two = lax.ppermute(latents, 'tile', both)  2.44 us
    ppermute x1, starting transfers between devices, exchanged(): moved = lax.ppermute(block, 'tile', [(i, i ^ step) for i in range(count)])  1.58 us
    ppermute x1, waiting for transfers between devices, exchanged(): moved = lax.ppermute(block, 'tile', [(i, i ^ step) for i in range(count)])  1.57 us
    ppermute x1, waiting for transfers between devices, on_device(): act_other = lax.ppermute(act, 'chan', swap)  1.57 us
    ppermute x1, starting transfers between devices, on_device(): two = lax.ppermute(latents, 'tile', both)  1.35 us
  transfers between devices with their start and end apart: 8, of which 4 were waited for; matrix products, arithmetic and copies ran while one was open for 5% of the time, Pallas kernels for 4%

profile of v10, /device:TPU:0, one launch (start us, length us, event | category | flops | bytes accessed | tf_op | source)
XLA Modules:
  0.0 32.1 jit_solution(12364648927721773652)
XLA Ops:
  0.0 0.5 %collective-permute-start.6 = (bf16[27,192,384]{2,1,0:T(8,128)(2,1)}, bf16[27,192,384]{2,1,0:T(8,128)(2,1)}, u32[]{:S(2)}, u32[]{:S(2)}) collective-permute-start(bf16[27,192,384]{2,1,0:T(8,128)(2,1)} %bitcast.20), channel_id=1, source_target_pairs={{0,1},{1,0},{2,3},{3,2},{4,5},{5,4},{6,7},{7,6},{8,9},{9,8},{10,11... | collective-permute-start | bytes 11943944 | tf_op jit(solution)/shard_map/ppermute | solution.py:517
  0.5 0.0 collective-permute-start.4
  0.5 0.8 %reshape.6 = bf16[1,60,128]{2,1,0:T(8,128)(2,1)S(1)} reshape(bf16[1,5,1536]{2,1,0:T(8,128)(2,1)} %param.14) | data formatting | bytes 30720 | tf_op jit(solution)/shard_map/reshape | solution.py:470
  1.3 4.1 %collective-permute-start = (bf16[1,60,128]{2,1,0:T(8,128)(2,1)S(1)}, bf16[1,60,128]{2,1,0:T(8,128)(2,1)S(1)}, u32[]{:S(2)}, u32[]{:S(2)}) collective-permute-start(bf16[1,60,128]{2,1,0:T(8,128)(2,1)S(1)} %reshape.6), channel_id=1, source_target_pairs={{0,8},{1,5},{2,10},{3,7},{4,12},{5,1},{6,14},{7,3},{8,0},{9,13},{1... | collective-permute-start | bytes 46088 | tf_op jit(solution)/shard_map/ppermute | solution.py:526
  5.4 1.3 %collective-permute-start.1 = (bf16[1,60,128]{2,1,0:T(8,128)(2,1)S(1)}, bf16[1,60,128]{2,1,0:T(8,128)(2,1)S(1)}, u32[]{:S(2)}, u32[]{:S(2)}) collective-permute-start(bf16[1,60,128]{2,1,0:T(8,128)(2,1)S(1)} %reshape.6), channel_id=1, source_target_pairs={{0,12},{2,14},{4,8},{6,10},{8,4},{10,6},{12,0},{14,2},{1,13},{3,15... | collective-permute-start | bytes 46088 | tf_op jit(solution)/shard_map/ppermute | solution.py:528
  6.8 0.4 %collective-permute-done = bf16[1,60,128]{2,1,0:T(8,128)(2,1)S(1)} collective-permute-done((bf16[1,60,128]{2,1,0:T(8,128)(2,1)S(1)}, bf16[1,60,128]{2,1,0:T(8,128)(2,1)S(1)}, u32[]{:S(2)}, u32[]{:S(2)}) %collective-permute-start) | collective-permute-done | bytes 15392 | tf_op jit(solution)/shard_map/ppermute | solution.py:526
  7.1 0.0 collective-permute-start.2
  7.1 0.8 %stack.31.small_own = f32[8,192]{1,0:T(8,128)S(1)} concatenate(f32[1,192]{1,0:T(1,128)} %bitcast.12, f32[1,192]{1,0:T(1,128)} %bitcast.13, f32[1,192]{1,0:T(1,128)} %bitcast.14, f32[1,192]{1,0:T(1,128)} %bitcast.15, f32[1,192]{1,0:T(1,128)} %bitcast.16, f32[1,192]{1,0:T(1,128)} %bitcast.17, f32[1,192]{1,0:T(1,128)} %bitcast.18, f32[1,192]{1,0:T(1,128)S(1)} %stack_broadcast_in_dim.3), dimensions={0} | concatenate | bytes 12288 | tf_op jit(solution)/shard_map/stack | solution.py:471
  7.9 0.6 %collective-permute-start.3 = (f32[8,192]{1,0:T(8,128)S(1)}, f32[8,192]{1,0:T(8,128)S(1)}, u32[]{:S(2)}, u32[]{:S(2)}) collective-permute-start(f32[8,192]{1,0:T(8,128)S(1)} %stack.31.small_own), channel_id=1, source_target_pairs={{0,1},{1,0},{2,3},{3,2},{4,5},{5,4},{6,7},{7,6},{8,9},{9,8},{10,11... | collective-permute-start | bytes 18440 | tf_op jit(solution)/shard_map/ppermute | solution.py:529
  8.5 2.4 %collective-permute-done.1 = bf16[1,60,128]{2,1,0:T(8,128)(2,1)S(1)} collective-permute-done((bf16[1,60,128]{2,1,0:T(8,128)(2,1)S(1)}, bf16[1,60,128]{2,1,0:T(8,128)(2,1)S(1)}, u32[]{:S(2)}, u32[]{:S(2)}) %collective-permute-start.1) | collective-permute-done | bytes 15392 | tf_op jit(solution)/shard_map/ppermute | solution.py:528
  11.0 0.0 collective-permute-done.2
  11.0 0.0 collective-permute-done.3.small_other
  11.0 0.0 collective-permute-done.4.stem_other
  11.0 1.6 %collective-permute-start.5 = (bf16[4,60,128]{2,1,0:T(8,128)(2,1)S(1)}, bf16[4,60,128]{2,1,0:T(8,128)(2,1)S(1)}, u32[]{:S(2)}, u32[]{:S(2)}) collective-permute-start(bf16[4,60,128]{2,1,0:T(8,128)(2,1)S(1)} %pad_maximum_fusion.1), channel_id=1, source_target_pairs={{0,2},{2,0},{4,6},{6,4},{8,10},{10,8},{12,14},{14,12},{1,3},{3,1},... | collective-permute-start | bytes 184328 | tf_op jit(solution)/shard_map/ppermute | solution.py:437
  12.6 1.2 %shard_map.136 = (bf16[576,512]{1,0:T(8,128)(2,1)S(1)}, bf16[3,256,384]{2,1,0:T(8,128)(2,1)S(1)}, f32[8,384]{1,0:T(8,128)S(1)}, bf16[384,384]{1,0:T(8,128)(2,1)S(1)}) custom-call(s32[8]{0:T(128)} %counts_far.1, bf16[27,16,192]{2,1,0:T(8,128)(2,1)} %stem_far.1, bf16[27,16,192]{2,1,0:T(8,128)(2,1)S(1)} %collective-permute-done.4.stem_other, ...), custom_call_target="tpu_custom_call" | custom-call | flops 100000000 | bytes 1000000 | tf_op jit(solution)/shard_map/pallas_call | solution.py:488
  13.8 1.6 %collective-permute-done.5 = bf16[4,60,128]{2,1,0:T(8,128)(2,1)S(1)} collective-permute-done((bf16[4,60,128]{2,1,0:T(8,128)(2,1)S(1)}, bf16[4,60,128]{2,1,0:T(8,128)(2,1)S(1)}, u32[]{:S(2)}, u32[]{:S(2)}) %collective-permute-start.5) | collective-permute-done | bytes 61472 | tf_op jit(solution)/shard_map/ppermute | solution.py:437
  15.3 0.0 collective-permute-done.6.others_far
  15.4 0.0 copy-start
  15.4 11.0 %shard_map.137 = (bf16[6,96,192]{2,1,0:T(8,128)(2,1)S(1)}, bf16[4,48,384]{2,1,0:T(8,128)(2,1)S(1)}, bf16[27,192,384]{2,1,0:T(8,128)(2,1)S(1)}, bf16[27,192,384]{2,1,0:T(8,128)(2,1)S(1)}, bf16[9,192,384]{2,1,0:T(8,128)(2,1)S(1)}) custom-call(bf16[8,60,128]{2,1,0:T(8,128)(2,1)S(1)} %pad_maximum_fusion.owners, ...), custom_call_target="tpu_custom_call" | custom-call | flops 4586471424 | bytes 3981312 | tf_op jit(solution)/shard_map/pallas_call | solution.py:545
  26.4 0.1 collective-permute-start.7
  26.5 1.6 %collective-permute-done.7.act_other = bf16[6,96,192]{2,1,0:T(8,128)(2,1)S(1)} collective-permute-done((bf16[6,96,192]{2,1,0:T(8,128)(2,1)S(1)}, bf16[6,96,192]{2,1,0:T(8,128)(2,1)S(1)}, u32[]{:S(2)}, u32[]{:S(2)}) %collective-permute-start.7) | collective-permute-done | bytes 221216 | tf_op jit(solution)/shard_map/ppermute | solution.py:589
  28.0 0.0 copy-done
  28.0 4.0 %shard_map.138 = bf16[2,48,4,192]{3,2,1,0:T(4,128)(2,1)} custom-call(bf16[6,96,192]{2,1,0:T(8,128)(2,1)S(1)} %get-tuple-element.24.act_own, bf16[6,96,192]{2,1,0:T(8,128)(2,1)S(1)} %collective-permute-done.7.act_other, bf16[4,48,384]{2,1,0:T(8,128)(2,1)S(1)} %get-tuple-element.25.hidden_in, bf16[27,192,384]{2,1,0:T(8,128)(2,1)S(1)} %get-tuple-element.26.weight_own, ...), custom_call_target="tpu_custom_call" | custom-call | flops 1528823808 | bytes 7962624 | tf_op jit(solution)/shard_map/pallas_call | solution.py:591
  (3 shorter events, 0.0 us)
Async XLA Ops:
  0.0 15.4 %collective-permute-start.6 = (bf16[27,192,384]{2,1,0:T(8,128)(2,1)}, bf16[27,192,384]{2,1,0:T(8,128)(2,1)}, u32[]{:S(2)}, u32[]{:S(2)}) collective-permute-start(bf16[27,192,384]{2,1,0:T(8,128)(2,1)} %bitcast.20), channel_id=1, source_target_pairs={{0,1},{1,0},{2,3},{3,2},{4,5},{5,4},{6,7},{7,6},{8,9},{9,8},{10,11... | collective-permute-start | bytes 11943944 | tf_op jit(solution)/shard_map/ppermute | solution.py:517
  0.5 10.5 %collective-permute-start.4 = (bf16[27,16,192]{2,1,0:T(8,128)(2,1)}, bf16[27,16,192]{2,1,0:T(8,128)(2,1)S(1)}, u32[]{:S(2)}, u32[]{:S(2)}) collective-permute-start(bf16[27,16,192]{2,1,0:T(8,128)(2,1)} %stem_far.1), channel_id=1, source_target_pairs={{0,1},{1,0},{2,3},{3,2},{4,5},{5,4},{6,7},{7,6},{8,9},{9,8},{10,11... | collective-permute-start | bytes 497672 | tf_op jit(solution)/shard_map/ppermute | solution.py:516
  1.3 5.8 %collective-permute-start = (bf16[1,60,128]{2,1,0:T(8,128)(2,1)S(1)}, bf16[1,60,128]{2,1,0:T(8,128)(2,1)S(1)}, u32[]{:S(2)}, u32[]{:S(2)}) collective-permute-start(bf16[1,60,128]{2,1,0:T(8,128)(2,1)S(1)} %reshape.6), channel_id=1, source_target_pairs={{0,8},{1,5},{2,10},{3,7},{4,12},{5,1},{6,14},{7,3},{8,0},{9,13},{1... | collective-permute-start | bytes 46088 | tf_op jit(solution)/shard_map/ppermute | solution.py:526
  5.4 5.5 %collective-permute-start.1 = (bf16[1,60,128]{2,1,0:T(8,128)(2,1)S(1)}, bf16[1,60,128]{2,1,0:T(8,128)(2,1)S(1)}, u32[]{:S(2)}, u32[]{:S(2)}) collective-permute-start(bf16[1,60,128]{2,1,0:T(8,128)(2,1)S(1)} %reshape.6), channel_id=1, source_target_pairs={{0,12},{2,14},{4,8},{6,10},{8,4},{10,6},{12,0},{14,2},{1,13},{3,15... | collective-permute-start | bytes 46088 | tf_op jit(solution)/shard_map/ppermute | solution.py:528
  7.1 3.8 %collective-permute-start.2 = (bf16[1,60,128]{2,1,0:T(8,128)(2,1)S(1)}, bf16[1,60,128]{2,1,0:T(8,128)(2,1)S(1)}, u32[]{:S(2)}, u32[]{:S(2)}) collective-permute-start(bf16[1,60,128]{2,1,0:T(8,128)(2,1)S(1)} %collective-permute-done), channel_id=1, source_target_pairs={{0,1},{1,0},{2,3},{3,2},{4,5},{5,4},{6,7},{7,6},{8,9},{9,8},{10,11... | collective-permute-start | bytes 46088 | tf_op jit(solution)/shard_map/ppermute | solution.py:530
  7.9 3.0 %collective-permute-start.3 = (f32[8,192]{1,0:T(8,128)S(1)}, f32[8,192]{1,0:T(8,128)S(1)}, u32[]{:S(2)}, u32[]{:S(2)}) collective-permute-start(f32[8,192]{1,0:T(8,128)S(1)} %stack.31.small_own), channel_id=1, source_target_pairs={{0,1},{1,0},{2,3},{3,2},{4,5},{5,4},{6,7},{7,6},{8,9},{9,8},{10,11... | collective-permute-start | bytes 18440 | tf_op jit(solution)/shard_map/ppermute | solution.py:529
  11.0 4.3 %collective-permute-start.5 = (bf16[4,60,128]{2,1,0:T(8,128)(2,1)S(1)}, bf16[4,60,128]{2,1,0:T(8,128)(2,1)S(1)}, u32[]{:S(2)}, u32[]{:S(2)}) collective-permute-start(bf16[4,60,128]{2,1,0:T(8,128)(2,1)S(1)} %pad_maximum_fusion.1), channel_id=1, source_target_pairs={{0,2},{2,0},{4,6},{6,4},{8,10},{10,8},{12,14},{14,12},{1,3},{3,1},... | collective-permute-start | bytes 184328 | tf_op jit(solution)/shard_map/ppermute | solution.py:437
  15.4 12.7 %copy-start = (f32[192]{0:T(256)S(1)}, f32[192]{0:T(256)}, u32[]{:S(2)}) copy-start(f32[192]{0:T(256)} %param.27) | copy-start | bytes 2308
  26.4 1.6 %collective-permute-start.7 = (bf16[6,96,192]{2,1,0:T(8,128)(2,1)S(1)}, bf16[6,96,192]{2,1,0:T(8,128)(2,1)S(1)}, u32[]{:S(2)}, u32[]{:S(2)}) collective-permute-start(bf16[6,96,192]{2,1,0:T(8,128)(2,1)S(1)} %get-tuple-element.24.act_own), channel_id=1, source_target_pairs={{0,1},{1,0},{2,3},{3,2},{4,5},{5,4},{6,7},{7,6},{8,9},{9,8},{10,11... | collective-permute-start | bytes 663560 | tf_op jit(solution)/shard_map/ppermute | solution.py:589
